TPU v7x, 32 devices: a whole 2x2x4 slice. The times are simulated.
32 devices in a mesh: ctx: 8 (over y, x, core), tp: 4 (over z).
Axes of the slice: x: 2, y: 2, z: 4, core: 2. Of those that a mesh axis runs over, the one named last changes fastest.
Arguments:
- tokens: bfloat16 [4096, 2048], P('ctx'), may hold values from -6 to 6
- cotangent: bfloat16 [4096, 2048], P('ctx'), may hold values from -6 to 6
- w_qkv: float32 [3, 2048, 2048], P(None, 'ctx', 'tp'), may hold values from -0.125 to 0.125
- w_out: float32 [2048, 2048], P('tp', 'ctx'), may hold values from -0.75 to 0.75
- w_up: float32 [2048, 8192], P('ctx', 'tp'), may hold values from -0.125 to 0.125
- w_down: float32 [8192, 2048], P('tp', 'ctx'), may hold values from -0.0625 to 0.0625
- norm_gains: float32 [2, 2048], P(None, 'ctx'), may hold values from 0.25 to 1.75
- norm_biases: float32 [2, 2048], P(None, 'ctx'), may hold values from -3 to 3
- m_qkv: float32 [3, 2048, 2048], P(None, 'ctx', 'tp'), may hold values from -0.00024414062 to 0.00024414062
- m_out: float32 [2048, 2048], P('tp', 'ctx'), may hold values from -0.00024414062 to 0.00024414062
- m_up: float32 [2048, 8192], P('ctx', 'tp'), may hold values from -0.00024414062 to 0.00024414062
- m_down: float32 [8192, 2048], P('tp', 'ctx'), may hold values from -0.00024414062 to 0.00024414062
- m_gains: float32 [2, 2048], P(None, 'ctx'), may hold values from -0.00024414062 to 0.00024414062
- m_biases: float32 [2, 2048], P(None, 'ctx'), may hold values from -0.00024414062 to 0.00024414062
- v_qkv: float32 [3, 2048, 2048], P(None, 'ctx', 'tp'), may hold values from 3.9729964e-10 to 3.9729965e-08
- v_out: float32 [2048, 2048], P('tp', 'ctx'), may hold values from 3.9729964e-10 to 3.9729965e-08
- v_up: float32 [2048, 8192], P('ctx', 'tp'), may hold values from 3.9729964e-10 to 3.9729965e-08
- v_down: float32 [8192, 2048], P('tp', 'ctx'), may hold values from 3.9729964e-10 to 3.9729965e-08
- v_gains: float32 [2, 2048], P(None, 'ctx'), may hold values from 3.9729964e-10 to 3.9729965e-08
- v_biases: float32 [2, 2048], P(None, 'ctx'), may hold values from 3.9729964e-10 to 3.9729965e-08
- seq_lengths: int32 [4], replicated, may hold values from 1 to 2048, 4096 in all
- decay_mask: int32 [6], replicated, may hold values 0 or 1
Outputs:
- block_out: bfloat16 [4096, 2048], P('ctx')
- grad_tokens: bfloat16 [4096, 2048], P('ctx')
- grad_norm: float32 [], replicated
- grad_qkv: float32 [3, 2048, 2048], P(None, 'ctx', 'tp')
- grad_out: float32 [2048, 2048], P('tp', 'ctx')
- grad_up: float32 [2048, 8192], P('ctx', 'tp')
- grad_down: float32 [8192, 2048], P('tp', 'ctx')
- grad_gains: float32 [2, 2048], P(None, 'ctx')
- grad_biases: float32 [2, 2048], P(None, 'ctx')
- step_qkv: float32 [3, 2048, 2048], P(None, 'ctx', 'tp')
- step_out: float32 [2048, 2048], P('tp', 'ctx')
- step_up: float32 [2048, 8192], P('ctx', 'tp')
- step_down: float32 [8192, 2048], P('tp', 'ctx')
- step_gains: float32 [2, 2048], P(None, 'ctx')
- step_biases: float32 [2, 2048], P(None, 'ctx')
- first_qkv: float32 [3, 2048, 2048], P(None, 'ctx', 'tp')
- first_out: float32 [2048, 2048], P('tp', 'ctx')
- first_up: float32 [2048, 8192], P('ctx', 'tp')
- first_down: float32 [8192, 2048], P('tp', 'ctx')
- first_gains: float32 [2, 2048], P(None, 'ctx')
- first_biases: float32 [2, 2048], P(None, 'ctx')
- second_qkv: float32 [3, 2048, 2048], P(None, 'ctx', 'tp')
- second_out: float32 [2048, 2048], P('tp', 'ctx')
- second_up: float32 [2048, 8192], P('ctx', 'tp')
- second_down: float32 [8192, 2048], P('tp', 'ctx')
- second_gains: float32 [2, 2048], P(None, 'ctx')
- second_biases: float32 [2, 2048], P(None, 'ctx')
Inputs may be any that keep to these rules, and one draw needn't show every extreme that they name: `seq_lengths`: the lengths sum to 4096.
All inputs are finite; a program needn't handle non-finite values.
Results may differ from a plain program's by a relative error of at most 0.012.
Values may be sent and summed in bfloat16 or wider, within the bound.
No kernel may reach another device: no remote copies, remote signals or barrier semaphores. Data moves between devices by JAX's collectives and lax.ppermute only.
A program may use at most 256 MiB of HBM per device.

v0:
```python
import math

import jax
import jax.numpy as jnp
from jax import lax
from jax.sharding import PartitionSpec as P

D = 2048
HEADS = 16
SEQ_MAX = 2048
BLOCK = 256


eps_norm = 1e-05
neg_big = -1e30
beta_one = 0.9
beta_two = 0.95
adam_eps = 1e-08
learn_rate = 0.001
decay_rate = 0.1
step_count = 10.0
inv_root_two = 1.0 / math.sqrt(2.0)
inv_root_two_pi = 1.0 / math.sqrt(2.0 * math.pi)


def passed_along(value, axis, steps):
    count = lax.axis_size(axis)
    first, last = (max(0, -steps), min(count, count - steps))
    return lax.ppermute(value, axis, [(source, source + steps) for source in range(first, last)])


def token_labels(global_rows, seq_lengths, total_rows):
    starts = jnp.cumsum(seq_lengths) - seq_lengths
    after = (global_rows[:, None] >= starts[None, :]).astype(jnp.int32)
    segment = jnp.sum(after, axis=1) - 1
    chosen = segment[:, None] == jnp.arange(seq_lengths.shape[0], dtype=jnp.int32)[None, :]
    begin = jnp.sum(jnp.where(chosen, starts[None, :], 0), axis=1)
    block = (global_rows - begin) // BLOCK
    valid = (global_rows >= 0) & (global_rows < total_rows)
    return (segment, block, valid)


def layer_norm(rows, gain, bias):
    mean = jnp.mean(rows, axis=1, keepdims=True)
    centred = rows - mean
    rstd = lax.rsqrt(jnp.mean(centred * centred, axis=1, keepdims=True) + eps_norm)
    normed = centred * rstd
    return (normed * gain + bias, normed, rstd)


def norm_back(grad_out, normed, rstd, gain):
    scaled = grad_out * gain
    inner = (
        scaled
        - jnp.mean(scaled, axis=1, keepdims=True)
        - normed * jnp.mean(scaled * normed, axis=1, keepdims=True)
    )
    return (inner * rstd, jnp.sum(grad_out * normed, axis=0), jnp.sum(grad_out, axis=0))


def gelu_slope(values):
    return (
        0.5 * (1.0 + lax.erf(values * inv_root_two))
        + values * jnp.exp(-0.5 * values * values) * inv_root_two_pi
    )


def split_heads(values, head_size):
    return values.reshape(values.shape[0], -1, head_size)


def attention_probs(query, keys, allowed, scale, lse_kept):
    raw = jnp.einsum("qhd,khd->hqk", query, keys, preferred_element_type=jnp.float32) * scale
    masked = jnp.where(allowed[None], raw, neg_big)
    if lse_kept is None:
        top = jnp.max(masked, axis=2, keepdims=True)
        lse = top + jnp.log(jnp.sum(jnp.exp(masked - top), axis=2, keepdims=True))
    else:
        lse = lse_kept
    return (jnp.exp(masked - lse), lse)


def adam_update(master, grad, first, second, factor, decays):
    clipped = grad * factor
    first_new = beta_one * first + (1.0 - beta_one) * clipped
    second_new = beta_two * second + (1.0 - beta_two) * clipped * clipped
    fix_one = 1.0 - beta_one**step_count
    fix_two = 1.0 - beta_two**step_count
    update = first_new / fix_one / (jnp.sqrt(second_new / fix_two) + adam_eps)
    amount = learn_rate * (update + decay_rate * decays * master)
    return (amount, first_new, second_new)


def per_device(
    tokens,
    cotangent,
    w_qkv,
    w_out,
    w_up,
    w_down,
    norm_gains,
    norm_biases,
    m_qkv,
    m_out,
    m_up,
    m_down,
    m_gains,
    m_biases,
    v_qkv,
    v_out,
    v_up,
    v_down,
    v_gains,
    v_biases,
    seq_lengths,
    decay_mask,
):
    rows = tokens.shape[0]
    ctx_count = lax.axis_size("ctx")
    ctx_place = lax.axis_index("ctx")
    tp_place = lax.axis_index("tp")
    total_rows = rows * ctx_count
    head_size = D // HEADS
    scale = head_size ** (-0.5)
    reach = SEQ_MAX // rows
    offsets = [-1] + list(range(1, reach + 1))
    local_rows = jnp.arange(rows, dtype=jnp.int32)
    full = (
        lax.all_gather(w_qkv.astype(jnp.bfloat16), "ctx", axis=1, tiled=True),
        lax.all_gather(w_out.astype(jnp.bfloat16), "ctx", axis=1, tiled=True),
        lax.all_gather(w_up.astype(jnp.bfloat16), "ctx", axis=0, tiled=True),
        lax.all_gather(w_down.astype(jnp.bfloat16), "ctx", axis=1, tiled=True),
        lax.all_gather(norm_gains.astype(jnp.bfloat16), "ctx", axis=1, tiled=True),
        lax.all_gather(norm_biases.astype(jnp.bfloat16), "ctx", axis=1, tiled=True),
    )
    qkv_full, out_full, up_full, down_full, gains_full, biases_full = full
    gains32 = gains_full.astype(jnp.float32)
    biases32 = biases_full.astype(jnp.float32)
    x32 = tokens.astype(jnp.float32)
    h1, normed1, rstd1 = layer_norm(x32, gains32[0], biases32[0])
    a1 = h1.astype(jnp.bfloat16)
    qkv = jnp.einsum("td,cdh->cth", a1, qkv_full, preferred_element_type=jnp.float32).astype(
        jnp.bfloat16
    )
    query = qkv[0]
    kv_own = qkv[1:]
    own_rows = ctx_place * rows + local_rows
    key_rows = [own_rows]
    for offset in offsets:
        key_rows.append((ctx_place - offset) * rows + local_rows)
    key_rows = jnp.concatenate(key_rows)
    q_seg, q_blk, _ = token_labels(own_rows, seq_lengths, total_rows)
    k_seg, k_blk, k_valid = token_labels(key_rows, seq_lengths, total_rows)
    allowed = (
        k_valid[None, :] & (k_seg[None, :] == q_seg[:, None]) & (k_blk[None, :] <= q_blk[:, None])
    )
    pieces = [kv_own]
    for offset in offsets:
        pieces.append(passed_along(kv_own, "ctx", offset))
    kv_all = jnp.concatenate(pieces, axis=1)
    q3 = split_heads(query, head_size)
    k3 = split_heads(kv_all[0], head_size)
    v3 = split_heads(kv_all[1], head_size)
    prob, lse = attention_probs(q3, k3, allowed, scale, None)
    prob_low = prob.astype(jnp.bfloat16)
    attn_vals = jnp.einsum("hqk,khd->qhd", prob_low, v3, preferred_element_type=jnp.float32)
    attn_vals = attn_vals.reshape(rows, -1).astype(jnp.bfloat16)
    attn = lax.psum(jnp.dot(attn_vals, out_full, preferred_element_type=jnp.float32), "tp")
    y1 = x32 + attn
    h2, normed2, rstd2 = layer_norm(y1, gains32[1], biases32[1])
    a2 = h2.astype(jnp.bfloat16)
    up = jnp.dot(a2, up_full, preferred_element_type=jnp.float32)
    act_low = jax.nn.gelu(up, approximate=False).astype(jnp.bfloat16)
    mixed = lax.psum(
        jnp.dot(act_low, down_full, preferred_element_type=jnp.float32).astype(jnp.bfloat16), "tp"
    ).astype(jnp.float32)
    block_out = (y1 + mixed).astype(jnp.bfloat16)
    grad_down = jnp.dot(act_low.T, cotangent, preferred_element_type=jnp.float32)
    grad_act = jnp.dot(cotangent, down_full.T, preferred_element_type=jnp.float32)
    grad_up_in = (grad_act * gelu_slope(up)).astype(jnp.bfloat16)
    grad_up = jnp.dot(a2.T, grad_up_in, preferred_element_type=jnp.float32)
    grad_h2 = lax.psum(jnp.dot(grad_up_in, up_full.T, preferred_element_type=jnp.float32), "tp")
    grad_y1_norm, gain_two, bias_two = norm_back(grad_h2, normed2, rstd2, gains32[1])
    grad_y1 = cotangent.astype(jnp.float32) + grad_y1_norm
    grad_attn = grad_y1.astype(jnp.bfloat16)
    grad_outw = jnp.dot(attn_vals.T, grad_attn, preferred_element_type=jnp.float32)
    grad_vals = jnp.dot(grad_attn, out_full.T, preferred_element_type=jnp.float32).astype(
        jnp.bfloat16
    )
    prob, _ = attention_probs(q3, k3, allowed, scale, lse)
    prob_low = prob.astype(jnp.bfloat16)
    g3 = split_heads(grad_vals, head_size)
    grad_prob = jnp.einsum("qhd,khd->hqk", g3, v3, preferred_element_type=jnp.float32)
    inner = jnp.sum(prob * grad_prob, axis=2, keepdims=True)
    grad_scores = (prob * (grad_prob - inner)).astype(jnp.bfloat16)
    grad_query = (
        jnp.einsum("hqk,khd->qhd", grad_scores, k3, preferred_element_type=jnp.float32) * scale
    )
    grad_keys = (
        jnp.einsum("hqk,qhd->khd", grad_scores, q3, preferred_element_type=jnp.float32) * scale
    )
    grad_values = jnp.einsum("hqk,qhd->khd", prob_low, g3, preferred_element_type=jnp.float32)
    kv_grad = jnp.stack(
        (grad_keys.reshape(grad_keys.shape[0], -1), grad_values.reshape(grad_values.shape[0], -1))
    )
    kv_total = kv_grad[:, :rows]
    for place, offset in enumerate(offsets):
        piece = kv_grad[:, (place + 1) * rows : (place + 2) * rows]
        kv_total = kv_total + passed_along(piece, "ctx", -offset)
    grad_qkv_in = jnp.concatenate((grad_query.reshape(rows, -1)[None], kv_total), axis=0).astype(
        jnp.bfloat16
    )
    grad_qkvw = jnp.einsum("td,cth->cdh", a1, grad_qkv_in, preferred_element_type=jnp.float32)
    part_one = jnp.einsum("cth,cdh->td", grad_qkv_in, qkv_full, preferred_element_type=jnp.float32)
    grad_h1 = lax.psum(part_one, "tp")
    grad_x_norm, gain_one, bias_one = norm_back(grad_h1, normed1, rstd1, gains32[0])
    grad_tokens = (grad_y1 + grad_x_norm).astype(jnp.bfloat16)
    grad_gainw = jnp.stack((gain_one, gain_two))
    grad_biasw = jnp.stack((bias_one, bias_two))
    shards = (
        lax.psum_scatter(grad_qkvw, "ctx", scatter_dimension=1, tiled=True),
        lax.psum_scatter(grad_outw, "ctx", scatter_dimension=1, tiled=True),
        lax.psum_scatter(grad_up, "ctx", scatter_dimension=0, tiled=True),
        lax.psum_scatter(grad_down, "ctx", scatter_dimension=1, tiled=True),
        lax.psum_scatter(grad_gainw, "ctx", scatter_dimension=1, tiled=True),
        lax.psum_scatter(grad_biasw, "ctx", scatter_dimension=1, tiled=True),
    )
    matrix_sq = jnp.sum(shards[0] * shards[0]) + jnp.sum(shards[1] * shards[1])
    matrix_sq = matrix_sq + jnp.sum(shards[2] * shards[2]) + jnp.sum(shards[3] * shards[3])
    small_sq = jnp.sum(shards[4] * shards[4]) + jnp.sum(shards[5] * shards[5])
    local_sq = matrix_sq + jnp.where(tp_place == 0, small_sq, jnp.float32(0.0))
    total_sq = lax.psum(local_sq, ("ctx", "tp"))
    grad_norm = jnp.sqrt(total_sq)
    factor = 1.0 / jnp.maximum(grad_norm, 1.0)
    masters = (w_qkv, w_out, w_up, w_down, norm_gains, norm_biases)
    firsts = (m_qkv, m_out, m_up, m_down, m_gains, m_biases)
    seconds = (v_qkv, v_out, v_up, v_down, v_gains, v_biases)
    amounts, new_first, new_second = ([], [], [])
    for place in range(6):
        decays = decay_mask[place].astype(jnp.float32)
        amount, first_new, second_new = adam_update(
            masters[place], shards[place], firsts[place], seconds[place], factor, decays
        )
        amounts.append(amount)
        new_first.append(first_new)
        new_second.append(second_new)
    return (
        block_out,
        grad_tokens,
        grad_norm,
        shards[0],
        shards[1],
        shards[2],
        shards[3],
        shards[4],
        shards[5],
        amounts[0],
        amounts[1],
        amounts[2],
        amounts[3],
        amounts[4],
        amounts[5],
        new_first[0],
        new_first[1],
        new_first[2],
        new_first[3],
        new_first[4],
        new_first[5],
        new_second[0],
        new_second[1],
        new_second[2],
        new_second[3],
        new_second[4],
        new_second[5],
    )


def solution(mesh):
    return jax.shard_map(
        per_device,
        mesh=mesh,
        in_specs=(
            P("ctx", None),
            P("ctx", None),
            P(None, "ctx", "tp"),
            P("tp", "ctx"),
            P("ctx", "tp"),
            P("tp", "ctx"),
            P(None, "ctx"),
            P(None, "ctx"),
            P(None, "ctx", "tp"),
            P("tp", "ctx"),
            P("ctx", "tp"),
            P("tp", "ctx"),
            P(None, "ctx"),
            P(None, "ctx"),
            P(None, "ctx", "tp"),
            P("tp", "ctx"),
            P("ctx", "tp"),
            P("tp", "ctx"),
            P(None, "ctx"),
            P(None, "ctx"),
            P(),
            P(),
        ),
        out_specs=(
            P("ctx", None),
            P("ctx", None),
            P(),
            P(None, "ctx", "tp"),
            P("tp", "ctx"),
            P("ctx", "tp"),
            P("tp", "ctx"),
            P(None, "ctx"),
            P(None, "ctx"),
            P(None, "ctx", "tp"),
            P("tp", "ctx"),
            P("ctx", "tp"),
            P("tp", "ctx"),
            P(None, "ctx"),
            P(None, "ctx"),
            P(None, "ctx", "tp"),
            P("tp", "ctx"),
            P("ctx", "tp"),
            P("tp", "ctx"),
            P(None, "ctx"),
            P(None, "ctx"),
            P(None, "ctx", "tp"),
            P("tp", "ctx"),
            P("ctx", "tp"),
            P("tp", "ctx"),
            P(None, "ctx"),
            P(None, "ctx"),
        ),
        check_vma=False,
    )
```

profile of v0, /device:TPU:0, one launch (start us, length us, event | category | flops | bytes accessed | tf_op | source)
XLA Modules:
  0.0 1714.5 jit_solution(7258916373576961367)
XLA Ops:
  7.3 3.2 copy.83
  13.8 10.3 all_gather.19
  24.2 8.9 all_gather.18
  34.8 27.6 %all-gather.5.cloned.1.call-done = bf16[3,2048,512]{1,2,0:T(8,128)(2,1)} async-done(((bf16[3,256,512]{1,2,0:T(8,128)(2,1)}), bf16[3,2048,512]{1,2,0:T(8,128)(2,1)}) %all-gather.5.cloned.1.call-update) | async-done | bytes 6291472 | tf_op jit(solution)/shard_map/all_gather | solution.py:129
  62.5 6.6 fusion.48
  70.7 3.1 collective-permute-start.1
  73.8 3.4 collective-permute-start.2
  77.2 3.9 collective-permute-start.3
  85.0 21.3 %collective-permute-done.2 = bf16[2,512,512]{1,2,0:T(8,128)(2,1)S(1)} collective-permute-done((bf16[2,512,512]{1,2,0:T(8,128)(2,1)S(1)}, bf16[2,512,512]{1,2,0:T(8,128)(2,1)S(1)}, u32[]{:S(2)}, u32[]{:S(2)}) %collective-permute-start.2) | collective-permute-done | bytes 1048608 | tf_op jit(solution)/shard_map/ppermute | solution.py:29
  106.5 19.8 %collective-permute-done.3 = bf16[2,512,512]{1,2,0:T(8,128)(2,1)S(1)} collective-permute-done((bf16[2,512,512]{1,2,0:T(8,128)(2,1)S(1)}, bf16[2,512,512]{1,2,0:T(8,128)(2,1)S(1)}, u32[]{:S(2)}, u32[]{:S(2)}) %collective-permute-start.3) | collective-permute-done | bytes 1048608 | tf_op jit(solution)/shard_map/ppermute | solution.py:29
  126.4 27.4 %collective-permute-done.4 = bf16[2,512,512]{1,2,0:T(8,128)(2,1)S(1)} collective-permute-done((bf16[2,512,512]{1,2,0:T(8,128)(2,1)S(1)}, bf16[2,512,512]{1,2,0:T(8,128)(2,1)S(1)}, u32[]{:S(2)}, u32[]{:S(2)}) %collective-permute-start.4) | collective-permute-done | bytes 1048608 | tf_op jit(solution)/shard_map/ppermute | solution.py:29
  156.0 11.1 fusion
  167.1 11.9 exponential_reduce_fusion
  179.0 12.3 convolution_convert_fusion.3
  191.3 5.1 fusion.81
  196.5 2.7 convert_element_type.130
  202.5 159.6 %all-reduce.5.cloned.1.call-done = f32[512,2048]{1,0:T(8,128)} async-done(((f32[512,2048]{1,0:T(8,128)}), f32[512,2048]{1,0:T(8,128)}) %all-reduce.5.cloned.1.call-update) | async-done | bytes 4194320 | tf_op jit(solution)/shard_map/psum | solution.py:168
  362.0 3.4 fusion.75
  367.9 50.0 %all-gather.9.cloned.1.call-done = bf16[2048,2048]{1,0:T(8,128)(2,1)} async-done(((bf16[256,2048]{1,0:T(8,128)(2,1)}), bf16[2048,2048]{1,0:T(8,128)(2,1)}) %all-gather.9.cloned.1.call-update) | async-done | bytes 8388624 | tf_op jit(solution)/shard_map/all_gather | solution.py:131
  417.9 18.3 %fusion.19 = (bf16[512,2048]{1,0:T(8,128)(2,1)}, f32[512,2048]{1,0:T(8,128)}) fusion(bf16[2048,2048]{1,0:T(8,128)(2,1)} %all-gather.9.cloned.1.call-done, f32[512,2048]{1,0:T(8,128)} %copy-done.1, f32[2048]{0:T(1024)S(1)} %bitcast.102, f32[2048]{0:T(1024)S(1)} %bitcast.94, f32[512]{0:T(512)S(1)} %add_rsqrt_fusion, f32[512]{0:T(512)S(1)} %broadcast_multiply_fusion.4), kind=kOutput, calls=%fused_computation.42 | convolution fusion | flops 4368367616 | bytes 18894848 | tf_op jit(solution)/shard_map/dot_general | solution.py:172
  436.3 40.1 %all-gather.11.cloned.1.call-done = bf16[2048,2048]{1,0:T(8,128)(2,1)} async-done(((bf16[2048,256]{1,0:T(8,128)(2,1)}), bf16[2048,2048]{1,0:T(8,128)(2,1)}) %all-gather.11.cloned.1.call-update) | async-done | bytes 8388624 | tf_op jit(solution)/shard_map/all_gather | solution.py:132
  476.4 9.3 fusion.25
  487.0 6.1 fusion.82
  493.4 9.8 convolution_convert_fusion
  503.3 145.0 %all-reduce.9.cloned.1.call-done = f32[512,2048]{1,0:T(8,128)} async-done(((f32[512,2048]{1,0:T(8,128)}), f32[512,2048]{1,0:T(8,128)}) %all-reduce.9.cloned.1.call-update) | async-done | bytes 4194320 | tf_op jit(solution)/shard_map/psum | solution.py:182
  648.3 4.4 multiply_reduce_fusion.1
  652.7 84.1 %all-reduce.7.cloned.1.call-done = bf16[512,2048]{1,0:T(8,128)(2,1)} async-done(((bf16[512,2048]{1,0:T(8,128)(2,1)}), bf16[512,2048]{1,0:T(8,128)(2,1)}) %all-reduce.7.cloned.1.call-update) | async-done | bytes 2097168 | tf_op jit(solution)/shard_map/psum | solution.py:174
  736.8 7.0 multiply_add_fusion
  747.1 21.0 %multiply_reduce_fusion = (f32[4,512]{1,0:T(4,128)S(1)}, f32[4,512,3072]{2,1,0:T(8,128)}) fusion(f32[4,512,3072]{2,1,0:T(8,128)} %get-tuple-element.158, f32[4,512]{1,0:T(4,128)S(1)} %log_add_fusion, pred[512,3072]{1,0:T(8,128)(4,1)S(1)} %compare_and_fusion, bf16[512,4,128]{0,2,1:T(8,128)(2,1)S(1)} %bitcast.86, bf16[3072,4,128]{0,2,1:T(8,128)(2,1)} %bitcast.77), kind=kOutput, calls=%fused_computation.1 | convolution fusion | flops 1642067968 | bytes 55590912 | tf_op jit(solution)/shard_map/qhd,khd->hqk/dot_general | solution.py:193
  768.1 14.9 fusion.64
  783.0 17.2 %multiply_convert_fusion = bf16[4,512,3072]{2,1,0:T(8,128)(2,1)S(1)} fusion(f32[4,512,3072]{2,1,0:T(8,128)} %get-tuple-element.162, f32[4,512,3072]{2,1,0:T(8,128)} %get-tuple-element.158, f32[4,512]{1,0:T(4,128)S(1)} %get-tuple-element.161, f32[4,512]{1,0:T(4,128)S(1)} %log_add_fusion, pred[512,3072]{1,0:T(8,128)(4,1)S(1)} %compare_and_fusion), kind=kLoop, calls=%fused_computation | loop fusion | flops 37748736 | bytes 64503808 | tf_op jit(solution)/shard_map/convert_element_type | solution.py:195
  800.3 5.1 convolution_multiply_fusion
  806.7 6.5 copy.88
  813.2 6.6 copy.89
  819.8 7.5 fusion.43
  832.5 4.3 collective-permute-start.5
  836.8 8.9 fusion.49
  845.9 30.8 %collective-permute-done.9 = f32[2,512,512]{2,1,0:T(8,128)S(1)} collective-permute-done((f32[2,512,512]{2,1,0:T(8,128)}, f32[2,512,512]{2,1,0:T(8,128)S(1)}, u32[]{:S(2)}, u32[]{:S(2)}) %collective-permute-start.9) | collective-permute-done | bytes 2097184 | tf_op jit(solution)/shard_map/ppermute | solution.py:29
  876.8 3.9 collective-permute-done.7
  880.6 5.3 fusion.46
  886.9 7.7 convolution_bitcast_fusion.1
  895.6 5.4 fusion.50
  901.2 254.9 %all-reduce.11.cloned.1.call-done = f32[512,2048]{1,0:T(8,128)} async-done(((f32[512,2048]{1,0:T(8,128)}), f32[512,2048]{1,0:T(8,128)}) %all-reduce.11.cloned.1.call-update) | async-done | bytes 4194320 | tf_op jit(solution)/shard_map/psum | solution.py:215
  1156.1 4.0 fusion.15
  1163.0 8.5 convolution_bitcast_fusion
  1172.2 14.0 fusion.67
  1186.5 12.7 fusion.83
  1201.1 3.1 copy.93
  1204.2 3.0 copy.94
  1212.3 38.1 %reduce-scatter.19.cloned.1.call-done = f32[256,2]{1,0:T(8,128)} async-done(((f32[2048,2]{1,0:T(8,128)}), f32[256,2]{1,0:T(8,128)}) %reduce-scatter.19.cloned.1.call-update) | async-done | bytes 2064
  1251.3 39.2 %reduce-scatter.21.cloned.1.call-done = f32[256,2]{1,0:T(8,128)} async-done(((f32[2048,2]{1,0:T(8,128)}), f32[256,2]{1,0:T(8,128)}) %reduce-scatter.21.cloned.1.call-update) | async-done | bytes 2064
  1294.0 92.7 %reduce-scatter.11.cloned.1.call-done = f32[3,256,512]{1,2,0:T(8,128)} async-done(((f32[3,2048,512]{1,2,0:T(8,128)}), f32[3,256,512]{1,2,0:T(8,128)}) %reduce-scatter.11.cloned.1.call-update) | async-done | bytes 1572880 | tf_op jit(solution)/shard_map/reduce_scatter | solution.py:221
  1390.4 116.8 %reduce-scatter.15.cloned.1.call-done = f32[256,2048]{1,0:T(8,128)} async-done(((f32[2048,2048]{1,0:T(8,128)}), f32[256,2048]{1,0:T(8,128)}) %reduce-scatter.15.cloned.1.call-update) | async-done | bytes 2097168 | tf_op jit(solution)/shard_map/reduce_scatter | solution.py:223
  1507.2 2.7 multiply_reduce_fusion.7
  1510.6 117.0 %reduce-scatter.17.cloned.1.call-done = f32[2048,256]{1,0:T(8,128)} async-done(((f32[2048,2048]{1,0:T(8,128)}), f32[2048,256]{1,0:T(8,128)}) %reduce-scatter.17.cloned.1.call-update) | async-done | bytes 2097168 | tf_op jit(solution)/shard_map/reduce_scatter | solution.py:224
  1627.7 2.7 multiply_reduce_fusion.6
  1631.0 5.3 fusion.14
  1636.4 39.5 %psum.39 = f32[]{:T(128)} all-reduce(f32[]{:T(128)S(6)} %add.330), channel_id=1, replica_groups=mesh['ctx'=8,'tp'=4] {'ctx','tp'}, use_global_device_ids=true, to_apply=%region_36.37 | all-reduce | flops 1 | bytes 8 | tf_op jit(solution)/shard_map/psum | solution.py:232
  1676.6 5.7 add_multiply_fusion.2
  1682.3 3.1 copy.97
  1685.5 3.0 copy.98
  1693.0 3.0 add_multiply_fusion.3
  1696.0 7.0 add_multiply_fusion.1
  1703.0 3.6 add_multiply_fusion
  (196 shorter events, 49.5 us)
Async XLA Ops:
  7.2 5.7 copy-start.16
  7.2 6.5 copy-start.33
  7.2 16.9 copy-start.31
  7.2 25.8 %copy-start.2 = (bf16[512,2048]{1,0:T(8,128)(2,1)S(1)}, bf16[512,2048]{1,0:T(8,128)(2,1)}, u32[]{:S(2)}) copy-start(bf16[512,2048]{1,0:T(8,128)(2,1)} %param.22) | copy-start | bytes 6291460
  7.2 55.2 %all-gather.5.cloned.1.call-start = ((), (), s32[]{:S(2)}) async-start(), calls=%async_computation.6 | async-start | bytes 7077888 | tf_op jit(solution)/shard_map/all_gather | solution.py:129
  10.5 23.7 %copy-start.44 = (s32[4]{0:T(128)S(1)}, s32[4]{0:T(128)}, u32[]{:S(2)}) copy-start(s32[4]{0:T(128)} %param.42) | copy-start | bytes 52
  12.9 178.5 %all-gather.7.cloned.1.call-start = ((), (), s32[]{:S(2)}) async-start(), calls=%async_computation.7 | async-start | bytes 2359296 | tf_op jit(solution)/shard_map/all_gather | solution.py:130
  13.7 348.3 %all-reduce.5.cloned.1.call-start = ((), (), s32[]{:S(2)}) async-start(), calls=%async_computation.8 | async-start | bytes 8388608 | tf_op jit(solution)/shard_map/psum | solution.py:168
  24.1 44.9 %copy-start.37 = (f32[1,2048]{1,0:T(1,128)}, f32[1,2048]{1,0:T(1,128)S(1)}, u32[]{:S(2)}) copy-start(f32[1,2048]{1,0:T(1,128)S(1)} %get-tuple-element.150) | copy-start | bytes 24580
  24.2 393.8 %copy-start.35 = (f32[1,2048]{1,0:T(1,128)}, f32[1,2048]{1,0:T(1,128)S(1)}, u32[]{:S(2)}) copy-start(f32[1,2048]{1,0:T(1,128)S(1)} %get-tuple-element.149) | copy-start | bytes 24580
  33.1 36.0 %copy-start.22 = (f32[1,2048]{1,0:T(1,128)}, f32[1,2048]{1,0:T(1,128)S(1)}, u32[]{:S(2)}) copy-start(f32[1,2048]{1,0:T(1,128)S(1)} %get-tuple-element.148) | copy-start | bytes 24580
  33.5 35.6 %copy-start.24 = (f32[512]{0:T(512)}, f32[512]{0:T(512)S(1)}, u32[]{:S(2)}) copy-start(f32[512]{0:T(512)S(1)} %broadcast_multiply_fusion.5) | copy-start | bytes 6148
  34.2 34.9 %copy-start.26 = (f32[512]{0:T(512)}, f32[512]{0:T(512)S(1)}, u32[]{:S(2)}) copy-start(f32[512]{0:T(512)S(1)} %add_rsqrt_fusion.1) | copy-start | bytes 6148
  69.3 15.4 collective-permute-start
  70.7 14.2 collective-permute-start.1
  73.8 32.5 %collective-permute-start.2 = (bf16[2,512,512]{1,2,0:T(8,128)(2,1)S(1)}, bf16[2,512,512]{1,2,0:T(8,128)(2,1)S(1)}, u32[]{:S(2)}, u32[]{:S(2)}) collective-permute-start(bf16[2,512,512]{1,2,0:T(8,128)(2,1)S(1)} %get-tuple-element.145), channel_id=1, source_target_pairs={{0,8},{4,12},{8,16},{12,20},{16,24},{20,28},{1,9},{5,13},{9,17},{1... | collective-permute-start | bytes 3145736 | tf_op jit(solution)/shard_map/ppermute | solution.py:29
  77.2 49.0 %collective-permute-start.3 = (bf16[2,512,512]{1,2,0:T(8,128)(2,1)S(1)}, bf16[2,512,512]{1,2,0:T(8,128)(2,1)S(1)}, u32[]{:S(2)}, u32[]{:S(2)}) collective-permute-start(bf16[2,512,512]{1,2,0:T(8,128)(2,1)S(1)} %get-tuple-element.145), channel_id=1, source_target_pairs={{0,12},{4,16},{8,20},{12,24},{16,28},{1,13},{5,17},{9,21},{13,25},... | collective-permute-start | bytes 3145736 | tf_op jit(solution)/shard_map/ppermute | solution.py:29
  81.1 72.7 %collective-permute-start.4 = (bf16[2,512,512]{1,2,0:T(8,128)(2,1)S(1)}, bf16[2,512,512]{1,2,0:T(8,128)(2,1)S(1)}, u32[]{:S(2)}, u32[]{:S(2)}) collective-permute-start(bf16[2,512,512]{1,2,0:T(8,128)(2,1)S(1)} %get-tuple-element.145), channel_id=1, source_target_pairs={{0,16},{4,20},{8,24},{12,28},{1,17},{5,21},{9,25},{13,29},{2,18},{... | collective-permute-start | bytes 3145736 | tf_op jit(solution)/shard_map/ppermute | solution.py:29
  84.7 71.3 %copy-start.11 = (bf16[1,512,512]{1,2,0:T(8,128)(2,1)}, bf16[1,512,512]{1,2,0:T(8,128)(2,1)S(1)}, u32[]{:S(2)}) copy-start(bf16[1,512,512]{1,2,0:T(8,128)(2,1)S(1)} %slice.86) | copy-start | bytes 1572868
  156.0 11.1 copy-start.4
  191.3 5.2 copy-start.13
  196.5 221.5 %all-gather.9.cloned.1.call-start = ((), (), s32[]{:S(2)}) async-start(), calls=%async_computation.9 | async-start | bytes 9437184 | tf_op jit(solution)/shard_map/all_gather | solution.py:131
  199.3 277.1 %all-gather.11.cloned.1.call-start = ((), (), s32[]{:S(2)}) async-start(), calls=%async_computation.10 | async-start | bytes 9437184 | tf_op jit(solution)/shard_map/all_gather | solution.py:132
  202.0 446.3 %all-reduce.9.cloned.1.call-start = ((), (), s32[]{:S(2)}) async-start(), calls=%async_computation.12 | async-start | bytes 8388608 | tf_op jit(solution)/shard_map/psum | solution.py:182
  476.4 10.6 copy-start.43
  493.1 243.6 %all-reduce.7.cloned.1.call-start = ((), (), s32[]{:S(2)}) async-start(), calls=%async_computation.11 | async-start | bytes 4194304 | tf_op jit(solution)/shard_map/psum | solution.py:174
  503.2 652.8 %all-reduce.11.cloned.1.call-start = ((), (), s32[]{:S(2)}) async-start(), calls=%async_computation.13 | async-start | bytes 8388608 | tf_op jit(solution)/shard_map/psum | solution.py:215
  736.8 9.0 copy-start.15
  743.8 2.1 copy-start.6
  783.0 17.2 %copy-start.12 = (bf16[1,512,512]{1,2,0:T(8,128)(2,1)S(1)}, bf16[1,512,512]{1,2,0:T(8,128)(2,1)}, u32[]{:S(2)}) copy-start(bf16[1,512,512]{1,2,0:T(8,128)(2,1)} %copy-done.11) | copy-start | bytes 1572868
  800.3 6.5 copy-start
  819.8 17.0 copy-start.5
  827.3 49.5 %collective-permute-start.9 = (f32[2,512,512]{2,1,0:T(8,128)}, f32[2,512,512]{2,1,0:T(8,128)S(1)}, u32[]{:S(2)}, u32[]{:S(2)}) collective-permute-start(f32[2,512,512]{2,1,0:T(8,128)} %get-tuple-element.139), channel_id=1, source_target_pairs={{16,0},{20,4},{24,8},{28,12},{17,1},{21,5},{25,9},{29,13},{18,2},{... | collective-permute-start | bytes 6291464 | tf_op jit(solution)/shard_map/ppermute | solution.py:29
  828.6 48.2 %collective-permute-start.8 = (f32[2,512,512]{2,1,0:T(8,128)}, f32[2,512,512]{2,1,0:T(8,128)}, u32[]{:S(2)}, u32[]{:S(2)}) collective-permute-start(f32[2,512,512]{2,1,0:T(8,128)} %get-tuple-element.140), channel_id=1, source_target_pairs={{12,0},{16,4},{20,8},{24,12},{28,16},{13,1},{17,5},{21,9},{25,13},... | collective-permute-start | bytes 6291464 | tf_op jit(solution)/shard_map/ppermute | solution.py:29
  829.9 50.8 %collective-permute-start.7 = (f32[2,512,512]{2,1,0:T(8,128)}, f32[2,512,512]{2,1,0:T(8,128)}, u32[]{:S(2)}, u32[]{:S(2)}) collective-permute-start(f32[2,512,512]{2,1,0:T(8,128)} %get-tuple-element.138), channel_id=1, source_target_pairs={{8,0},{12,4},{16,8},{20,12},{24,16},{28,20},{9,1},{13,5},{17,9},{2... | collective-permute-start | bytes 6291464 | tf_op jit(solution)/shard_map/ppermute | solution.py:29
  831.2 49.5 %collective-permute-start.6 = (f32[2,512,512]{2,1,0:T(8,128)}, f32[2,512,512]{2,1,0:T(8,128)}, u32[]{:S(2)}, u32[]{:S(2)}) collective-permute-start(f32[2,512,512]{2,1,0:T(8,128)} %get-tuple-element.137), channel_id=1, source_target_pairs={{4,0},{8,4},{12,8},{16,12},{20,16},{24,20},{28,24},{5,1},{9,5},{13... | collective-permute-start | bytes 6291464 | tf_op jit(solution)/shard_map/ppermute | solution.py:29
  832.5 48.2 %collective-permute-start.5 = (f32[2,512,512]{2,1,0:T(8,128)}, f32[2,512,512]{2,1,0:T(8,128)}, u32[]{:S(2)}, u32[]{:S(2)}) collective-permute-start(f32[2,512,512]{2,1,0:T(8,128)} %get-tuple-element.136), channel_id=1, source_target_pairs={{0,4},{4,8},{8,12},{12,16},{16,20},{20,24},{24,28},{1,5},{5,9},{9,... | collective-permute-start | bytes 6291464 | tf_op jit(solution)/shard_map/ppermute | solution.py:29
  845.9 40.0 %copy-start.21 = (bf16[1,512,512]{2,1,0:T(8,128)(2,1)}, bf16[1,512,512]{2,1,0:T(8,128)(2,1)S(1)}, u32[]{:S(2)}) copy-start(bf16[1,512,512]{2,1,0:T(8,128)(2,1)S(1)} %copy.90) | copy-start | bytes 1572868
  894.6 315.9 %reduce-scatter.13.cloned.1.call-start = ((), (), s32[]{:S(2)}) async-start(), calls=%async_computation.15 | async-start | bytes 4718592 | tf_op jit(solution)/shard_map/reduce_scatter | solution.py:222
  901.1 255.0 %copy-start.3 = (bf16[512,2048]{1,0:T(8,128)(2,1)S(1)}, bf16[512,2048]{1,0:T(8,128)(2,1)}, u32[]{:S(2)}) copy-start(bf16[512,2048]{1,0:T(8,128)(2,1)} %param.22) | copy-start | bytes 6291460
  901.1 255.0 %copy-start.23 = (f32[1,2048]{1,0:T(1,128)S(1)}, f32[1,2048]{1,0:T(1,128)}, u32[]{:S(2)}) copy-start(f32[1,2048]{1,0:T(1,128)} %copy-done.22) | copy-start | bytes 24580
  901.1 255.0 %copy-start.25 = (f32[512]{0:T(512)S(1)}, f32[512]{0:T(512)}, u32[]{:S(2)}) copy-start(f32[512]{0:T(512)} %copy-done.24) | copy-start | bytes 6148
  901.1 255.0 %copy-start.27 = (f32[512]{0:T(512)S(1)}, f32[512]{0:T(512)}, u32[]{:S(2)}) copy-start(f32[512]{0:T(512)} %copy-done.26) | copy-start | bytes 6148
  901.1 261.9 %copy-start.20 = (bf16[2,512,512]{2,1,0:T(8,128)(2,1)S(1)}, bf16[2,512,512]{2,1,0:T(8,128)(2,1)}, u32[]{:S(2)}) copy-start(bf16[2,512,512]{2,1,0:T(8,128)(2,1)} %copy-done.19) | copy-start | bytes 3145732
  901.1 261.9 %copy-start.38 = (f32[1,2048]{1,0:T(1,128)S(1)}, f32[1,2048]{1,0:T(1,128)}, u32[]{:S(2)}) copy-start(f32[1,2048]{1,0:T(1,128)} %copy-done.37) | copy-start | bytes 24580
  901.1 349.2 %reduce-scatter.19.cloned.1.call-start = ((), (), s32[]{:S(2)}) async-start(), calls=%async_computation.18 | async-start | bytes 1179648
  1161.5 129.0 %reduce-scatter.21.cloned.1.call-start = ((), (), s32[]{:S(2)}) async-start(), calls=%async_computation.19 | async-start | bytes 1179648
  1163.0 223.7 %reduce-scatter.11.cloned.1.call-start = ((), (), s32[]{:S(2)}) async-start(), calls=%async_computation.14 | async-start | bytes 14155776 | tf_op jit(solution)/shard_map/reduce_scatter | solution.py:221
  1171.6 335.7 %reduce-scatter.15.cloned.1.call-start = ((), (), s32[]{:S(2)}) async-start(), calls=%async_computation.16 | async-start | bytes 18874368 | tf_op jit(solution)/shard_map/reduce_scatter | solution.py:223
  1186.3 441.4 %reduce-scatter.17.cloned.1.call-start = ((), (), s32[]{:S(2)}) async-start(), calls=%async_computation.17 | async-start | bytes 18874368 | tf_op jit(solution)/shard_map/reduce_scatter | solution.py:224
  1251.3 438.8 %copy-start.28 = (f32[2,256]{1,0:T(2,128)}, f32[2,256]{1,0:T(2,128)S(1)}, u32[]{:S(2)}) copy-start(f32[2,256]{1,0:T(2,128)S(1)} %copy.107) | copy-start | bytes 6148
  1291.5 399.2 %copy-start.29 = (f32[2,256]{1,0:T(2,128)}, f32[2,256]{1,0:T(2,128)S(1)}, u32[]{:S(2)}) copy-start(f32[2,256]{1,0:T(2,128)S(1)} %copy.109) | copy-start | bytes 6148
  1682.3 7.8 copy-start.32
  1682.3 7.8 copy-start.39
  1682.3 7.8 copy-start.40
  1682.3 8.4 copy-start.34
  1682.3 8.4 copy-start.41
  1682.3 8.4 copy-start.42
  1682.3 9.0 copy-start.7
  1693.0 3.0 copy-start.8
  1696.0 7.0 copy-start.9
  1696.0 7.0 copy-start.10
  1696.0 7.0 copy-start.17
  1696.0 7.0 copy-start.18
  (6 other events, 6.7 us)
Sparse Core Ops, SparseCore 0:
  13.0 49.4 all-gather.4
  64.9 37.4 all-gather.6
  196.6 165.3 all-reduce.4
  364.5 53.3 all-gather.8
  420.4 55.9 all-gather.10
  493.3 154.9 all-reduce.8
  651.2 85.5 all-reduce.6
  894.7 261.2 all-reduce.10
  1160.0 50.3 reduce-scatter.12
  1214.3 36.0 reduce-scatter.18
  1254.4 36.0 reduce-scatter.20
  1294.3 92.3 reduce-scatter.10
  1391.2 115.9 reduce-scatter.14
  1511.7 115.9 reduce-scatter.16
where the time goes:
time: 1720 us; the launch traced here: 1710 us
  waiting for transfers between devices  1270 us (74%)
  matrix products  178 us (10%)
  other arithmetic  110 us (6%)
  blocking collectives  58.7 us (3%)
  local copies, waits for them, and re-layouts  50.4 us (3%)
  between operations  24.7 us (1%)
  starting transfers between devices  24.1 us (1%)
    psum x1, waiting for transfers between devices, per_device(): grad_h1 = lax.psum(part_one, 'tp')  255 us
    psum x1, waiting for transfers between devices, per_device(): lax.psum(jnp.dot(attn_vals, out_full, preferred_element_type=jnp.float32)...  160 us
    psum x1, waiting for transfers between devices, per_device(): lax.psum(jnp.dot(grad_up_in, up_full.T, preferred_element_type=jnp.float3...  145 us
    reduce_scatter x1, waiting for transfers between devices, per_device(): lax.psum_scatter(grad_down, 'ctx', scatter_dimension=1, tiled=True)  117 us
    reduce_scatter x1, waiting for transfers between devices, per_device(): lax.psum_scatter(grad_up, 'ctx', scatter_dimension=0, tiled=True)  117 us
    ppermute x10, waiting for transfers between devices, passed_along(): lax.ppermute(value, axis, [(source, source + steps) for source in range(f...  103 us
    reduce_scatter x1, waiting for transfers between devices, per_device(): lax.psum_scatter(grad_qkvw, 'ctx', scatter_dimension=1, tiled=True)  92.7 us
    psum x1, waiting for transfers between devices, per_device(): lax.psum(jnp.dot(act_low, down_full, preferred_element_type=jnp.float32)....  84.1 us
  transfers between devices with their start and end apart: 24, of which 17 were waited for; matrix products, arithmetic and copies ran while one was open for 10% of the time, Pallas kernels for 0%

commit v1 on v0

v1 whole, which is shorter than its diff:
```python
import functools
import math

import jax
import jax.numpy as jnp
from jax import lax
from jax.experimental import pallas as pl
from jax.experimental.pallas import tpu as pltpu
from jax.sharding import PartitionSpec as P

HEAD = 128
BLOCK = 256
Q_TILE = 256
K_TILE = 512

eps_norm = 1e-05
neg_big = -1e30
beta_one = 0.9
beta_two = 0.95
adam_eps = 1e-08
learn_rate = 0.001
decay_rate = 0.1
step_count = 10.0
inv_root_two = 1.0 / math.sqrt(2.0)
inv_root_two_pi = 1.0 / math.sqrt(2.0 * math.pi)
bf16 = jnp.bfloat16
f32 = jnp.float32


def ctx_xor(value, mask):
    count = lax.axis_size("ctx")
    return lax.ppermute(value, "ctx", [(place, place ^ mask) for place in range(count)])


def tp_shift(value, steps):
    count = lax.axis_size("tp")
    return lax.ppermute(value, "tp", [(place, (place + steps) % count) for place in range(count)])


def tp_gather(own):
    return [own] + [tp_shift(own, s) for s in range(1, lax.axis_size("tp"))]


def tp_scatter(partial):
    count = lax.axis_size("tp")
    rows = partial.shape[0] // count
    pieces = [partial[s * rows : (s + 1) * rows] for s in range(count)]
    got = [tp_shift(pieces[s], -s) for s in range(1, count)]
    total = pieces[0].astype(f32)
    for piece in got:
        total = total + piece.astype(f32)
    return total


def slots_to_rows(parts, tp_place):
    count = len(parts)
    rows = parts[0].shape[0]
    stacked = jnp.concatenate(parts, axis=0)
    order = [lax.rem(tp_place - j + count, count) * rows for j in range(count)]
    return jnp.concatenate([lax.dynamic_slice_in_dim(stacked, o, rows, 0) for o in order], axis=0)


def rows_to_slots(value, tp_place, count):
    rows = value.shape[0] // count
    order = [lax.rem(tp_place - s + count, count) * rows for s in range(count)]
    return jnp.concatenate([lax.dynamic_slice_in_dim(value, o, rows, 0) for o in order], axis=0)


def sum_over_all(value):
    ctx_bits = lax.axis_size("ctx").bit_length() - 1
    value = value + ctx_xor(value, 1)
    bit = 1
    while bit < ctx_bits:
        if bit + 1 < ctx_bits:
            low, high = 1 << bit, 1 << (bit + 1)
            one, two, three = (ctx_xor(value, low), ctx_xor(value, high), ctx_xor(value, low | high))
            value = (value + one) + (two + three)
            bit += 2
        else:
            value = value + ctx_xor(value, 1 << bit)
            bit += 1
    one, two, three = (tp_shift(value, 1), tp_shift(value, 2), tp_shift(value, 3))
    return (value + two) + (one + three)


def place_of(me, tp_place, mask, chunk, rows, chunks):
    part = rows // chunks
    inner = lax.rem(tp_place - chunk + chunks, chunks)
    return pl.multiple_of(jnp.bitwise_xor(me, mask) * rows + inner * part, part)


def scores_of(keys, query, lo, hi, base, scale):
    raw = lax.dot_general(keys, query, (((1,), (1,)), ((), ())), preferred_element_type=f32) * scale
    at = base + lax.broadcasted_iota(jnp.int32, raw.shape, 0)
    return jnp.where((at >= lo) & (at < hi), raw, neg_big)


def forward_kernel(rows, chunks, masks, scale, place, tiles, *refs):
    others = len(masks) - 1
    span, own = refs[0], refs[1]
    rest = refs[2 : 2 + others]
    out, out_t, lse_out, k_all, vt_all = refs[2 + others :]
    me, tp_place = place[0], place[1]
    part = rows // chunks
    for which, group in enumerate(masks):
        source = own if which == 0 else rest[which - 1]
        left = HEAD if which == 0 else 0
        for slot, mask in enumerate(group):
            for chunk in range(chunks):
                at = place_of(me, tp_place, mask, chunk, rows, chunks)
                top = slot * rows + chunk * part
                k_all[pl.ds(at, part), :] = source[top : top + part, left : left + HEAD]
                vt_all[:, pl.ds(at, part)] = source[top : top + part, left + HEAD : left + 2 * HEAD].T

    for tile in range(own.shape[0] // Q_TILE):
        cut = slice(tile * Q_TILE, (tile + 1) * Q_TILE)
        query = own[cut, :HEAD]
        lo, hi = span[0:1, cut], span[1:2, cut]

        def step(index, carry, query=query, lo=lo, hi=hi):
            top, total, acc = carry
            base = pl.multiple_of(index * K_TILE, K_TILE)
            scores = scores_of(k_all[pl.ds(base, K_TILE), :], query, lo, hi, base, scale)
            new_top = jnp.maximum(top, jnp.max(scores, axis=0, keepdims=True))
            fade = jnp.exp(top - new_top)
            prob = jnp.exp(scores - new_top)
            total = total * fade + jnp.sum(prob, axis=0, keepdims=True)
            acc = acc * fade + jnp.dot(
                vt_all[:, pl.ds(base, K_TILE)], prob.astype(bf16), preferred_element_type=f32
            )
            return (new_top, total, acc)

        start = (
            jnp.full((1, Q_TILE), neg_big, f32),
            jnp.zeros((1, Q_TILE), f32),
            jnp.zeros((HEAD, Q_TILE), f32),
        )
        top, total, acc = lax.fori_loop(tiles[0, tile], tiles[1, tile], step, start)
        result = acc / total
        out_t[:, cut] = result
        out[cut, :] = result.T.astype(bf16)
        lse_out[:, cut] = top + jnp.log(total)


def backward_kernel(rows, chunks, masks, scale, place, tiles, *refs):
    others = len(masks) - 1
    span, own, grad_out, out_t, lse_in = refs[:5]
    rest = refs[5 : 5 + others]
    dq_out, dkv_own = refs[5 + others : 7 + others]
    dkv_rest = refs[7 + others : 7 + 2 * others]
    k_all, kt_all, v_all, dk_all, dv_all = refs[7 + 2 * others :]
    me, tp_place = place[0], place[1]
    part = rows // chunks
    for which, group in enumerate(masks):
        source = own if which == 0 else rest[which - 1]
        left = HEAD if which == 0 else 0
        for slot, mask in enumerate(group):
            for chunk in range(chunks):
                at = place_of(me, tp_place, mask, chunk, rows, chunks)
                top = slot * rows + chunk * part
                keys = source[top : top + part, left : left + HEAD]
                k_all[pl.ds(at, part), :] = keys
                kt_all[:, pl.ds(at, part)] = keys.T
                v_all[pl.ds(at, part), :] = source[top : top + part, left + HEAD : left + 2 * HEAD]
    dk_all[...] = jnp.zeros_like(dk_all)
    dv_all[...] = jnp.zeros_like(dv_all)

    for tile in range(own.shape[0] // Q_TILE):
        cut = slice(tile * Q_TILE, (tile + 1) * Q_TILE)
        query, grad = own[cut, :HEAD], grad_out[cut, :]
        lo, hi, lse = span[0:1, cut], span[1:2, cut], lse_in[:, cut]
        inner = jnp.sum(grad.astype(f32).T * out_t[:, cut], axis=0, keepdims=True)

        def step(index, dq_t, query=query, grad=grad, lo=lo, hi=hi, lse=lse, inner=inner):
            base = pl.multiple_of(index * K_TILE, K_TILE)
            here = pl.ds(base, K_TILE)
            scores = scores_of(k_all[here, :], query, lo, hi, base, scale)
            prob = jnp.exp(scores - lse)
            grad_prob = lax.dot_general(
                v_all[here, :], grad, (((1,), (1,)), ((), ())), preferred_element_type=f32
            )
            grad_scores = (prob * (grad_prob - inner)).astype(bf16)
            dv_all[here, :] += jnp.dot(prob.astype(bf16), grad, preferred_element_type=f32)
            dk_all[here, :] += jnp.dot(grad_scores, query, preferred_element_type=f32)
            return dq_t + jnp.dot(kt_all[:, here], grad_scores, preferred_element_type=f32)

        dq_t = lax.fori_loop(
            tiles[0, tile], tiles[1, tile], step, jnp.zeros((HEAD, Q_TILE), f32)
        )
        dq_out[cut, :] = (dq_t * scale).T.astype(bf16)

    for which, group in enumerate(masks):
        target = dkv_own if which == 0 else dkv_rest[which - 1]
        for slot, mask in enumerate(group):
            for chunk in range(chunks):
                at = place_of(me, tp_place, mask, chunk, rows, chunks)
                top = slot * rows + chunk * part
                target[top : top + part, :HEAD] = (dk_all[pl.ds(at, part), :] * scale).astype(target.dtype)
                target[top : top + part, HEAD:] = dv_all[pl.ds(at, part), :].astype(target.dtype)


def in_vmem():
    return pl.BlockSpec(memory_space=pltpu.VMEM)


def in_smem():
    return pl.BlockSpec(memory_space=pltpu.SMEM)


def attention_forward(place, tiles, span, own, rest, rows, chunks, masks, total, scale):
    queries = own.shape[0]
    return pl.pallas_call(
        functools.partial(forward_kernel, rows, chunks, masks, scale),
        out_shape=(
            jax.ShapeDtypeStruct((queries, HEAD), bf16),
            jax.ShapeDtypeStruct((HEAD, queries), f32),
            jax.ShapeDtypeStruct((1, queries), f32),
        ),
        in_specs=[in_smem(), in_smem()] + [in_vmem()] * (2 + len(rest)),
        out_specs=(in_vmem(), in_vmem(), in_vmem()),
        scratch_shapes=[pltpu.VMEM((total, HEAD), bf16), pltpu.VMEM((HEAD, total), bf16)],
        compiler_params=pltpu.CompilerParams(vmem_limit_bytes=58 << 20),
        name="attention_forward",
    )(place, tiles, span, own, *rest)


def attention_backward(place, tiles, span, own, grad, out_t, lse, rest, rows, chunks, masks, total, scale):
    queries = own.shape[0]
    return pl.pallas_call(
        functools.partial(backward_kernel, rows, chunks, masks, scale),
        out_shape=(
            jax.ShapeDtypeStruct((queries, HEAD), bf16),
            jax.ShapeDtypeStruct((queries, 2 * HEAD), f32),
        )
        + tuple(jax.ShapeDtypeStruct(r.shape, bf16) for r in rest),
        in_specs=[in_smem(), in_smem()] + [in_vmem()] * (5 + len(rest)),
        out_specs=tuple(in_vmem() for _ in range(2 + len(rest))),
        scratch_shapes=[
            pltpu.VMEM((total, HEAD), bf16),
            pltpu.VMEM((HEAD, total), bf16),
            pltpu.VMEM((total, HEAD), bf16),
            pltpu.VMEM((total, HEAD), f32),
            pltpu.VMEM((total, HEAD), f32),
        ],
        compiler_params=pltpu.CompilerParams(vmem_limit_bytes=58 << 20),
        name="attention_backward",
    )(place, tiles, span, own, grad, out_t, lse, *rest)


def norm_parts(rows):
    mean = jnp.mean(rows, axis=1, keepdims=True)
    centred = rows - mean
    rstd = lax.rsqrt(jnp.mean(centred * centred, axis=1, keepdims=True) + eps_norm)
    return (centred * rstd, rstd)


def norm_back(grad_out, normed, rstd, gain):
    scaled = grad_out * gain
    inner = (
        scaled
        - jnp.mean(scaled, axis=1, keepdims=True)
        - normed * jnp.mean(scaled * normed, axis=1, keepdims=True)
    )
    return (inner * rstd, jnp.sum(grad_out * normed, axis=0), jnp.sum(grad_out, axis=0))


def adam_update(master, grad, first, second, factor, decays):
    clipped = grad * factor
    first_new = beta_one * first + (1.0 - beta_one) * clipped
    second_new = beta_two * second + (1.0 - beta_two) * clipped * clipped
    fix_one = 1.0 - beta_one**step_count
    fix_two = 1.0 - beta_two**step_count
    update = first_new / fix_one / (jnp.sqrt(second_new / fix_two) + adam_eps)
    amount = learn_rate * (update + decay_rate * decays * master)
    return (amount, first_new, second_new)


def key_span(positions, seq_lengths):
    ends = jnp.cumsum(seq_lengths)
    starts = ends - seq_lengths
    inside = (positions[:, None] >= starts[None, :]) & (positions[:, None] < ends[None, :])
    begin = jnp.sum(jnp.where(inside, starts[None, :], 0), axis=1)
    end = jnp.sum(jnp.where(inside, ends[None, :], 0), axis=1)
    block = (positions - begin) // BLOCK
    return (begin, jnp.minimum(begin + (block + 1) * BLOCK, end))


def per_device(
    tokens,
    cotangent,
    w_qkv,
    w_out,
    w_up,
    w_down,
    norm_gains,
    norm_biases,
    m_qkv,
    m_out,
    m_up,
    m_down,
    m_gains,
    m_biases,
    v_qkv,
    v_out,
    v_up,
    v_down,
    v_gains,
    v_biases,
    seq_lengths,
    decay_mask,
):
    rows, width = tokens.shape
    ctx_count, tp_count = lax.axis_size("ctx"), lax.axis_size("tp")
    ctx_place = lax.axis_index("ctx").astype(jnp.int32)
    tp_place = lax.axis_index("tp").astype(jnp.int32)
    total_rows = rows * ctx_count
    part_rows = rows // tp_count
    head_cols = w_out.shape[0]
    heads = head_cols // HEAD
    units = w_up.shape[1]
    ctx_cols = w_out.shape[1]
    scale = HEAD ** (-0.5)
    my_head = lax.rem(ctx_place // 2, heads)

    first_pack = jnp.concatenate((w_qkv[0], w_qkv[1], w_qkv[2], w_out.T), axis=1).astype(bf16)
    second_pack = jnp.concatenate((w_up, w_down.T), axis=1).astype(bf16)
    first_full = lax.all_gather(first_pack, "ctx", axis=0, tiled=True)
    second_pack, first_full = lax.optimization_barrier((second_pack, first_full))
    second_full = lax.all_gather(second_pack, "ctx", axis=0, tiled=True)
    qkv_full, out_full = first_full[:, : 3 * head_cols], first_full[:, 3 * head_cols :]
    up_full, down_full = second_full[:, :units], second_full[:, units:]

    small = jnp.concatenate((norm_gains, norm_biases), axis=0).astype(bf16)
    small = lax.all_gather(small, "ctx", axis=1, tiled=True).astype(f32)
    gain_one, gain_two, bias_one, bias_two = small[0], small[1], small[2], small[3]

    x_slots = rows_to_slots(tokens, tp_place, tp_count)
    c_slots = rows_to_slots(cotangent, tp_place, tp_count)
    normed, _ = norm_parts(x_slots.astype(f32))
    a1 = (normed * gain_one + bias_one).astype(bf16)

    group = [s << 1 for s in range(heads)]
    masks, rest_bits = ([group], [0] + list(range(heads.bit_length(), ctx_count.bit_length() - 1)))
    for bit in rest_bits:
        masks.append([m ^ (1 << bit) for g in masks for m in g])
    inner_rows = jnp.arange(part_rows, dtype=jnp.int32)
    positions = jnp.concatenate(
        [
            jnp.bitwise_xor(ctx_place, m) * rows + lax.rem(tp_place - s + tp_count, tp_count) * part_rows + inner_rows
            for m in group
            for s in range(tp_count)
        ]
    )
    lo, hi = key_span(positions, seq_lengths)
    span = jnp.stack((lo, hi))
    tiles = jnp.stack(
        (
            jnp.min(lo.reshape(-1, Q_TILE), axis=1) // K_TILE,
            (jnp.max(hi.reshape(-1, Q_TILE), axis=1) + K_TILE - 1) // K_TILE,
        )
    )
    place = jnp.stack((ctx_place, tp_place))

    qkv = jnp.dot(a1, qkv_full, preferred_element_type=f32).astype(bf16)
    own_parts = []
    for s in range(heads):
        at = jnp.bitwise_xor(my_head, s) * HEAD
        piece = jnp.concatenate(
            [lax.dynamic_slice_in_dim(qkv, j * head_cols + at, HEAD, 1) for j in range(3)], axis=1
        )
        own_parts.append(piece if s == 0 else ctx_xor(piece, s << 1))
    own = jnp.concatenate(own_parts, axis=0)
    rest, known = ([], own[:, HEAD:])
    for count, bit in enumerate(rest_bits):
        other = ctx_xor(known, 1 << bit)
        rest.append(other)
        if count + 1 < len(rest_bits):
            known = jnp.concatenate((known, other), axis=0)
    shape = (rows, tp_count, masks, total_rows, scale)
    mixed_low, mixed_t, lse = attention_forward(place, tiles, span, own, rest, *shape)

    back = [mixed_low[:rows]]
    for s in range(1, heads):
        back.append(ctx_xor(mixed_low[s * rows : (s + 1) * rows], s << 1))
    back = jnp.concatenate(back, axis=0)
    attn_vals = jnp.concatenate(
        [lax.dynamic_slice_in_dim(back, jnp.bitwise_xor(my_head, h) * rows, rows, 0) for h in range(heads)],
        axis=1,
    )
    attn = lax.dot_general(attn_vals, out_full, (((1,), (1,)), ((), ())), preferred_element_type=f32)
    x_own = x_slots[:part_rows].astype(f32)
    y1 = x_own + tp_scatter(attn.astype(bf16))
    normed2, rstd2 = norm_parts(y1)
    a2_own = (normed2 * gain_two + bias_two).astype(bf16)
    a2 = jnp.concatenate(tp_gather(a2_own), axis=0)

    grad_act = jnp.dot(c_slots, down_full, preferred_element_type=f32)
    up = jnp.dot(a2, up_full, preferred_element_type=f32)
    cdf = 0.5 * (1.0 + lax.erf(up * inv_root_two))
    act = (up * cdf).astype(bf16)
    slope = cdf + up * jnp.exp(-0.5 * up * up) * inv_root_two_pi
    grad_up_in = (grad_act * slope).astype(bf16)
    grad_h2 = lax.dot_general(grad_up_in, up_full, (((1,), (1,)), ((), ())), preferred_element_type=f32)
    grad_h2 = tp_scatter(grad_h2.astype(bf16))
    pair_left = jnp.stack((a2, c_slots))
    pair_right = jnp.stack((grad_up_in, act))
    pair_grad = jnp.einsum("btd,btf->bdf", pair_left, pair_right, preferred_element_type=f32).astype(bf16)
    pair_shard = lax.psum_scatter(pair_grad, "ctx", scatter_dimension=1, tiled=True)

    dx2, dg2, dc2 = norm_back(grad_h2, normed2, rstd2, gain_two)
    c_own = c_slots[:part_rows].astype(f32)
    grad_y1 = c_own + dx2
    grad_attn = jnp.concatenate(tp_gather(grad_y1.astype(bf16)), axis=0)
    mixed = lax.dot_general(act, down_full, (((1,), (1,)), ((), ())), preferred_element_type=f32).astype(bf16)
    mixed, grad_attn = lax.optimization_barrier((mixed, grad_attn))
    block_out = (y1 + tp_scatter(mixed)).astype(bf16)
    block_out = slots_to_rows(tp_gather(block_out), tp_place)

    grad_vals = jnp.dot(grad_attn, out_full, preferred_element_type=f32).astype(bf16)
    grad_outw = lax.dot_general(grad_attn, attn_vals, (((0,), (0,)), ((), ())), preferred_element_type=f32)
    out_shard = lax.psum_scatter(grad_outw.astype(bf16), "ctx", scatter_dimension=0, tiled=True)

    grads = []
    for s in range(heads):
        piece = lax.dynamic_slice_in_dim(grad_vals, jnp.bitwise_xor(my_head, s) * HEAD, HEAD, 1)
        grads.append(piece if s == 0 else ctx_xor(piece, s << 1))
    grads = jnp.concatenate(grads, axis=0)
    results = attention_backward(place, tiles, span, own, grads, mixed_t, lse, rest, *shape)
    grad_q, grad_kv, grad_rest = results[0], results[1], list(results[2:])
    for bit in reversed(rest_bits):
        got = ctx_xor(grad_rest.pop(), 1 << bit)
        cut = grad_kv.shape[0]
        grad_kv = grad_kv + got[:cut].astype(f32)
        grad_rest = split_add(grad_rest, got[cut:])
    grad_own = jnp.concatenate((grad_q, grad_kv.astype(bf16)), axis=1)
    back = [grad_own[:rows]]
    for s in range(1, heads):
        back.append(ctx_xor(grad_own[s * rows : (s + 1) * rows], s << 1))
    back = jnp.concatenate(back, axis=0)
    by_head = [
        lax.dynamic_slice_in_dim(back, jnp.bitwise_xor(my_head, h) * rows, rows, 0) for h in range(heads)
    ]
    grad_qkv_in = jnp.concatenate(
        [by_head[h][:, j * HEAD : (j + 1) * HEAD] for j in range(3) for h in range(heads)], axis=1
    )
    grad_qkvw = lax.dot_general(a1, grad_qkv_in, (((0,), (0,)), ((), ())), preferred_element_type=f32)
    qkv_shard = lax.psum_scatter(grad_qkvw.astype(bf16), "ctx", scatter_dimension=0, tiled=True)
    grad_h1 = lax.dot_general(grad_qkv_in, qkv_full, (((1,), (1,)), ((), ())), preferred_element_type=f32)
    grad_h1 = tp_scatter(grad_h1.astype(bf16))
    normed1, rstd1 = norm_parts(x_own)
    dx1, dg1, dc1 = norm_back(grad_h1, normed1, rstd1, gain_one)
    grad_tokens = (grad_y1 + dx1).astype(bf16)
    grad_tokens = slots_to_rows(tp_gather(grad_tokens), tp_place)

    qkv_grad = qkv_shard.astype(f32)
    out_grad = out_shard.astype(f32)
    up_grad = pair_shard[0].astype(f32)
    down_grad = pair_shard[1].astype(f32)
    square = jnp.sum(qkv_grad * qkv_grad) + jnp.sum(out_grad * out_grad)
    square = square + jnp.sum(up_grad * up_grad) + jnp.sum(down_grad * down_grad)
    lines = jnp.stack((dg1, dg2, dc1, dc2)).reshape(-1, HEAD)
    sent = jnp.concatenate((lines, jnp.full((8, HEAD), square, f32)), axis=0)
    total = sum_over_all(sent)
    small_grad = total[:-8].reshape(4, width)
    total_sq = total[-1, 0] + jnp.sum(small_grad * small_grad)
    grad_norm = jnp.sqrt(total_sq)
    factor = 1.0 / jnp.maximum(grad_norm, 1.0)
    small_own = lax.dynamic_slice_in_dim(small_grad, ctx_place * ctx_cols, ctx_cols, 1)

    shards = (
        jnp.stack([qkv_grad[:, j * head_cols : (j + 1) * head_cols] for j in range(3)]),
        out_grad.T,
        up_grad,
        down_grad.T,
        small_own[:2],
        small_own[2:],
    )
    masters = (w_qkv, w_out, w_up, w_down, norm_gains, norm_biases)
    firsts = (m_qkv, m_out, m_up, m_down, m_gains, m_biases)
    seconds = (v_qkv, v_out, v_up, v_down, v_gains, v_biases)
    amounts, new_first, new_second = ([], [], [])
    for index in range(6):
        decays = decay_mask[index].astype(f32)
        amount, first_new, second_new = adam_update(
            masters[index], shards[index], firsts[index], seconds[index], factor, decays
        )
        amounts.append(amount)
        new_first.append(first_new)
        new_second.append(second_new)
    return (block_out, grad_tokens, grad_norm, *shards, *amounts, *new_first, *new_second)


def split_add(arrays, extra):
    at, result = (0, [])
    for array in arrays:
        count = array.shape[0]
        result.append((array.astype(f32) + extra[at : at + count].astype(f32)).astype(array.dtype))
        at += count
    return result


def solution(mesh):
    small = P(None, "ctx")
    weights = (P(None, "ctx", "tp"), P("tp", "ctx"), P("ctx", "tp"), P("tp", "ctx"), small, small)
    rows = (P("ctx", None), P("ctx", None))
    return jax.shard_map(
        per_device,
        mesh=mesh,
        in_specs=(*rows, *weights, *weights, *weights, P(), P()),
        out_specs=(*rows, P(), *weights, *weights, *weights, *weights),
        check_vma=False,
    )
```

time: 1720 us -> 757 us (0.44)
  waiting for transfers between devices: 1270 us -> 379 us
  matrix products: 178 us -> 73.9 us
  starting transfers between devices: 24.1 us -> 92.8 us
  blocking collectives: 58.7 us -> 8.86 us
  Pallas kernels: 0 us -> 28.6 us
  other arithmetic: 110 us -> 81.9 us
    psum x4 -> x0, waiting for transfers between devices: 644 us -> none  [the longest x1 255 us: per_device(): grad_h1 = lax.psum(part_one, 'tp')]
    reduce_scatter x4 -> x3, waiting for transfers between devices: 327 us -> 0.02 us  [the longest x1 0.02 us: per_device(): lax.psum_scatter(pair_grad, 'ctx', scatter_dimension=1, tiled=True)]
    ppermute x10 -> x45, waiting for transfers between devices: 103 us -> 324 us  [the longest x27 269 us: tp_shift(): lax.ppermute(value, 'tp', [(place, (place + steps) % count) for place in...]
    dot_general x18 -> x11, matrix products: 178 us -> 73.9 us  [the longest x1 15.9 us: per_device(): jnp.einsum('btd,btf->bdf', pair_left, pair_right, preferred_element_type=...]
    unnamed x16 -> x5, waiting for transfers between devices: 77.5 us -> 0.08 us
    ppermute x10 -> x45, starting transfers between devices: 22.8 us -> 92.6 us  [the longest x27 74.8 us: tp_shift(): lax.ppermute(value, 'tp', [(place, (place + steps) % count) for place in...]
    all_gather x4 -> x2, waiting for transfers between devices: 118 us -> 55 us  [the longest x1 55 us: per_device(): first_full = lax.all_gather(first_pack, 'ctx', axis=0, tiled=True)]
    psum x1 -> x0, blocking collectives: 39.5 us -> none  [per_device(): total_sq = lax.psum(local_sq, ('ctx', 'tp'))]
  transfers between devices with their start and end apart: 24 -> 50, of which waited for: 17 -> 30; matrix products, arithmetic and copies ran while one was open for 10% -> 17% of each run, Pallas kernels for 0% -> 2%
where the time goes in v1:
time: 757 us; the launch traced here: 747 us
  waiting for transfers between devices  379 us (50%)
  starting transfers between devices  92.8 us (12%)
  other arithmetic  81.9 us (11%)
  matrix products  73.9 us (10%)
  local copies, waits for them, and re-layouts  56.4 us (7%)
  Pallas kernels  28.6 us (4%)
  between operations  25 us (3%)
  blocking collectives  8.86 us (1%)
    ppermute x27, waiting for transfers between devices, tp_shift(): lax.ppermute(value, 'tp', [(place, (place + steps) % count) for place in...  269 us
    ppermute x27, starting transfers between devices, tp_shift(): lax.ppermute(value, 'tp', [(place, (place + steps) % count) for place in...  74.8 us
    all_gather x1, waiting for transfers between devices, per_device(): first_full = lax.all_gather(first_pack, 'ctx', axis=0, tiled=True)  55 us
    ppermute x18, waiting for transfers between devices, ctx_xor(): lax.ppermute(value, 'ctx', [(place, place ^ mask) for place in range(coun...  54.8 us
    unnamed x171, local copies, waits for them, and re-layouts  42.3 us
    mul x5, other arithmetic, adam_update(): amount = learn_rate * (update + decay_rate * decays * master)  20.8 us
    ppermute x18, starting transfers between devices, ctx_xor(): lax.ppermute(value, 'ctx', [(place, place ^ mask) for place in range(coun...  17.8 us
    dot_general x1, matrix products, per_device(): jnp.einsum('btd,btf->bdf', pair_left, pair_right, preferred_element_type=...  15.9 us
  transfers between devices with their start and end apart: 50, of which 30 were waited for; matrix products, arithmetic and copies ran while one was open for 17% of the time, Pallas kernels for 2%

profile of v1, /device:TPU:0, one launch (start us, length us, event | category | flops | bytes accessed | tf_op | source)
XLA Modules:
  0.0 746.8 jit_solution(5774638457470307153)
XLA Ops:
  14.9 55.0 %all-gather.3.cloned.1.call-done = bf16[2048,2048]{0,1:T(8,128)(2,1)} async-done(((bf16[256,2048]{0,1:T(8,128)(2,1)}), bf16[2048,2048]{0,1:T(8,128)(2,1)}) %all-gather.3.cloned.1.call-update) | async-done | bytes 8388624 | tf_op jit(solution)/shard_map/all_gather | solution.py:327
  70.4 8.9 %all_gather.9 = bf16[4,2048]{1,0:T(4,128)(2,1)S(1)} all-gather(bf16[4,256]{1,0:T(4,128)(2,1)S(1)} %pad_maximum_fusion.25), channel_id=1, replica_groups=mesh['ctx'=8,'tp'=4] {'ctx'}, dimensions={1}, use_global_device_ids=true | all-gather | bytes 18432 | tf_op jit(solution)/shard_map/all_gather | solution.py:334
  94.2 3.5 fusion.32
  107.0 9.2 %collective-permute-done.2 = bf16[512,384]{1,0:T(8,128)(2,1)S(1)} collective-permute-done((bf16[512,384]{1,0:T(8,128)(2,1)}, bf16[512,384]{1,0:T(8,128)(2,1)S(1)}, u32[]{:S(2)}, u32[]{:S(2)}) %collective-permute-start.2) | collective-permute-done | bytes 393248 | tf_op jit(solution)/shard_map/ppermute | solution.py:32
  116.2 7.9 %collective-permute-done.1 = bf16[512,384]{1,0:T(8,128)(2,1)} collective-permute-done((bf16[512,384]{1,0:T(8,128)(2,1)}, bf16[512,384]{1,0:T(8,128)(2,1)}, u32[]{:S(2)}, u32[]{:S(2)}) %collective-permute-start.1) | collective-permute-done | bytes 393248 | tf_op jit(solution)/shard_map/ppermute | solution.py:32
  130.5 13.2 %attention_forward.1 = (bf16[2048,128]{1,0:T(8,128)(2,1)}, f32[128,2048]{1,0:T(8,128)}, f32[1,2048]{1,0:T(1,128)}) custom-call(s32[2]{0:T(128)} %pad_add_fusion.2.place, s32[2,8]{1,0:T(2,128)} %pad_add_fusion.1.tiles, s32[2,2048]{1,0:T(2,128)} %pad_add_fusion.refs_0_, bf16[2048,384]{1,0:T(8,128)(2,1)} %copy-done, bf16[2048,256]{1,0:T(8,128)(2,1)} %copy-done.9), custom_call_target="tpu_custom_call" | custom-call | tf_op jit(solution)/shard_map/attention_forward/pallas_call | solution.py:212
  145.0 2.9 collective-permute-start.5
  148.5 6.3 collective-permute-done.6
  154.8 2.9 collective-permute-done.5
  160.5 2.8 convolution_convert_fusion.3
  164.3 2.4 collective-permute-start.8
  166.7 2.2 collective-permute-start.7
  168.9 11.4 %collective-permute-done.9 = bf16[128,2048]{1,0:T(8,128)(2,1)S(1)} collective-permute-done((bf16[128,2048]{1,0:T(8,128)(2,1)S(1)}, bf16[128,2048]{1,0:T(8,128)(2,1)S(1)}, u32[]{:S(2)}, u32[]{:S(2)}) %collective-permute-start.9) | collective-permute-done | bytes 524320 | tf_op jit(solution)/shard_map/ppermute | solution.py:37
  180.3 22.0 %collective-permute-done.8 = bf16[128,2048]{1,0:T(8,128)(2,1)S(1)} collective-permute-done((bf16[128,2048]{1,0:T(8,128)(2,1)S(1)}, bf16[128,2048]{1,0:T(8,128)(2,1)S(1)}, u32[]{:S(2)}, u32[]{:S(2)}) %collective-permute-start.8) | collective-permute-done | bytes 524320 | tf_op jit(solution)/shard_map/ppermute | solution.py:37
  204.0 13.1 %collective-permute-start.12 = (bf16[128,2048]{1,0:T(8,128)(2,1)S(1)}, bf16[128,2048]{1,0:T(8,128)(2,1)S(1)}, u32[]{:S(2)}, u32[]{:S(2)}) collective-permute-start(bf16[128,2048]{1,0:T(8,128)(2,1)S(1)} %add_convert_fusion.2), channel_id=1, source_target_pairs={{0,3},{1,0},{2,1},{3,2},{4,7},{5,4},{6,5},{7,6},{8,11},{9,8},{10,9... | collective-permute-start | bytes 1572872 | tf_op jit(solution)/shard_map/ppermute | solution.py:37
  219.1 10.4 %collective-permute-done.12 = bf16[128,2048]{1,0:T(8,128)(2,1)S(1)} collective-permute-done((bf16[128,2048]{1,0:T(8,128)(2,1)S(1)}, bf16[128,2048]{1,0:T(8,128)(2,1)S(1)}, u32[]{:S(2)}, u32[]{:S(2)}) %collective-permute-start.12) | collective-permute-done | bytes 524320 | tf_op jit(solution)/shard_map/ppermute | solution.py:37
  229.4 33.5 %collective-permute-done.11 = bf16[128,2048]{1,0:T(8,128)(2,1)S(1)} collective-permute-done((bf16[128,2048]{1,0:T(8,128)(2,1)S(1)}, bf16[128,2048]{1,0:T(8,128)(2,1)S(1)}, u32[]{:S(2)}, u32[]{:S(2)}) %collective-permute-start.11) | collective-permute-done | bytes 524320 | tf_op jit(solution)/shard_map/ppermute | solution.py:37
  263.8 9.6 %multiply_convert_fusion = (bf16[512,2048]{1,0:T(8,128)(2,1)}, f32[512,2048]{1,0:T(8,128)}) fusion(bf16[2048,4096]{0,1:T(8,128)(2,1)} %all-gather.5.cloned.1.call-done, bf16[128,2048]{1,0:T(8,128)(2,1)} %copy-done.31, bf16[128,2048]{1,0:T(8,128)(2,1)} %copy-done.33, bf16[128,2048]{1,0:T(8,128)(2,1)} %collective-permute-done.10, bf16[128,2048]{1,0:T(8,128)(2,1)} %copy-done.22), kind=kOutput, calls=%fused_computation.35 | convolution fusion | flops 4308598784 | bytes 16777216 | tf_op jit(solution)/shard_map/dot_general | solution.py:398
  275.5 9.0 %fusion.23 = bf16[512,2048]{1,0:T(8,128)(2,1)} fusion(f32[512,2048]{1,0:T(8,128)} %get-tuple-element.224, bf16[2048,4096]{0,1:T(8,128)(2,1)S(1)} %copy-done.68, bf16[128,2048]{1,0:T(8,128)(2,1)S(1)} %copy-done.26, bf16[128,2048]{1,0:T(8,128)(2,1)S(1)} %copy-done.27, bf16[128,2048]{1,0:T(8,128)(2,1)S(1)} %copy-done.24, bf16[128,2048]{1,0:T(8,128)(2,1)S(1)} %copy-done.6), kind=kOutput, calls=%fused_computation.28 | convolution fusion | flops 4313841664 | bytes 16777216 | tf_op jit(solution)/shard_map/dot_general | solution.py:397
  284.5 6.4 fusion.38
  294.7 3.3 collective-permute-start.13
  298.0 12.5 %collective-permute-done.15 = bf16[128,2048]{1,0:T(8,128)(2,1)} collective-permute-done((bf16[128,2048]{1,0:T(8,128)(2,1)}, bf16[128,2048]{1,0:T(8,128)(2,1)}, u32[]{:S(2)}, u32[]{:S(2)}) %collective-permute-start.15) | collective-permute-done | bytes 524320 | tf_op jit(solution)/shard_map/ppermute | solution.py:37
  310.5 20.8 %collective-permute-done.14 = bf16[128,2048]{1,0:T(8,128)(2,1)} collective-permute-done((bf16[128,2048]{1,0:T(8,128)(2,1)}, bf16[128,2048]{1,0:T(8,128)(2,1)}, u32[]{:S(2)}, u32[]{:S(2)}) %collective-permute-start.14) | collective-permute-done | bytes 524320 | tf_op jit(solution)/shard_map/ppermute | solution.py:37
  331.3 2.9 multiply_reduce_fusion.2
  335.8 11.4 %collective-permute-start.18 = (bf16[128,2048]{1,0:T(8,128)(2,1)S(1)}, bf16[128,2048]{1,0:T(8,128)(2,1)S(1)}, u32[]{:S(2)}, u32[]{:S(2)}) collective-permute-start(bf16[128,2048]{1,0:T(8,128)(2,1)S(1)} %get-tuple-element.139), channel_id=1, source_target_pairs={{0,3},{1,0},{2,1},{3,2},{4,7},{5,4},{6,5},{7,6},{8,11},{9,8},{10,9... | collective-permute-start | bytes 1572872 | tf_op jit(solution)/shard_map/ppermute | solution.py:37
  348.0 9.1 %fusion.41 = bf16[512,2048]{1,0:T(8,128)(2,1)} fusion(bf16[512,2048]{1,0:T(8,128)(2,1)S(1)} %copy-done.71, bf16[2048,4096]{0,1:T(8,128)(2,1)} %all-gather.5.cloned.1.call-done), kind=kOutput, calls=%fused_computation.42 | convolution fusion | flops 4296015872 | bytes 12582912 | tf_op jit(solution)/shard_map/dot_general | solution.py:414
  357.1 2.5 collective-permute-done.18
  359.6 33.0 %collective-permute-done.17 = bf16[128,2048]{1,0:T(8,128)(2,1)S(1)} collective-permute-done((bf16[128,2048]{1,0:T(8,128)(2,1)S(1)}, bf16[128,2048]{1,0:T(8,128)(2,1)S(1)}, u32[]{:S(2)}, u32[]{:S(2)}) %collective-permute-start.17) | collective-permute-done | bytes 524320 | tf_op jit(solution)/shard_map/ppermute | solution.py:37
  392.8 2.9 fusion.51
  399.3 3.1 collective-permute-done.27
  404.5 15.3 %attention_backward.1 = (bf16[2048,128]{1,0:T(8,128)(2,1)}, f32[2048,256]{1,0:T(8,128)}, bf16[2048,256]{1,0:T(8,128)(2,1)}) custom-call(s32[2]{0:T(128)} %pad_add_fusion.2.place, s32[2,8]{1,0:T(2,128)} %pad_add_fusion.1.tiles, s32[2,2048]{1,0:T(2,128)} %pad_add_fusion.refs_0_, bf16[2048,384]{1,0:T(8,128)(2,1)} %copy-done, ...), custom_call_target="tpu_custom_call" | custom-call | tf_op jit(solution)/shard_map/attention_backward/pallas_call | solution.py:229
  419.9 2.6 convolution_convert_fusion.2
  429.6 9.7 %collective-permute-done.31 = bf16[512,384]{1,0:T(8,128)(2,1)} collective-permute-done((bf16[512,384]{1,0:T(8,128)(2,1)}, bf16[512,384]{1,0:T(8,128)(2,1)}, u32[]{:S(2)}, u32[]{:S(2)}) %collective-permute-start.31) | collective-permute-done | bytes 393248 | tf_op jit(solution)/shard_map/ppermute | solution.py:32
  439.3 9.3 %collective-permute-done.30 = bf16[512,384]{1,0:T(8,128)(2,1)} collective-permute-done((bf16[512,384]{1,0:T(8,128)(2,1)}, bf16[512,384]{1,0:T(8,128)(2,1)}, u32[]{:S(2)}, u32[]{:S(2)}) %collective-permute-start.30) | collective-permute-done | bytes 393248 | tf_op jit(solution)/shard_map/ppermute | solution.py:32
  452.0 5.7 convolution_convert_fusion.1
  460.5 2.5 fusion.73
  463.0 15.9 %convolution_convert_fusion = bf16[2,2048,2048]{2,1,0:T(8,128)(2,1)} fusion(bf16[1,512,2048]{2,1,0:T(8,128)(2,1)S(1)} %fusion.72, bf16[1,512,2048]{2,1,0:T(8,128)(2,1)} %fusion.73, bf16[1,512,2048]{2,1,0:T(8,128)(2,1)} %bitcast.152, bf16[1,512,2048]{2,1,0:T(8,128)(2,1)} %bitcast.153), kind=kOutput, calls=%fused_computation | convolution fusion | flops 8602517504 | bytes 25165824 | tf_op jit(solution)/shard_map/btd,btf->bdf/dot_general | solution.py:407
  480.8 2.6 collective-permute-start.20
  483.3 2.8 collective-permute-start.19
  486.2 11.3 %collective-permute-done.21 = bf16[128,2048]{1,0:T(8,128)(2,1)S(1)} collective-permute-done((bf16[128,2048]{1,0:T(8,128)(2,1)S(1)}, bf16[128,2048]{1,0:T(8,128)(2,1)S(1)}, u32[]{:S(2)}, u32[]{:S(2)}) %collective-permute-start.21) | collective-permute-done | bytes 524320 | tf_op jit(solution)/shard_map/ppermute | solution.py:37
  497.5 21.3 %collective-permute-done.20 = bf16[128,2048]{1,0:T(8,128)(2,1)S(1)} collective-permute-done((bf16[128,2048]{1,0:T(8,128)(2,1)S(1)}, bf16[128,2048]{1,0:T(8,128)(2,1)S(1)}, u32[]{:S(2)}, u32[]{:S(2)}) %collective-permute-start.20) | collective-permute-done | bytes 524320 | tf_op jit(solution)/shard_map/ppermute | solution.py:37
  518.7 2.2 add_convert_fusion.1
  521.0 11.7 %collective-permute-start.24 = (bf16[128,2048]{1,0:T(8,128)(2,1)}, bf16[128,2048]{1,0:T(8,128)(2,1)}, u32[]{:S(2)}, u32[]{:S(2)}) collective-permute-start(bf16[128,2048]{1,0:T(8,128)(2,1)} %add_convert_fusion.1), channel_id=1, source_target_pairs={{0,3},{1,0},{2,1},{3,2},{4,7},{5,4},{6,5},{7,6},{8,11},{9,8},{10,9... | collective-permute-start | bytes 1572872 | tf_op jit(solution)/shard_map/ppermute | solution.py:37
  533.5 6.4 fusion.35
  542.4 2.8 collective-permute-start.34
  546.8 2.9 collective-permute-start.32
  563.8 2.9 copy.73
  566.7 36.0 %collective-permute-done.23 = bf16[128,2048]{1,0:T(8,128)(2,1)} collective-permute-done((bf16[128,2048]{1,0:T(8,128)(2,1)}, bf16[128,2048]{1,0:T(8,128)(2,1)}, u32[]{:S(2)}, u32[]{:S(2)}) %collective-permute-start.23) | collective-permute-done | bytes 524320 | tf_op jit(solution)/shard_map/ppermute | solution.py:37
  604.7 9.1 %collective-permute-done.33 = bf16[128,2048]{1,0:T(8,128)(2,1)} collective-permute-done((bf16[128,2048]{1,0:T(8,128)(2,1)}, bf16[128,2048]{1,0:T(8,128)(2,1)}, u32[]{:S(2)}, u32[]{:S(2)}) %collective-permute-start.33) | collective-permute-done | bytes 524320 | tf_op jit(solution)/shard_map/ppermute | solution.py:37
  613.9 3.8 collective-permute-done.32
  617.7 2.2 fusion.64
  620.6 7.4 collective-permute-start.37
  630.5 9.8 %collective-permute-done.37 = bf16[128,2048]{1,0:T(8,128)(2,1)S(1)} collective-permute-done((bf16[128,2048]{1,0:T(8,128)(2,1)S(1)}, bf16[128,2048]{1,0:T(8,128)(2,1)S(1)}, u32[]{:S(2)}, u32[]{:S(2)}) %collective-permute-start.37) | collective-permute-done | bytes 524320 | tf_op jit(solution)/shard_map/ppermute | solution.py:37
  640.4 31.9 %collective-permute-done.36 = bf16[128,2048]{1,0:T(8,128)(2,1)} collective-permute-done((bf16[128,2048]{1,0:T(8,128)(2,1)S(1)}, bf16[128,2048]{1,0:T(8,128)(2,1)}, u32[]{:S(2)}, u32[]{:S(2)}) %collective-permute-start.36) | collective-permute-done | bytes 524320 | tf_op jit(solution)/shard_map/ppermute | solution.py:37
  680.7 4.0 multiply_reduce_fusion
  688.7 2.3 collective-permute-start.39
  694.6 2.9 collective-permute-start.44
  700.4 2.9 copy.76
  705.8 2.6 add_multiply_fusion.4
  710.5 6.6 add_multiply_fusion.1
  717.1 2.9 copy.78
  721.0 3.0 copy.80
  726.9 7.6 %add_multiply_fusion.2 = (f32[256,2048]{1,0:T(8,128)}, f32[256,2048]{1,0:T(8,128)}, f32[256,2048]{1,0:T(8,128)}) fusion(f32[256,2048]{1,0:T(8,128)} %param.26, f32[]{:T(128)} %bitcast.53, f32[256,2048]{1,0:T(8,128)} %get-tuple-element.135, f32[]{:T(128)S(6)} %div.187, f32[256,2048]{1,0:T(8,128)} %param.32, f32[256,2048]{1,0:T(8,128)} %param.38), kind=kLoop, calls=%fused_computation.65 | loop fusion | flops 7864320 | bytes 14680072 | tf_op jit(solution)/shard_map/mul | solution.py:274
  734.6 3.3 add_multiply_fusion.3
  (353 shorter events, 121.3 us)
Async XLA Ops:
  7.2 62.7 %all-gather.3.cloned.1.call-start = ((), (), s32[]{:S(2)}) async-start(), calls=%async_computation.3 | async-start | bytes 9437184 | tf_op jit(solution)/shard_map/all_gather | solution.py:327
  11.1 252.6 %all-gather.5.cloned.1.call-start = ((), (), s32[]{:S(2)}) async-start(), calls=%async_computation.4 | async-start | bytes 18874368 | tf_op jit(solution)/shard_map/all_gather | solution.py:329
  14.9 55.2 %copy-start.70 = (s32[4]{0:T(128)S(1)}, s32[4]{0:T(128)}, u32[]{:S(2)}) copy-start(s32[4]{0:T(128)} %param.42) | copy-start | bytes 52
  14.9 55.4 %copy-start.46 = (f32[2,256]{1,0:T(2,128)S(1)}, f32[2,256]{1,0:T(2,128)}, u32[]{:S(2)}) copy-start(f32[2,256]{1,0:T(2,128)} %param.29) | copy-start | bytes 6148
  14.9 55.4 %copy-start.48 = (f32[2,256]{1,0:T(2,128)S(1)}, f32[2,256]{1,0:T(2,128)}, u32[]{:S(2)}) copy-start(f32[2,256]{1,0:T(2,128)} %param.28) | copy-start | bytes 6148
  70.0 605.6 %reduce-scatter.6.cloned.1.call-start = ((), (), s32[]{:S(2)}) async-start(), calls=%async_computation.6 | async-start | bytes 2359296 | tf_op jit(solution)/shard_map/reduce_scatter | solution.py:421
  98.8 17.3 %collective-permute-start.2 = (bf16[512,384]{1,0:T(8,128)(2,1)}, bf16[512,384]{1,0:T(8,128)(2,1)S(1)}, u32[]{:S(2)}, u32[]{:S(2)}) collective-permute-start(bf16[512,384]{1,0:T(8,128)(2,1)} %pad_maximum_fusion.19), channel_id=1, source_target_pairs={{0,24},{4,28},{8,16},{12,20},{16,8},{20,12},{24,0},{28,4},{1,25},{... | collective-permute-start | bytes 1179656 | tf_op jit(solution)/shard_map/ppermute | solution.py:32
  101.2 22.9 %collective-permute-start.1 = (bf16[512,384]{1,0:T(8,128)(2,1)}, bf16[512,384]{1,0:T(8,128)(2,1)}, u32[]{:S(2)}, u32[]{:S(2)}) collective-permute-start(bf16[512,384]{1,0:T(8,128)(2,1)} %pad_maximum_fusion.18), channel_id=1, source_target_pairs={{0,16},{4,20},{8,24},{12,28},{16,0},{20,4},{24,8},{28,12},{1,17},{... | collective-permute-start | bytes 1179656 | tf_op jit(solution)/shard_map/ppermute | solution.py:32
  102.6 21.5 %collective-permute-start = (bf16[512,384]{1,0:T(8,128)(2,1)}, bf16[512,384]{1,0:T(8,128)(2,1)S(1)}, u32[]{:S(2)}, u32[]{:S(2)}) collective-permute-start(bf16[512,384]{1,0:T(8,128)(2,1)} %pad_maximum_fusion.17), channel_id=1, source_target_pairs={{0,8},{4,12},{8,0},{12,4},{16,24},{20,28},{24,16},{28,20},{1,9},{5... | collective-permute-start | bytes 1179656 | tf_op jit(solution)/shard_map/ppermute | solution.py:32
  125.3 4.2 collective-permute-start.3
  144.9 9.9 %collective-permute-start.6 = (bf16[512,128]{1,0:T(8,128)(2,1)S(1)}, bf16[512,128]{1,0:T(8,128)(2,1)S(1)}, u32[]{:S(2)}, u32[]{:S(2)}) collective-permute-start(bf16[512,128]{1,0:T(8,128)(2,1)S(1)} %get-tuple-element.204), channel_id=1, source_target_pairs={{0,24},{4,28},{8,16},{12,20},{16,8},{20,12},{24,0},{28,4},{1,25},{... | collective-permute-start | bytes 393224 | tf_op jit(solution)/shard_map/ppermute | solution.py:32
  145.0 12.6 %collective-permute-start.5 = (bf16[512,128]{1,0:T(8,128)(2,1)S(1)}, bf16[512,128]{1,0:T(8,128)(2,1)S(1)}, u32[]{:S(2)}, u32[]{:S(2)}) collective-permute-start(bf16[512,128]{1,0:T(8,128)(2,1)S(1)} %get-tuple-element.205), channel_id=1, source_target_pairs={{0,16},{4,20},{8,24},{12,28},{16,0},{20,4},{24,8},{28,12},{1,17},{... | collective-permute-start | bytes 393224 | tf_op jit(solution)/shard_map/ppermute | solution.py:32
  147.9 11.9 %collective-permute-start.4 = (bf16[512,128]{1,0:T(8,128)(2,1)S(1)}, bf16[512,128]{1,0:T(8,128)(2,1)S(1)}, u32[]{:S(2)}, u32[]{:S(2)}) collective-permute-start(bf16[512,128]{1,0:T(8,128)(2,1)S(1)} %get-tuple-element.206), channel_id=1, source_target_pairs={{0,8},{4,12},{8,0},{12,4},{16,24},{20,28},{24,16},{28,20},{1,9},{5... | collective-permute-start | bytes 393224 | tf_op jit(solution)/shard_map/ppermute | solution.py:32
  163.5 16.8 %collective-permute-start.9 = (bf16[128,2048]{1,0:T(8,128)(2,1)S(1)}, bf16[128,2048]{1,0:T(8,128)(2,1)S(1)}, u32[]{:S(2)}, u32[]{:S(2)}) collective-permute-start(bf16[128,2048]{1,0:T(8,128)(2,1)S(1)} %get-tuple-element.167), channel_id=1, source_target_pairs={{0,1},{1,2},{2,3},{3,0},{4,5},{5,6},{6,7},{7,4},{8,9},{9,10},{10,1... | collective-permute-start | bytes 1572872 | tf_op jit(solution)/shard_map/ppermute | solution.py:37
  164.3 38.0 %collective-permute-start.8 = (bf16[128,2048]{1,0:T(8,128)(2,1)S(1)}, bf16[128,2048]{1,0:T(8,128)(2,1)S(1)}, u32[]{:S(2)}, u32[]{:S(2)}) collective-permute-start(bf16[128,2048]{1,0:T(8,128)(2,1)S(1)} %get-tuple-element.168), channel_id=1, source_target_pairs={{0,2},{1,3},{2,0},{3,1},{4,6},{5,7},{6,4},{7,5},{8,10},{9,11},{10,... | collective-permute-start | bytes 1572872 | tf_op jit(solution)/shard_map/ppermute | solution.py:37
  166.7 35.6 %collective-permute-start.7 = (bf16[128,2048]{1,0:T(8,128)(2,1)S(1)}, bf16[128,2048]{1,0:T(8,128)(2,1)S(1)}, u32[]{:S(2)}, u32[]{:S(2)}) collective-permute-start(bf16[128,2048]{1,0:T(8,128)(2,1)S(1)} %get-tuple-element.166), channel_id=1, source_target_pairs={{0,3},{1,0},{2,1},{3,2},{4,7},{5,4},{6,5},{7,6},{8,11},{9,8},{10,9... | collective-permute-start | bytes 1572872 | tf_op jit(solution)/shard_map/ppermute | solution.py:37
  168.9 34.8 %copy-start.56 = (f32[128]{0:T(128)}, f32[128]{0:T(128)S(1)}, u32[]{:S(2)}) copy-start(f32[128]{0:T(128)S(1)} %broadcast_multiply_fusion.2) | copy-start | bytes 1540
  168.9 34.8 %copy-start.41 = (f32[1,2048]{1,0:T(1,128)S(1)}, f32[1,2048]{1,0:T(1,128)}, u32[]{:S(2)}) copy-start(f32[1,2048]{1,0:T(1,128)} %get-tuple-element.214) | copy-start | bytes 24580
  204.0 15.1 %copy-start.22 = (bf16[128,2048]{1,0:T(8,128)(2,1)}, bf16[128,2048]{1,0:T(8,128)(2,1)S(1)}, u32[]{:S(2)}) copy-start(bf16[128,2048]{1,0:T(8,128)(2,1)S(1)} %add_convert_fusion.2) | copy-start | bytes 1572868
  204.0 25.4 %collective-permute-start.12 = (bf16[128,2048]{1,0:T(8,128)(2,1)S(1)}, bf16[128,2048]{1,0:T(8,128)(2,1)S(1)}, u32[]{:S(2)}, u32[]{:S(2)}) collective-permute-start(bf16[128,2048]{1,0:T(8,128)(2,1)S(1)} %add_convert_fusion.2), channel_id=1, source_target_pairs={{0,3},{1,0},{2,1},{3,2},{4,7},{5,4},{6,5},{7,6},{8,11},{9,8},{10,9... | collective-permute-start | bytes 1572872 | tf_op jit(solution)/shard_map/ppermute | solution.py:37
  217.1 45.9 %collective-permute-start.11 = (bf16[128,2048]{1,0:T(8,128)(2,1)S(1)}, bf16[128,2048]{1,0:T(8,128)(2,1)S(1)}, u32[]{:S(2)}, u32[]{:S(2)}) collective-permute-start(bf16[128,2048]{1,0:T(8,128)(2,1)S(1)} %add_convert_fusion.2), channel_id=1, source_target_pairs={{0,2},{1,3},{2,0},{3,1},{4,6},{5,7},{6,4},{7,5},{8,10},{9,11},{10,... | collective-permute-start | bytes 1572872 | tf_op jit(solution)/shard_map/ppermute | solution.py:37
  217.3 46.4 %collective-permute-start.10 = (bf16[128,2048]{1,0:T(8,128)(2,1)S(1)}, bf16[128,2048]{1,0:T(8,128)(2,1)}, u32[]{:S(2)}, u32[]{:S(2)}) collective-permute-start(bf16[128,2048]{1,0:T(8,128)(2,1)S(1)} %add_convert_fusion.2), channel_id=1, source_target_pairs={{0,1},{1,2},{2,3},{3,0},{4,5},{5,6},{6,7},{7,4},{8,9},{9,10},{10,1... | collective-permute-start | bytes 1572872 | tf_op jit(solution)/shard_map/ppermute | solution.py:37
  229.4 33.5 %copy-start.31 = (bf16[128,2048]{1,0:T(8,128)(2,1)}, bf16[128,2048]{1,0:T(8,128)(2,1)S(1)}, u32[]{:S(2)}) copy-start(bf16[128,2048]{1,0:T(8,128)(2,1)S(1)} %collective-permute-done.12) | copy-start | bytes 1572868
  293.4 17.1 %collective-permute-start.15 = (bf16[128,2048]{1,0:T(8,128)(2,1)}, bf16[128,2048]{1,0:T(8,128)(2,1)}, u32[]{:S(2)}, u32[]{:S(2)}) collective-permute-start(bf16[128,2048]{1,0:T(8,128)(2,1)} %get-tuple-element.160), channel_id=1, source_target_pairs={{0,1},{1,2},{2,3},{3,0},{4,5},{5,6},{6,7},{7,4},{8,9},{9,10},{10,1... | collective-permute-start | bytes 1572872 | tf_op jit(solution)/shard_map/ppermute | solution.py:37
  293.4 37.9 %collective-permute-start.14 = (bf16[128,2048]{1,0:T(8,128)(2,1)}, bf16[128,2048]{1,0:T(8,128)(2,1)}, u32[]{:S(2)}, u32[]{:S(2)}) collective-permute-start(bf16[128,2048]{1,0:T(8,128)(2,1)} %get-tuple-element.161), channel_id=1, source_target_pairs={{0,2},{1,3},{2,0},{3,1},{4,6},{5,7},{6,4},{7,5},{8,10},{9,11},{10,... | collective-permute-start | bytes 1572872 | tf_op jit(solution)/shard_map/ppermute | solution.py:37
  294.7 36.7 %collective-permute-start.13 = (bf16[128,2048]{1,0:T(8,128)(2,1)}, bf16[128,2048]{1,0:T(8,128)(2,1)}, u32[]{:S(2)}, u32[]{:S(2)}) collective-permute-start(bf16[128,2048]{1,0:T(8,128)(2,1)} %get-tuple-element.159), channel_id=1, source_target_pairs={{0,3},{1,0},{2,1},{3,2},{4,7},{5,4},{6,5},{7,6},{8,11},{9,8},{10,9... | collective-permute-start | bytes 1572872 | tf_op jit(solution)/shard_map/ppermute | solution.py:37
  298.0 36.2 %copy-start.7 = (bf16[128,2048]{1,0:T(8,128)(2,1)S(1)}, bf16[128,2048]{1,0:T(8,128)(2,1)}, u32[]{:S(2)}) copy-start(bf16[128,2048]{1,0:T(8,128)(2,1)} %get-tuple-element.162) | copy-start | bytes 1572868
  298.0 36.2 %copy-start.55 = (f32[128]{0:T(128)S(1)}, f32[128]{0:T(128)}, u32[]{:S(2)}) copy-start(f32[128]{0:T(128)} %copy-done.54) | copy-start | bytes 1540
  298.0 36.2 %copy-start.59 = (f32[128]{0:T(128)S(1)}, f32[128]{0:T(128)}, u32[]{:S(2)}) copy-start(f32[128]{0:T(128)} %copy-done.58) | copy-start | bytes 1540
  335.8 23.8 %collective-permute-start.18 = (bf16[128,2048]{1,0:T(8,128)(2,1)S(1)}, bf16[128,2048]{1,0:T(8,128)(2,1)S(1)}, u32[]{:S(2)}, u32[]{:S(2)}) collective-permute-start(bf16[128,2048]{1,0:T(8,128)(2,1)S(1)} %get-tuple-element.139), channel_id=1, source_target_pairs={{0,3},{1,0},{2,1},{3,2},{4,7},{5,4},{6,5},{7,6},{8,11},{9,8},{10,9... | collective-permute-start | bytes 1572872 | tf_op jit(solution)/shard_map/ppermute | solution.py:37
  347.1 45.4 %collective-permute-start.17 = (bf16[128,2048]{1,0:T(8,128)(2,1)S(1)}, bf16[128,2048]{1,0:T(8,128)(2,1)S(1)}, u32[]{:S(2)}, u32[]{:S(2)}) collective-permute-start(bf16[128,2048]{1,0:T(8,128)(2,1)S(1)} %get-tuple-element.139), channel_id=1, source_target_pairs={{0,2},{1,3},{2,0},{3,1},{4,6},{5,7},{6,4},{7,5},{8,10},{9,11},{10,... | collective-permute-start | bytes 1572872 | tf_op jit(solution)/shard_map/ppermute | solution.py:37
  348.0 44.6 %collective-permute-start.16 = (bf16[128,2048]{1,0:T(8,128)(2,1)S(1)}, bf16[128,2048]{1,0:T(8,128)(2,1)S(1)}, u32[]{:S(2)}, u32[]{:S(2)}) collective-permute-start(bf16[128,2048]{1,0:T(8,128)(2,1)S(1)} %get-tuple-element.139), channel_id=1, source_target_pairs={{0,1},{1,2},{2,3},{3,0},{4,5},{5,6},{6,7},{7,4},{8,9},{9,10},{10,1... | collective-permute-start | bytes 1572872 | tf_op jit(solution)/shard_map/ppermute | solution.py:37
  395.8 6.7 collective-permute-start.27
  397.9 5.8 collective-permute-start.26
  397.9 5.8 collective-permute-start.25
  404.5 15.3 %copy-start.36 = (bf16[512,128]{1,0:T(8,128)(2,1)S(1)}, bf16[512,128]{1,0:T(8,128)(2,1)}, u32[]{:S(2)}) copy-start(bf16[512,128]{1,0:T(8,128)(2,1)} %copy-done.35) | copy-start | bytes 393220
  419.8 3.0 collective-permute-start.28
  422.5 254.7 %reduce-scatter.4.cloned.1.call-start = ((), (), s32[]{:S(2)}) async-start(), calls=%async_computation.5 | async-start | bytes 7077888 | tf_op jit(solution)/shard_map/reduce_scatter | solution.py:447
  426.1 13.2 %collective-permute-start.31 = (bf16[512,384]{1,0:T(8,128)(2,1)}, bf16[512,384]{1,0:T(8,128)(2,1)}, u32[]{:S(2)}, u32[]{:S(2)}) collective-permute-start(bf16[512,384]{1,0:T(8,128)(2,1)} %get-tuple-element.177), channel_id=1, source_target_pairs={{0,24},{4,28},{8,16},{12,20},{16,8},{20,12},{24,0},{28,4},{1,25},{... | collective-permute-start | bytes 1179656 | tf_op jit(solution)/shard_map/ppermute | solution.py:32
  427.6 21.0 %collective-permute-start.30 = (bf16[512,384]{1,0:T(8,128)(2,1)}, bf16[512,384]{1,0:T(8,128)(2,1)}, u32[]{:S(2)}, u32[]{:S(2)}) collective-permute-start(bf16[512,384]{1,0:T(8,128)(2,1)} %get-tuple-element.178), channel_id=1, source_target_pairs={{0,16},{4,20},{8,24},{12,28},{16,0},{20,4},{24,8},{28,12},{1,17},{... | collective-permute-start | bytes 1179656 | tf_op jit(solution)/shard_map/ppermute | solution.py:32
  428.2 20.6 %collective-permute-start.29 = (bf16[512,384]{1,0:T(8,128)(2,1)}, bf16[512,384]{1,0:T(8,128)(2,1)}, u32[]{:S(2)}, u32[]{:S(2)}) collective-permute-start(bf16[512,384]{1,0:T(8,128)(2,1)} %get-tuple-element.176), channel_id=1, source_target_pairs={{0,8},{4,12},{8,0},{12,4},{16,24},{20,28},{24,16},{28,20},{1,9},{5... | collective-permute-start | bytes 1179656 | tf_op jit(solution)/shard_map/ppermute | solution.py:32
  457.7 223.0 %reduce-scatter.8.cloned.1.call-start = ((), (), s32[]{:S(2)}) async-start(), calls=%async_computation.7 | async-start | bytes 18874368 | tf_op jit(solution)/shard_map/reduce_scatter | solution.py:408
  480.7 52.8 %copy-start.45 = (bf16[512,1536]{1,0:T(8,128)(2,1)S(1)}, bf16[512,1536]{1,0:T(8,128)(2,1)}, u32[]{:S(2)}) copy-start(bf16[512,1536]{1,0:T(8,128)(2,1)} %copy-done.44) | copy-start | bytes 4718596
  480.7 16.8 %collective-permute-start.21 = (bf16[128,2048]{1,0:T(8,128)(2,1)S(1)}, bf16[128,2048]{1,0:T(8,128)(2,1)S(1)}, u32[]{:S(2)}, u32[]{:S(2)}) collective-permute-start(bf16[128,2048]{1,0:T(8,128)(2,1)S(1)} %get-tuple-element.157), channel_id=1, source_target_pairs={{0,1},{1,2},{2,3},{3,0},{4,5},{5,6},{6,7},{7,4},{8,9},{9,10},{10,1... | collective-permute-start | bytes 1572872 | tf_op jit(solution)/shard_map/ppermute | solution.py:37
  480.8 38.0 %collective-permute-start.20 = (bf16[128,2048]{1,0:T(8,128)(2,1)S(1)}, bf16[128,2048]{1,0:T(8,128)(2,1)S(1)}, u32[]{:S(2)}, u32[]{:S(2)}) collective-permute-start(bf16[128,2048]{1,0:T(8,128)(2,1)S(1)} %get-tuple-element.158), channel_id=1, source_target_pairs={{0,2},{1,3},{2,0},{3,1},{4,6},{5,7},{6,4},{7,5},{8,10},{9,11},{10,... | collective-permute-start | bytes 1572872 | tf_op jit(solution)/shard_map/ppermute | solution.py:37
  483.3 35.4 %collective-permute-start.19 = (bf16[128,2048]{1,0:T(8,128)(2,1)S(1)}, bf16[128,2048]{1,0:T(8,128)(2,1)S(1)}, u32[]{:S(2)}, u32[]{:S(2)}) collective-permute-start(bf16[128,2048]{1,0:T(8,128)(2,1)S(1)} %get-tuple-element.156), channel_id=1, source_target_pairs={{0,3},{1,0},{2,1},{3,2},{4,7},{5,4},{6,5},{7,6},{8,11},{9,8},{10,9... | collective-permute-start | bytes 1572872 | tf_op jit(solution)/shard_map/ppermute | solution.py:37
  521.0 25.8 %collective-permute-start.24 = (bf16[128,2048]{1,0:T(8,128)(2,1)}, bf16[128,2048]{1,0:T(8,128)(2,1)}, u32[]{:S(2)}, u32[]{:S(2)}) collective-permute-start(bf16[128,2048]{1,0:T(8,128)(2,1)} %add_convert_fusion.1), channel_id=1, source_target_pairs={{0,3},{1,0},{2,1},{3,2},{4,7},{5,4},{6,5},{7,6},{8,11},{9,8},{10,9... | collective-permute-start | bytes 1572872 | tf_op jit(solution)/shard_map/ppermute | solution.py:37
  532.6 70.1 %collective-permute-start.23 = (bf16[128,2048]{1,0:T(8,128)(2,1)}, bf16[128,2048]{1,0:T(8,128)(2,1)}, u32[]{:S(2)}, u32[]{:S(2)}) collective-permute-start(bf16[128,2048]{1,0:T(8,128)(2,1)} %add_convert_fusion.1), channel_id=1, source_target_pairs={{0,2},{1,3},{2,0},{3,1},{4,6},{5,7},{6,4},{7,5},{8,10},{9,11},{10,... | collective-permute-start | bytes 1572872 | tf_op jit(solution)/shard_map/ppermute | solution.py:37
  533.3 69.4 %collective-permute-start.22 = (bf16[128,2048]{1,0:T(8,128)(2,1)}, bf16[128,2048]{1,0:T(8,128)(2,1)}, u32[]{:S(2)}, u32[]{:S(2)}) collective-permute-start(bf16[128,2048]{1,0:T(8,128)(2,1)} %add_convert_fusion.1), channel_id=1, source_target_pairs={{0,1},{1,2},{2,3},{3,0},{4,5},{5,6},{6,7},{7,4},{8,9},{9,10},{10,1... | collective-permute-start | bytes 1572872 | tf_op jit(solution)/shard_map/ppermute | solution.py:37
  542.4 62.3 %collective-permute-start.34 = (bf16[128,2048]{1,0:T(8,128)(2,1)}, bf16[128,2048]{1,0:T(8,128)(2,1)}, u32[]{:S(2)}, u32[]{:S(2)}) collective-permute-start(bf16[128,2048]{1,0:T(8,128)(2,1)} %get-tuple-element.150), channel_id=1, source_target_pairs={{0,1},{1,2},{2,3},{3,0},{4,5},{5,6},{6,7},{7,4},{8,9},{9,10},{10,1... | collective-permute-start | bytes 1572872 | tf_op jit(solution)/shard_map/ppermute | solution.py:37
  545.2 68.7 %collective-permute-start.33 = (bf16[128,2048]{1,0:T(8,128)(2,1)}, bf16[128,2048]{1,0:T(8,128)(2,1)}, u32[]{:S(2)}, u32[]{:S(2)}) collective-permute-start(bf16[128,2048]{1,0:T(8,128)(2,1)} %get-tuple-element.151), channel_id=1, source_target_pairs={{0,2},{1,3},{2,0},{3,1},{4,6},{5,7},{6,4},{7,5},{8,10},{9,11},{10,... | collective-permute-start | bytes 1572872 | tf_op jit(solution)/shard_map/ppermute | solution.py:37
  546.8 70.9 %collective-permute-start.32 = (bf16[128,2048]{1,0:T(8,128)(2,1)}, bf16[128,2048]{1,0:T(8,128)(2,1)}, u32[]{:S(2)}, u32[]{:S(2)}) collective-permute-start(bf16[128,2048]{1,0:T(8,128)(2,1)} %get-tuple-element.149), channel_id=1, source_target_pairs={{0,3},{1,0},{2,1},{3,2},{4,7},{5,4},{6,5},{7,6},{8,11},{9,8},{10,9... | collective-permute-start | bytes 1572872 | tf_op jit(solution)/shard_map/ppermute | solution.py:37
  566.7 51.0 %copy-start.57 = (f32[128]{0:T(128)S(1)}, f32[128]{0:T(128)}, u32[]{:S(2)}) copy-start(f32[128]{0:T(128)} %copy-done.56) | copy-start | bytes 1540
  604.7 15.2 %copy-start.10 = (f32[128,2048]{1,0:T(8,128)S(1)}, f32[128,2048]{1,0:T(8,128)}, u32[]{:S(2)}) copy-start(f32[128,2048]{1,0:T(8,128)} %get-tuple-element.140) | copy-start | bytes 3145732
  620.6 19.8 %collective-permute-start.37 = (bf16[128,2048]{1,0:T(8,128)(2,1)S(1)}, bf16[128,2048]{1,0:T(8,128)(2,1)S(1)}, u32[]{:S(2)}, u32[]{:S(2)}) collective-permute-start(bf16[128,2048]{1,0:T(8,128)(2,1)S(1)} %fusion.63), channel_id=1, source_target_pairs={{0,3},{1,0},{2,1},{3,2},{4,7},{5,4},{6,5},{7,6},{8,11},{9,8},{10,9... | collective-permute-start | bytes 1572872 | tf_op jit(solution)/shard_map/ppermute | solution.py:37
  628.0 44.3 %collective-permute-start.36 = (bf16[128,2048]{1,0:T(8,128)(2,1)S(1)}, bf16[128,2048]{1,0:T(8,128)(2,1)}, u32[]{:S(2)}, u32[]{:S(2)}) collective-permute-start(bf16[128,2048]{1,0:T(8,128)(2,1)S(1)} %fusion.63), channel_id=1, source_target_pairs={{0,2},{1,3},{2,0},{3,1},{4,6},{5,7},{6,4},{7,5},{8,10},{9,11},{10,... | collective-permute-start | bytes 1572872 | tf_op jit(solution)/shard_map/ppermute | solution.py:37
  628.8 43.5 %collective-permute-start.35 = (bf16[128,2048]{1,0:T(8,128)(2,1)S(1)}, bf16[128,2048]{1,0:T(8,128)(2,1)}, u32[]{:S(2)}, u32[]{:S(2)}) collective-permute-start(bf16[128,2048]{1,0:T(8,128)(2,1)S(1)} %fusion.63), channel_id=1, source_target_pairs={{0,1},{1,2},{2,3},{3,0},{4,5},{5,6},{6,7},{7,4},{8,9},{9,10},{10,1... | collective-permute-start | bytes 1572872 | tf_op jit(solution)/shard_map/ppermute | solution.py:37
  686.1 1.3 collective-permute-start.38
  687.4 4.7 collective-permute-start.40
  688.0 5.2 collective-permute-start.41
  688.7 4.7 collective-permute-start.39
  693.3 9.9 %collective-permute-start.43 = (f32[72,128]{1,0:T(8,128)S(1)}, f32[72,128]{1,0:T(8,128)S(1)}, u32[]{:S(2)}, u32[]{:S(2)}) collective-permute-start(f32[72,128]{1,0:T(8,128)S(1)} %add_add_fusion.1), channel_id=1, source_target_pairs={{0,1},{1,2},{2,3},{3,0},{4,5},{5,6},{6,7},{7,4},{8,9},{9,10},{10,1... | collective-permute-start | bytes 110600 | tf_op jit(solution)/shard_map/ppermute | solution.py:37
  694.6 8.7 %collective-permute-start.44 = (f32[72,128]{1,0:T(8,128)S(1)}, f32[72,128]{1,0:T(8,128)S(1)}, u32[]{:S(2)}, u32[]{:S(2)}) collective-permute-start(f32[72,128]{1,0:T(8,128)S(1)} %add_add_fusion.1), channel_id=1, source_target_pairs={{0,3},{1,0},{2,1},{3,2},{4,7},{5,4},{6,5},{7,6},{8,11},{9,8},{10,9... | collective-permute-start | bytes 110600 | tf_op jit(solution)/shard_map/ppermute | solution.py:37
  697.5 5.8 collective-permute-start.42
  (58 other events, 299.7 us)
Sparse Core Ops, SparseCore 0:
  11.3 58.6 all-gather.2
  72.4 111.6 all-gather.4
  422.6 41.2 reduce-scatter.5
  467.6 61.7 reduce-scatter.3
  532.7 115.9 reduce-scatter.7

commit v2 on v1

--- a/solution.py
+++ b/solution.py
@@ -32,43 +32,59 @@
     return lax.ppermute(value, "ctx", [(place, place ^ mask) for place in range(count)])
 
 
-def tp_shift(value, steps):
+def ctx_gather(own, early):
+    blocks = [None] * lax.axis_size("ctx")
+    for mask in range(0, len(blocks), 2):
+        blocks[mask] = own if mask == 0 else ctx_xor(own, mask)
+    blocks[2], early = lax.optimization_barrier((blocks[2], early))
+    for mask in range(0, len(blocks), 2):
+        blocks[mask + 1] = ctx_xor(blocks[mask], 1)
+    return (blocks, early)
+
+
+def tp_xor(value, mask):
     count = lax.axis_size("tp")
-    return lax.ppermute(value, "tp", [(place, (place + steps) % count) for place in range(count)])
+    return lax.ppermute(value, "tp", [(place, place ^ mask) for place in range(count)])
 
 
 def tp_gather(own):
-    return [own] + [tp_shift(own, s) for s in range(1, lax.axis_size("tp"))]
-
-
-def tp_scatter(partial):
+    far_first = [tp_xor(own, s) for s in reversed(range(1, lax.axis_size("tp")))]
+    return [own] + far_first[::-1]
+
+
+def tp_send(partial):
     count = lax.axis_size("tp")
     rows = partial.shape[0] // count
     pieces = [partial[s * rows : (s + 1) * rows] for s in range(count)]
-    got = [tp_shift(pieces[s], -s) for s in range(1, count)]
-    total = pieces[0].astype(f32)
-    for piece in got:
+    far_first = [tp_xor(pieces[s], s) for s in reversed(range(1, count))]
+    return [pieces[0]] + far_first[::-1]
+
+
+def tp_total(parts):
+    total = parts[0].astype(f32)
+    for piece in parts[1:]:
         total = total + piece.astype(f32)
     return total
 
 
+def tp_scatter(partial):
+    return tp_total(tp_send(partial))
+
+
 def slots_to_rows(parts, tp_place):
-    count = len(parts)
-    rows = parts[0].shape[0]
-    stacked = jnp.concatenate(parts, axis=0)
-    order = [lax.rem(tp_place - j + count, count) * rows for j in range(count)]
-    return jnp.concatenate([lax.dynamic_slice_in_dim(stacked, o, rows, 0) for o in order], axis=0)
-
-
-def rows_to_slots(value, tp_place, count):
+    return in_slots(jnp.concatenate(parts, axis=0), tp_place, len(parts))
+
+
+def in_slots(value, tp_place, count):
     rows = value.shape[0] // count
-    order = [lax.rem(tp_place - s + count, count) * rows for s in range(count)]
+    order = [jnp.bitwise_xor(tp_place, s) * rows for s in range(count)]
     return jnp.concatenate([lax.dynamic_slice_in_dim(value, o, rows, 0) for o in order], axis=0)
 
 
 def sum_over_all(value):
     ctx_bits = lax.axis_size("ctx").bit_length() - 1
-    value = value + ctx_xor(value, 1)
+    one, two, three = (tp_xor(value, 1), tp_xor(value, 2), tp_xor(value, 3))
+    value = (value + one) + (two + three)
     bit = 1
     while bit < ctx_bits:
         if bit + 1 < ctx_bits:
@@ -79,14 +95,12 @@
         else:
             value = value + ctx_xor(value, 1 << bit)
             bit += 1
-    one, two, three = (tp_shift(value, 1), tp_shift(value, 2), tp_shift(value, 3))
-    return (value + two) + (one + three)
+    return value + ctx_xor(value, 1)
 
 
 def place_of(me, tp_place, mask, chunk, rows, chunks):
     part = rows // chunks
-    inner = lax.rem(tp_place - chunk + chunks, chunks)
-    return pl.multiple_of(jnp.bitwise_xor(me, mask) * rows + inner * part, part)
+    return pl.multiple_of(jnp.bitwise_xor(me, mask) * rows + jnp.bitwise_xor(tp_place, chunk) * part, part)
 
 
 def scores_of(keys, query, lo, hi, base, scale):
@@ -112,12 +126,13 @@
                 k_all[pl.ds(at, part), :] = source[top : top + part, left : left + HEAD]
                 vt_all[:, pl.ds(at, part)] = source[top : top + part, left + HEAD : left + 2 * HEAD].T
 
-    for tile in range(own.shape[0] // Q_TILE):
-        cut = slice(tile * Q_TILE, (tile + 1) * Q_TILE)
+    @pl.loop(0, own.shape[0] // Q_TILE)
+    def _(tile):
+        cut = pl.ds(pl.multiple_of(tile * Q_TILE, Q_TILE), Q_TILE)
         query = own[cut, :HEAD]
         lo, hi = span[0:1, cut], span[1:2, cut]
 
-        def step(index, carry, query=query, lo=lo, hi=hi):
+        def step(index, carry):
             top, total, acc = carry
             base = pl.multiple_of(index * K_TILE, K_TILE)
             scores = scores_of(k_all[pl.ds(base, K_TILE), :], query, lo, hi, base, scale)
@@ -165,13 +180,14 @@
     dk_all[...] = jnp.zeros_like(dk_all)
     dv_all[...] = jnp.zeros_like(dv_all)
 
-    for tile in range(own.shape[0] // Q_TILE):
-        cut = slice(tile * Q_TILE, (tile + 1) * Q_TILE)
+    @pl.loop(0, own.shape[0] // Q_TILE)
+    def _(tile):
+        cut = pl.ds(pl.multiple_of(tile * Q_TILE, Q_TILE), Q_TILE)
         query, grad = own[cut, :HEAD], grad_out[cut, :]
         lo, hi, lse = span[0:1, cut], span[1:2, cut], lse_in[:, cut]
         inner = jnp.sum(grad.astype(f32).T * out_t[:, cut], axis=0, keepdims=True)
 
-        def step(index, dq_t, query=query, grad=grad, lo=lo, hi=hi, lse=lse, inner=inner):
+        def step(index, dq_t):
             base = pl.multiple_of(index * K_TILE, K_TILE)
             here = pl.ds(base, K_TILE)
             scores = scores_of(k_all[here, :], query, lo, hi, base, scale)
@@ -197,6 +213,10 @@
                 top = slot * rows + chunk * part
                 target[top : top + part, :HEAD] = (dk_all[pl.ds(at, part), :] * scale).astype(target.dtype)
                 target[top : top + part, HEAD:] = dv_all[pl.ds(at, part), :].astype(target.dtype)
+
+
+LARGE = pl.CostEstimate(flops=200_000_000_000, bytes_accessed=600_000_000, transcendentals=0)
+LITTLE = pl.CostEstimate(flops=1, bytes_accessed=1, transcendentals=0)
 
 
 def in_vmem():
@@ -220,6 +240,7 @@
         out_specs=(in_vmem(), in_vmem(), in_vmem()),
         scratch_shapes=[pltpu.VMEM((total, HEAD), bf16), pltpu.VMEM((HEAD, total), bf16)],
         compiler_params=pltpu.CompilerParams(vmem_limit_bytes=58 << 20),
+        cost_estimate=LITTLE,
         name="attention_forward",
     )(place, tiles, span, own, *rest)
 
@@ -243,8 +264,238 @@
             pltpu.VMEM((total, HEAD), f32),
         ],
         compiler_params=pltpu.CompilerParams(vmem_limit_bytes=58 << 20),
+        cost_estimate=LITTLE,
         name="attention_backward",
     )(place, tiles, span, own, grad, out_t, lse, *rest)
+
+
+def merge_kernel(grad_q, grad_kv, *refs):
+    got, outs = refs[0], refs[1:]
+    rows = outs[0].shape[0]
+    for slot, out in enumerate(outs):
+        cut = slice(slot * rows, (slot + 1) * rows)
+        out[:, :HEAD] = grad_q[cut, :]
+        out[:, HEAD:] = (grad_kv[cut, :] + got[cut, :].astype(f32)).astype(bf16)
+
+
+def merge(grad_q, grad_kv, got, count):
+    rows = grad_q.shape[0] // count
+    return pl.pallas_call(
+        merge_kernel,
+        out_shape=(jax.ShapeDtypeStruct((rows, 3 * HEAD), bf16),) * count,
+        in_specs=[in_vmem()] * 3,
+        out_specs=(in_vmem(),) * count,
+        compiler_params=pltpu.CompilerParams(vmem_limit_bytes=58 << 20),
+        cost_estimate=LARGE,
+        name="merge",
+    )(grad_q, grad_kv, got)
+
+
+def lanes_of(me, mask, depth):
+    at = jnp.bitwise_xor(me, mask) * depth
+    return pl.ds(pl.multiple_of(at, depth), depth)
+
+
+def project_kernel(rows, heads, depth, place, rows_in, *refs):
+    blocks, (out, a1, small, weights, result) = refs[:-5], refs[-5:]
+    me = place[0]
+    my_head = lax.rem(me // 2, heads)
+    if depth % HEAD:
+        small[...] = blocks[-1][...]
+        blocks = blocks[:-1]
+    for mask, block in enumerate(blocks):
+        at = lanes_of(me, mask, depth)
+        weights[at, :] = block[:depth, :]
+        if depth % HEAD == 0:
+            small[:, at] = block[depth : depth + 8, :depth].astype(f32)
+    part = rows // 4
+    for quarter in range(4):
+        cut = slice(quarter * part, (quarter + 1) * part)
+        normed, _ = norm_parts(rows_in[cut, :].astype(f32))
+        a1[cut, :] = (normed * small[0:1, :] + small[2:3, :]).astype(bf16)
+    width = heads * HEAD
+    for j in range(3):
+        result[:, j * width : (j + 1) * width] = jnp.dot(
+            a1[...], weights[:, j * width : (j + 1) * width], preferred_element_type=f32
+        ).astype(bf16)
+    for s in range(heads):
+        at = jnp.bitwise_xor(my_head, s) * HEAD
+        for j in range(3):
+            here = pl.ds(pl.multiple_of(j * width + at, HEAD), HEAD)
+            out[s * rows : (s + 1) * rows, j * HEAD : (j + 1) * HEAD] = result[:, here]
+
+
+def project(place, rows_in, blocks, heads, depth):
+    rows, width = rows_in.shape
+    cols = 3 * heads * HEAD
+    if depth % HEAD:
+        known = jnp.stack([block[depth : depth + 8, :depth] for block in blocks])
+        order = jnp.bitwise_xor(place[0], jnp.arange(len(blocks), dtype=jnp.int32))
+        known = jnp.take(known, order, axis=0).transpose(1, 0, 2).reshape(8, width)
+        blocks = [*blocks, known.astype(f32)]
+    return pl.pallas_call(
+        functools.partial(project_kernel, rows, heads, depth),
+        out_shape=(
+            jax.ShapeDtypeStruct((heads * rows, 3 * HEAD), bf16),
+            jax.ShapeDtypeStruct((rows, width), bf16),
+            jax.ShapeDtypeStruct((8, width), f32),
+        ),
+        in_specs=[in_smem()] + [in_vmem()] * (1 + len(blocks)),
+        out_specs=(in_vmem(),) * 3,
+        scratch_shapes=[pltpu.VMEM((width, cols), bf16), pltpu.VMEM((rows, cols), bf16)],
+        compiler_params=pltpu.CompilerParams(vmem_limit_bytes=58 << 20),
+        cost_estimate=LITTLE,
+        name="project",
+    )(place, rows_in, *blocks)
+
+
+def weight_grad_kernel(masks, added, place, rows_in, grads, *refs):
+    me, add, out = place[0], refs[0], refs[int(added)]
+    depth = out.shape[0] // len(masks)
+    whole = refs[-1] if depth % HEAD else None
+    if whole is not None:
+        whole[...] = lax.dot_general(rows_in[...], grads[...], (((0,), (0,)), ((), ())), preferred_element_type=f32)
+    for slot, mask in enumerate(masks):
+        at = lanes_of(me, mask, depth)
+        here = slice(slot * depth, (slot + 1) * depth)
+        if whole is not None:
+            block = whole[at, :]
+        else:
+            block = lax.dot_general(
+                rows_in[:, at], grads[...], (((0,), (0,)), ((), ())), preferred_element_type=f32
+            )
+        if added:
+            block = block + add[here, :].astype(f32)
+        out[here, :] = block.astype(bf16)
+
+
+def weight_grad(place, rows_in, grads, masks, add, depth):
+    extra = [] if add is None else [add]
+    return pl.pallas_call(
+        functools.partial(weight_grad_kernel, masks, add is not None),
+        out_shape=jax.ShapeDtypeStruct((len(masks) * depth, grads.shape[1]), bf16),
+        in_specs=[in_smem()] + [in_vmem()] * (2 + len(extra)),
+        out_specs=in_vmem(),
+        scratch_shapes=[pltpu.VMEM((rows_in.shape[1], grads.shape[1]), f32)] if depth % HEAD else [],
+        compiler_params=pltpu.CompilerParams(vmem_limit_bytes=58 << 20),
+        cost_estimate=LITTLE,
+        name="weight_grad",
+    )(place, rows_in, grads, *extra)
+
+
+def input_grad_kernel(depth, place, grads, *refs):
+    me = place[0]
+    if depth % HEAD:
+        blocks, out, weights = refs[:-2], refs[-2], refs[-1]
+        for mask, block in enumerate(blocks):
+            weights[lanes_of(me, mask, depth), :] = block[:depth, :]
+        out[...] = lax.dot_general(
+            grads[...], weights[...], (((1,), (1,)), ((), ())), preferred_element_type=f32
+        ).astype(bf16)
+        return
+    blocks, out = refs[:-1], refs[-1]
+    for mask, block in enumerate(blocks):
+        out[:, lanes_of(me, mask, depth)] = lax.dot_general(
+            grads[...], block[:depth, :], (((1,), (1,)), ((), ())), preferred_element_type=f32
+        ).astype(bf16)
+
+
+def input_grad(place, grads, blocks, depth):
+    return pl.pallas_call(
+        functools.partial(input_grad_kernel, depth),
+        out_shape=jax.ShapeDtypeStruct((grads.shape[0], depth * len(blocks)), bf16),
+        in_specs=[in_smem()] + [in_vmem()] * (1 + len(blocks)),
+        out_specs=in_vmem(),
+        scratch_shapes=[pltpu.VMEM((depth * len(blocks), grads.shape[1]), bf16)] if depth % HEAD else [],
+        compiler_params=pltpu.CompilerParams(vmem_limit_bytes=58 << 20),
+        cost_estimate=LITTLE,
+        name="input_grad",
+    )(place, grads, *blocks)
+
+
+def pair_grad_kernel(half, left, right, other_left, other_right, out):
+    def block(rows_in, grads):
+        out[0] = lax.dot_general(
+            rows_in[...], grads[...], (((0,), (0,)), ((), ())), preferred_element_type=f32
+        ).astype(bf16)
+
+    pl.when(pl.program_id(0) < half)(lambda: block(left, right))
+    pl.when(pl.program_id(0) >= half)(lambda: block(other_left, other_right))
+
+
+def pair_grad_of(left, right, other_left, other_right):
+    rows, width = left.shape
+    cols = right.shape[1]
+    step, half = 256, width // 256
+    first = pl.BlockSpec((rows, step), lambda i: (0, jnp.minimum(i, half - 1)))
+    second = pl.BlockSpec((rows, step), lambda i: (0, jnp.maximum(i - half, 0)))
+    return pl.pallas_call(
+        functools.partial(pair_grad_kernel, half),
+        grid=(2 * half,),
+        out_shape=jax.ShapeDtypeStruct((2, width, cols), bf16),
+        in_specs=[first, in_vmem(), second, in_vmem()],
+        out_specs=pl.BlockSpec((1, step, cols), lambda i: (i // half, i % half, 0)),
+        compiler_params=pltpu.CompilerParams(vmem_limit_bytes=58 << 20),
+        cost_estimate=LITTLE,
+        name="pair_grad",
+    )(left, right, other_left, other_right)
+
+
+def widen_kernel(pair, out_t, up, down, out, square):
+    part = jnp.zeros((1, 1), f32)
+    for source, target, turn in ((pair.at[0], up, False), (pair.at[1], down, True), (out_t, out, True)):
+        value = source[...].astype(f32)
+        part = part + jnp.sum(jnp.sum(value * value, axis=0, keepdims=True), axis=1, keepdims=True)
+        target[...] = value.T if turn else value
+    square[...] = jnp.broadcast_to(part, square.shape)
+
+
+def widen(pair, out_t):
+    _, cols, units = pair.shape
+    shapes = ((cols, units), (units, cols), out_t.shape[::-1], (8, HEAD))
+    return pl.pallas_call(
+        widen_kernel,
+        out_shape=tuple(jax.ShapeDtypeStruct(s, f32) for s in shapes),
+        in_specs=[in_vmem(), in_vmem()],
+        out_specs=(in_vmem(),) * 4,
+        compiler_params=pltpu.CompilerParams(vmem_limit_bytes=58 << 20),
+        cost_estimate=LITTLE,
+        name="widen",
+    )(pair, out_t)
+
+
+ADAM_STEPS = 8
+
+
+def adam_kernel(count, factor, decays, *refs):
+    ins, outs = refs[: 4 * count], refs[4 * count :]
+    for index in range(count):
+        master, grad, first, second = (r[...] for r in ins[4 * index : 4 * index + 4])
+        results = adam_update(master, grad, first, second, factor[0], decays[index])
+        for target, value in zip(outs[3 * index : 3 * index + 3], results):
+            target[...] = value
+
+
+def adam(factor, decays, groups):
+    specs, shapes, flat = ([], [], [])
+    for group in groups:
+        lines, cols = group[0].shape
+        spec = pl.BlockSpec((lines // ADAM_STEPS, cols), lambda step: (step, 0))
+        flat.extend(group)
+        specs.extend([spec] * 3)
+        shapes.extend([jax.ShapeDtypeStruct((lines, cols), f32)] * 3)
+    in_specs = [s for spec in specs[::3] for s in [spec] * 4]
+    results = pl.pallas_call(
+        functools.partial(adam_kernel, len(groups)),
+        grid=(ADAM_STEPS,),
+        out_shape=tuple(shapes),
+        in_specs=[in_smem(), in_smem()] + in_specs,
+        out_specs=tuple(specs),
+        compiler_params=pltpu.CompilerParams(vmem_limit_bytes=58 << 20),
+        cost_estimate=LITTLE,
+        name="adam",
+    )(factor.reshape(1), decays, *flat)
+    return [results[3 * i : 3 * i + 3] for i in range(len(groups))]
 
 
 def norm_parts(rows):
@@ -322,22 +573,21 @@
     scale = HEAD ** (-0.5)
     my_head = lax.rem(ctx_place // 2, heads)
 
-    first_pack = jnp.concatenate((w_qkv[0], w_qkv[1], w_qkv[2], w_out.T), axis=1).astype(bf16)
-    second_pack = jnp.concatenate((w_up, w_down.T), axis=1).astype(bf16)
-    first_full = lax.all_gather(first_pack, "ctx", axis=0, tiled=True)
-    second_pack, first_full = lax.optimization_barrier((second_pack, first_full))
-    second_full = lax.all_gather(second_pack, "ctx", axis=0, tiled=True)
-    qkv_full, out_full = first_full[:, : 3 * head_cols], first_full[:, 3 * head_cols :]
-    up_full, down_full = second_full[:, :units], second_full[:, units:]
-
-    small = jnp.concatenate((norm_gains, norm_biases), axis=0).astype(bf16)
-    small = lax.all_gather(small, "ctx", axis=1, tiled=True).astype(f32)
-    gain_one, gain_two, bias_one, bias_two = small[0], small[1], small[2], small[3]
-
-    x_slots = rows_to_slots(tokens, tp_place, tp_count)
-    c_slots = rows_to_slots(cotangent, tp_place, tp_count)
-    normed, _ = norm_parts(x_slots.astype(f32))
-    a1 = (normed * gain_one + bias_one).astype(bf16)
+    place = jnp.stack((ctx_place, tp_place))
+
+    small = jnp.concatenate((norm_gains, norm_biases), axis=0)
+    small = jnp.pad(small, ((0, 12), (0, 3 * head_cols - ctx_cols)))
+    qkv_pack = jnp.concatenate((w_qkv[0], w_qkv[1], w_qkv[2]), axis=1)
+    qkv_pack = jnp.concatenate((qkv_pack, small), axis=0).astype(bf16)
+    out_pack = w_out.T.astype(bf16)
+    rest_pack = jnp.concatenate((w_up, w_down.T), axis=1).astype(bf16)
+
+    x_slots = in_slots(tokens, tp_place, tp_count)
+    c_slots = in_slots(cotangent, tp_place, tp_count)
+    qkv_blocks, early = ctx_gather(qkv_pack, (out_pack, rest_pack, x_slots))
+    out_pack, rest_pack, x_slots = early
+    out_pack, rest_pack, qkv_blocks = lax.optimization_barrier((out_pack, rest_pack, qkv_blocks))
+    out_full = lax.all_gather(out_pack, "ctx", axis=0, tiled=True)
 
     group = [s << 1 for s in range(heads)]
     masks, rest_bits = ([group], [0] + list(range(heads.bit_length(), ctx_count.bit_length() - 1)))
@@ -346,7 +596,7 @@
     inner_rows = jnp.arange(part_rows, dtype=jnp.int32)
     positions = jnp.concatenate(
         [
-            jnp.bitwise_xor(ctx_place, m) * rows + lax.rem(tp_place - s + tp_count, tp_count) * part_rows + inner_rows
+            jnp.bitwise_xor(ctx_place, m) * rows + jnp.bitwise_xor(tp_place, s) * part_rows + inner_rows
             for m in group
             for s in range(tp_count)
         ]
@@ -359,16 +609,14 @@
             (jnp.max(hi.reshape(-1, Q_TILE), axis=1) + K_TILE - 1) // K_TILE,
         )
     )
-    place = jnp.stack((ctx_place, tp_place))
-
-    qkv = jnp.dot(a1, qkv_full, preferred_element_type=f32).astype(bf16)
-    own_parts = []
-    for s in range(heads):
-        at = jnp.bitwise_xor(my_head, s) * HEAD
-        piece = jnp.concatenate(
-            [lax.dynamic_slice_in_dim(qkv, j * head_cols + at, HEAD, 1) for j in range(3)], axis=1
-        )
-        own_parts.append(piece if s == 0 else ctx_xor(piece, s << 1))
+    pieces, a1, small = project(place, x_slots, qkv_blocks, heads, ctx_cols)
+    gain_one, gain_two, bias_two = small[0], small[1], small[3]
+    own_parts = [pieces[:rows]]
+    for s in range(1, heads):
+        own_parts.append(ctx_xor(pieces[s * rows : (s + 1) * rows], s << 1))
+    own_parts, rest_pack = lax.optimization_barrier((own_parts, rest_pack))
+    rest_full = lax.all_gather(rest_pack, "ctx", axis=0, tiled=True)
+    up_full, down_full = rest_full[:, :units], rest_full[:, units:]
     own = jnp.concatenate(own_parts, axis=0)
     rest, known = ([], own[:, HEAD:])
     for count, bit in enumerate(rest_bits):
@@ -392,20 +640,22 @@
     y1 = x_own + tp_scatter(attn.astype(bf16))
     normed2, rstd2 = norm_parts(y1)
     a2_own = (normed2 * gain_two + bias_two).astype(bf16)
-    a2 = jnp.concatenate(tp_gather(a2_own), axis=0)
-
     grad_act = jnp.dot(c_slots, down_full, preferred_element_type=f32)
+    a2, grad_act = lax.optimization_barrier((tp_gather(a2_own), grad_act))
+    a2 = jnp.concatenate(a2, axis=0)
+
     up = jnp.dot(a2, up_full, preferred_element_type=f32)
     cdf = 0.5 * (1.0 + lax.erf(up * inv_root_two))
     act = (up * cdf).astype(bf16)
     slope = cdf + up * jnp.exp(-0.5 * up * up) * inv_root_two_pi
     grad_up_in = (grad_act * slope).astype(bf16)
-    grad_h2 = lax.dot_general(grad_up_in, up_full, (((1,), (1,)), ((), ())), preferred_element_type=f32)
-    grad_h2 = tp_scatter(grad_h2.astype(bf16))
-    pair_left = jnp.stack((a2, c_slots))
-    pair_right = jnp.stack((grad_up_in, act))
-    pair_grad = jnp.einsum("btd,btf->bdf", pair_left, pair_right, preferred_element_type=f32).astype(bf16)
+    grad_h2 = lax.dot_general(grad_up_in, up_full, (((1,), (1,)), ((), ())), preferred_element_type=f32).astype(bf16)
+    grad_h2 = tp_send(grad_h2)
+    grad_h2[1], act, grad_up_in = lax.optimization_barrier((grad_h2[1], act, grad_up_in))
+    grad_h2 = tp_total(grad_h2)
+    pair_grad = pair_grad_of(a2, grad_up_in, c_slots, act)
     pair_shard = lax.psum_scatter(pair_grad, "ctx", scatter_dimension=1, tiled=True)
+    grad_h2, pair_grad = lax.optimization_barrier((grad_h2, pair_grad))
 
     dx2, dg2, dc2 = norm_back(grad_h2, normed2, rstd2, gain_two)
     c_own = c_slots[:part_rows].astype(f32)
@@ -414,11 +664,10 @@
     mixed = lax.dot_general(act, down_full, (((1,), (1,)), ((), ())), preferred_element_type=f32).astype(bf16)
     mixed, grad_attn = lax.optimization_barrier((mixed, grad_attn))
     block_out = (y1 + tp_scatter(mixed)).astype(bf16)
-    block_out = slots_to_rows(tp_gather(block_out), tp_place)
 
     grad_vals = jnp.dot(grad_attn, out_full, preferred_element_type=f32).astype(bf16)
     grad_outw = lax.dot_general(grad_attn, attn_vals, (((0,), (0,)), ((), ())), preferred_element_type=f32)
-    out_shard = lax.psum_scatter(grad_outw.astype(bf16), "ctx", scatter_dimension=0, tiled=True)
+    grad_outw = grad_outw.astype(bf16)
 
     grads = []
     for s in range(heads):
@@ -426,68 +675,76 @@
         grads.append(piece if s == 0 else ctx_xor(piece, s << 1))
     grads = jnp.concatenate(grads, axis=0)
     results = attention_backward(place, tiles, span, own, grads, mixed_t, lse, rest, *shape)
+    results, block_out = lax.optimization_barrier((results, block_out))
     grad_q, grad_kv, grad_rest = results[0], results[1], list(results[2:])
     for bit in reversed(rest_bits):
         got = ctx_xor(grad_rest.pop(), 1 << bit)
         cut = grad_kv.shape[0]
-        grad_kv = grad_kv + got[:cut].astype(f32)
-        grad_rest = split_add(grad_rest, got[cut:])
-    grad_own = jnp.concatenate((grad_q, grad_kv.astype(bf16)), axis=1)
-    back = [grad_own[:rows]]
+        if grad_rest:
+            grad_kv = grad_kv + got[:cut].astype(f32)
+            grad_rest = split_add(grad_rest, got[cut:])
+    grad_q, grad_outw = lax.optimization_barrier((grad_q, grad_outw))
+    grad_own = merge(grad_q, grad_kv, got, heads)
+    back = [grad_own[0]]
     for s in range(1, heads):
-        back.append(ctx_xor(grad_own[s * rows : (s + 1) * rows], s << 1))
+        back.append(ctx_xor(grad_own[s], s << 1))
     back = jnp.concatenate(back, axis=0)
+    back, late, pair_shard = lax.optimization_barrier((back, grad_outw, pair_shard))
+    out_shard = lax.psum_scatter(late, "ctx", scatter_dimension=0, tiled=True)
     by_head = [
         lax.dynamic_slice_in_dim(back, jnp.bitwise_xor(my_head, h) * rows, rows, 0) for h in range(heads)
     ]
     grad_qkv_in = jnp.concatenate(
         [by_head[h][:, j * HEAD : (j + 1) * HEAD] for j in range(3) for h in range(heads)], axis=1
     )
-    grad_qkvw = lax.dot_general(a1, grad_qkv_in, (((0,), (0,)), ((), ())), preferred_element_type=f32)
-    qkv_shard = lax.psum_scatter(grad_qkvw.astype(bf16), "ctx", scatter_dimension=0, tiled=True)
-    grad_h1 = lax.dot_general(grad_qkv_in, qkv_full, (((1,), (1,)), ((), ())), preferred_element_type=f32)
-    grad_h1 = tp_scatter(grad_h1.astype(bf16))
+    grad_h1 = input_grad(place, grad_qkv_in, qkv_blocks, ctx_cols)
+    grad_h1, grad_qkv_in = lax.optimization_barrier((grad_h1, grad_qkv_in))
+    chips = list(range(0, ctx_count, 2))
+    sent = weight_grad(place, a1, grad_qkv_in, [m ^ 1 for m in chips], None, ctx_cols)
+    block_out, sent = lax.optimization_barrier((tp_gather(block_out), sent))
+    got = ctx_xor(sent, 1)
+    summed = weight_grad(place, a1, grad_qkv_in, chips, got, ctx_cols)
+    grad_h1, summed = lax.optimization_barrier((grad_h1, summed))
+    qkv_grad = summed[:ctx_cols].astype(f32)
+    for slot, mask in enumerate(chips[1:], 1):
+        qkv_grad = qkv_grad + ctx_xor(summed[slot * ctx_cols : (slot + 1) * ctx_cols], mask).astype(f32)
+    grad_h1, qkv_grad = lax.optimization_barrier((tp_scatter(grad_h1), qkv_grad))
+    block_out = slots_to_rows(block_out, tp_place)
     normed1, rstd1 = norm_parts(x_own)
     dx1, dg1, dc1 = norm_back(grad_h1, normed1, rstd1, gain_one)
     grad_tokens = (grad_y1 + dx1).astype(bf16)
-    grad_tokens = slots_to_rows(tp_gather(grad_tokens), tp_place)
-
-    qkv_grad = qkv_shard.astype(f32)
-    out_grad = out_shard.astype(f32)
-    up_grad = pair_shard[0].astype(f32)
-    down_grad = pair_shard[1].astype(f32)
-    square = jnp.sum(qkv_grad * qkv_grad) + jnp.sum(out_grad * out_grad)
-    square = square + jnp.sum(up_grad * up_grad) + jnp.sum(down_grad * down_grad)
+    dx1, pair_shard, out_shard = lax.optimization_barrier((dx1, pair_shard, out_shard))
+    up_grad, down_grad, out_grad, square = widen(pair_shard, out_shard)
+    square = square[0, 0] + jnp.sum(qkv_grad * qkv_grad)
     lines = jnp.stack((dg1, dg2, dc1, dc2)).reshape(-1, HEAD)
     sent = jnp.concatenate((lines, jnp.full((8, HEAD), square, f32)), axis=0)
     total = sum_over_all(sent)
+    grad_tokens = slots_to_rows(tp_gather(grad_tokens), tp_place)
     small_grad = total[:-8].reshape(4, width)
     total_sq = total[-1, 0] + jnp.sum(small_grad * small_grad)
     grad_norm = jnp.sqrt(total_sq)
     factor = 1.0 / jnp.maximum(grad_norm, 1.0)
     small_own = lax.dynamic_slice_in_dim(small_grad, ctx_place * ctx_cols, ctx_cols, 1)
 
-    shards = (
-        jnp.stack([qkv_grad[:, j * head_cols : (j + 1) * head_cols] for j in range(3)]),
-        out_grad.T,
-        up_grad,
-        down_grad.T,
-        small_own[:2],
-        small_own[2:],
+    qkv_grad = jnp.stack([qkv_grad[:, j * head_cols : (j + 1) * head_cols] for j in range(3)])
+    flags = decay_mask.astype(f32)
+    flat = lambda value: value.reshape(-1, head_cols)
+    matrices = adam(
+        factor,
+        flags,
+        (
+            (flat(w_qkv), flat(qkv_grad), flat(m_qkv), flat(v_qkv)),
+            (w_out, out_grad, m_out, v_out),
+            (w_up, up_grad, m_up, v_up),
+            (w_down, down_grad, m_down, v_down),
+        ),
     )
-    masters = (w_qkv, w_out, w_up, w_down, norm_gains, norm_biases)
-    firsts = (m_qkv, m_out, m_up, m_down, m_gains, m_biases)
-    seconds = (v_qkv, v_out, v_up, v_down, v_gains, v_biases)
-    amounts, new_first, new_second = ([], [], [])
-    for index in range(6):
-        decays = decay_mask[index].astype(f32)
-        amount, first_new, second_new = adam_update(
-            masters[index], shards[index], firsts[index], seconds[index], factor, decays
-        )
-        amounts.append(amount)
-        new_first.append(first_new)
-        new_second.append(second_new)
-    return (block_out, grad_tokens, grad_norm, *shards, *amounts, *new_first, *new_second)
+    matrices[0] = [value.reshape(w_qkv.shape) for value in matrices[0]]
+    gains_new = adam_update(norm_gains, small_own[:2], m_gains, v_gains, factor, flags[4])
+    biases_new = adam_update(norm_biases, small_own[2:], m_biases, v_biases, factor, flags[5])
+    shards = (qkv_grad, out_grad, up_grad, down_grad, small_own[:2], small_own[2:])
+    updates = list(zip(*matrices, gains_new, biases_new))
+    return (block_out, grad_tokens, grad_norm, *shards, *updates[0], *updates[1], *updates[2])
 
 
 def split_add(arrays, extra):

time: 757 us -> 604 us (0.80)
  waiting for transfers between devices: 379 us -> 272 us
  Pallas kernels: 28.6 us -> 112 us
  other arithmetic: 81.9 us -> 37.8 us
  matrix products: 73.9 us -> 42.4 us
  local copies, waits for them, and re-layouts: 56.4 us -> 29.2 us
  starting transfers between devices: 92.8 us -> 82.8 us
  blocking collectives: 8.86 us -> 0 us
    ppermute x27, waiting for transfers between devices: 269 us -> 158 us  [tp_xor(): lax.ppermute(value, 'tp', [(place, place ^ mask) for place in range(count)])]
    pallas_call x0 -> x8, Pallas kernels: none -> 73.6 us  [the longest x1 18.8 us: pair_grad_of(): pl.pallas_call(functools.partial(pair_grad_kernel, half), grid=(2 * half,...]
    ppermute x18 -> x29, waiting for transfers between devices: 54.8 us -> 106 us  [ctx_xor(): lax.ppermute(value, 'ctx', [(place, place ^ mask) for place in range(coun...]
    all_gather x2, waiting for transfers between devices: 55 us -> 7.64 us  [the longest x1 7.62 us: per_device(): rest_full = lax.all_gather(rest_pack, 'ctx', axis=0, tiled=True)]
    dot_general x4 -> x0, matrix products: 31.5 us -> none  [the longest x1 15.9 us: per_device(): jnp.einsum('btd,btf->bdf', pair_left, pair_right, preferred_element_type=...]
    unnamed x171 -> x131, local copies, waits for them, and re-layouts: 42.3 us -> 11.2 us
    mul x5 -> x1, other arithmetic: 20.8 us -> 0.7 us  [adam_update(): amount = learn_rate * (update + decay_rate * decays * master)]
    ppermute x27, starting transfers between devices: 74.8 us -> 58 us  [tp_xor(): lax.ppermute(value, 'tp', [(place, place ^ mask) for place in range(count)])]
  transfers between devices with their start and end apart: 50 -> 60, of which waited for: 30 -> 35; matrix products, arithmetic and copies ran while one was open for 17% -> 13% of each run, Pallas kernels for 2% -> 18%
where the time goes in v2:
time: 604 us; the launch traced here: 597 us
  waiting for transfers between devices  272 us (45%)
  Pallas kernels  112 us (19%)
  starting transfers between devices  82.8 us (14%)
  matrix products  42.4 us (7%)
  other arithmetic  37.8 us (6%)
  local copies, waits for them, and re-layouts  29.2 us (5%)
  between operations  20.7 us (3%)
    ppermute x27, waiting for transfers between devices, tp_xor(): lax.ppermute(value, 'tp', [(place, place ^ mask) for place in range(count)])  158 us
    ppermute x29, waiting for transfers between devices, ctx_xor(): lax.ppermute(value, 'ctx', [(place, place ^ mask) for place in range(coun...  106 us
    ppermute x27, starting transfers between devices, tp_xor(): lax.ppermute(value, 'tp', [(place, place ^ mask) for place in range(count)])  58 us
    ppermute x29, starting transfers between devices, ctx_xor(): lax.ppermute(value, 'ctx', [(place, place ^ mask) for place in range(coun...  24.7 us
    pallas_call x1, Pallas kernels, attention_backward(): pl.pallas_call(functools.partial(backward_kernel, rows, chunks, masks, sc...  21 us
    pallas_call x1, Pallas kernels, pair_grad_of(): pl.pallas_call(functools.partial(pair_grad_kernel, half), grid=(2 * half,...  18.8 us
    pallas_call x1, Pallas kernels, attention_forward(): pl.pallas_call(functools.partial(forward_kernel, rows, chunks, masks, sca...  17.6 us
    pallas_call x1, Pallas kernels, adam(): pl.pallas_call(functools.partial(adam_kernel, len(groups)), grid=(ADAM_ST...  17.2 us
  transfers between devices with their start and end apart: 60, of which 35 were waited for; matrix products, arithmetic and copies ran while one was open for 13% of the time, Pallas kernels for 18%

profile of v2, /device:TPU:0, one launch (start us, length us, event | category | flops | bytes accessed | tf_op | source)
XLA Modules:
  0.0 597.0 jit_solution(12245755704381818549)
XLA Ops:
  10.3 3.0 collective-permute-start
  16.0 2.9 constant_dynamic-slice_fusion.24
  21.0 3.1 pad_maximum_fusion.1.rows_in
  25.5 7.3 %collective-permute-done.refs_2_ = bf16[272,1536]{1,0:T(8,128)(2,1)} collective-permute-done((bf16[272,1536]{1,0:T(8,128)(2,1)S(1)}, bf16[272,1536]{1,0:T(8,128)(2,1)}, u32[]{:S(2)}, u32[]{:S(2)}) %collective-permute-start) | collective-permute-done | bytes 835616 | tf_op jit(solution)/shard_map/ppermute | solution.py:32
  32.8 19.5 %collective-permute-done.3.refs_4_ = bf16[272,1536]{1,0:T(8,128)(2,1)} collective-permute-done((bf16[272,1536]{1,0:T(8,128)(2,1)S(1)}, bf16[272,1536]{1,0:T(8,128)(2,1)}, u32[]{:S(2)}, u32[]{:S(2)}) %collective-permute-start.3) | collective-permute-done | bytes 835616 | tf_op jit(solution)/shard_map/ppermute | solution.py:32
  52.8 2.0 collective-permute-done.4.refs_5_
  57.0 9.6 %project.1 = (bf16[2048,384]{1,0:T(8,128)(2,1)}, bf16[512,2048]{1,0:T(8,128)(2,1)}, f32[8,2048]{1,0:T(8,128)}) custom-call(s32[2]{0:T(128)} %pad_add_fusion.2.place, bf16[512,2048]{1,0:T(8,128)(2,1)} %pad_maximum_fusion.1.rows_in, bf16[272,1536]{1,0:T(8,128)(2,1)} %copy-done.9, bf16[272,1536]{1,0:T(8,128)(2,1)} %collective-permute-done.1.refs_1_, ...), custom_call_target="tpu_custom_call" | custom-call | flops 1 | bytes 1 | tf_op jit(solution)/shard_map/project/pallas_call | solution.py:336
  68.2 2.0 collective-permute-start.8
  71.7 11.3 %collective-permute-done.7 = bf16[512,384]{1,0:T(8,128)(2,1)S(1)} collective-permute-done((bf16[512,384]{1,0:T(8,128)(2,1)S(1)}, bf16[512,384]{1,0:T(8,128)(2,1)S(1)}, u32[]{:S(2)}, u32[]{:S(2)}) %collective-permute-start.7) | collective-permute-done | bytes 393248 | tf_op jit(solution)/shard_map/ppermute | solution.py:32
  83.0 2.4 collective-permute-done.8
  85.4 9.0 %collective-permute-done.9 = bf16[512,384]{1,0:T(8,128)(2,1)S(1)} collective-permute-done((bf16[512,384]{1,0:T(8,128)(2,1)S(1)}, bf16[512,384]{1,0:T(8,128)(2,1)S(1)}, u32[]{:S(2)}, u32[]{:S(2)}) %collective-permute-start.9) | collective-permute-done | bytes 393248 | tf_op jit(solution)/shard_map/ppermute | solution.py:32
  100.6 17.6 %attention_forward.1 = (bf16[2048,128]{1,0:T(8,128)(2,1)}, f32[128,2048]{1,0:T(8,128)}, f32[1,2048]{1,0:T(1,128)}) custom-call(s32[2]{0:T(128)} %pad_add_fusion.2.place, s32[2,8]{1,0:T(2,128)} %pad_add_fusion.1.tiles, s32[2,2048]{1,0:T(2,128)} %pad_add_fusion.refs_0_, bf16[2048,384]{1,0:T(8,128)(2,1)} %copy-done.4, bf16[2048,256]{1,0:T(8,128)(2,1)} %copy-done.11), custom_call_target="tpu_custom_call" | custom-call | flops 1 | bytes 1 | tf_op jit(solution)/shard_map/attention_forward/pallas_call | solution.py:232
  123.1 6.4 %collective-permute-done.13 = bf16[512,128]{1,0:T(8,128)(2,1)S(1)} collective-permute-done((bf16[512,128]{1,0:T(8,128)(2,1)S(1)}, bf16[512,128]{1,0:T(8,128)(2,1)S(1)}, u32[]{:S(2)}, u32[]{:S(2)}) %collective-permute-start.13) | collective-permute-done | bytes 131104 | tf_op jit(solution)/shard_map/ppermute | solution.py:32
  129.5 1.7 collective-permute-done.12
  131.2 2.6 collective-permute-done.11
  133.9 2.9 convolution_convert_fusion.1
  137.0 3.7 collective-permute-start.16
  143.0 10.8 %collective-permute-done.16 = bf16[128,2048]{1,0:T(8,128)(2,1)S(1)} collective-permute-done((bf16[128,2048]{1,0:T(8,128)(2,1)S(1)}, bf16[128,2048]{1,0:T(8,128)(2,1)S(1)}, u32[]{:S(2)}, u32[]{:S(2)}) %collective-permute-start.16) | collective-permute-done | bytes 524320 | tf_op jit(solution)/shard_map/ppermute | solution.py:47
  153.8 30.7 %collective-permute-done.15 = bf16[128,2048]{1,0:T(8,128)(2,1)S(1)} collective-permute-done((bf16[128,2048]{1,0:T(8,128)(2,1)S(1)}, bf16[128,2048]{1,0:T(8,128)(2,1)S(1)}, u32[]{:S(2)}, u32[]{:S(2)}) %collective-permute-start.15) | collective-permute-done | bytes 524320 | tf_op jit(solution)/shard_map/ppermute | solution.py:47
  186.2 3.0 collective-permute-start.18
  190.6 7.6 %all-gather.5.cloned.1.call-done = bf16[2048,4096]{0,1:T(8,128)(2,1)} async-done(((bf16[256,4096]{0,1:T(8,128)(2,1)}), bf16[2048,4096]{0,1:T(8,128)(2,1)}) %all-gather.5.cloned.1.call-update) | async-done | bytes 16777232 | tf_op jit(solution)/shard_map/all_gather | solution.py:618
  198.2 10.1 %fusion.6 = f32[512,2048]{1,0:T(8,128)} fusion(bf16[2048,4096]{0,1:T(8,128)(2,1)} %all-gather.5.cloned.1.call-done, bf16[128,2048]{1,0:T(8,128)(2,1)S(1)} %copy-done.26, bf16[128,2048]{1,0:T(8,128)(2,1)} %get-tuple-element.241, bf16[128,2048]{1,0:T(8,128)(2,1)S(1)} %copy-done.25, bf16[128,2048]{1,0:T(8,128)(2,1)S(1)} %copy-done.10), kind=kOutput, calls=%fused_computation.6 | convolution fusion | flops 4303355904 | bytes 14680064 | tf_op jit(solution)/shard_map/dot_general | solution.py:643
  208.3 1.9 collective-permute-done.17
  210.2 14.4 %collective-permute-done.18 = bf16[128,2048]{1,0:T(8,128)(2,1)} collective-permute-done((bf16[128,2048]{1,0:T(8,128)(2,1)S(1)}, bf16[128,2048]{1,0:T(8,128)(2,1)}, u32[]{:S(2)}, u32[]{:S(2)}) %collective-permute-start.18) | collective-permute-done | bytes 524320 | tf_op jit(solution)/shard_map/ppermute | solution.py:47
  228.2 11.0 %multiply_convert_fusion = (bf16[512,2048]{1,0:T(8,128)(2,1)}, bf16[512,2048]{1,0:T(8,128)(2,1)S(1)}) fusion(f32[512,2048]{1,0:T(8,128)} %fusion.6, bf16[512,2048]{1,0:T(8,128)(2,1)S(1)} %constant_dynamic-update-slice_fusion.21.left, bf16[2048,4096]{0,1:T(8,128)(2,1)} %all-gather.5.cloned.1.call-done), kind=kOutput, calls=%fused_computation.15 | convolution fusion | flops 4307550208 | bytes 18874368 | tf_op jit(solution)/shard_map/dot_general | solution.py:647
  239.2 4.9 fusion.17
  246.0 9.9 %collective-permute-start.20 = (bf16[128,2048]{1,0:T(8,128)(2,1)}, bf16[128,2048]{1,0:T(8,128)(2,1)}, u32[]{:S(2)}, u32[]{:S(2)}) collective-permute-start(bf16[128,2048]{1,0:T(8,128)(2,1)} %get-tuple-element.237), channel_id=1, source_target_pairs={{0,1},{1,0},{2,3},{3,2},{4,5},{5,4},{6,7},{7,6},{8,9},{9,8},{10,11... | collective-permute-start | bytes 1572872 | tf_op jit(solution)/shard_map/ppermute | solution.py:47
  258.7 16.7 %collective-permute-done.20 = bf16[128,2048]{1,0:T(8,128)(2,1)} collective-permute-done((bf16[128,2048]{1,0:T(8,128)(2,1)}, bf16[128,2048]{1,0:T(8,128)(2,1)}, u32[]{:S(2)}, u32[]{:S(2)}) %collective-permute-start.20) | collective-permute-done | bytes 524320 | tf_op jit(solution)/shard_map/ppermute | solution.py:47
  275.4 18.8 %pair_grad.1 = bf16[2,2048,2048]{2,1,0:T(8,128)(2,1)} custom-call(bf16[512,2048]{1,0:T(8,128)(2,1)} %copy-done.17, bf16[512,2048]{1,0:T(8,128)(2,1)} %copy-done.19, bf16[512,2048]{1,0:T(8,128)(2,1)} %pad_maximum_fusion.2.other_left, bf16[512,2048]{1,0:T(8,128)(2,1)} %get-tuple-element.135.other_right), custom_call_target="tpu_custom_call" | custom-call | flops 1 | bytes 1 | tf_op jit(solution)/shard_map/pair_grad/pallas_call | solution.py:432
  294.3 7.0 %collective-permute-done.21 = bf16[128,2048]{1,0:T(8,128)(2,1)} collective-permute-done((bf16[128,2048]{1,0:T(8,128)(2,1)}, bf16[128,2048]{1,0:T(8,128)(2,1)}, u32[]{:S(2)}, u32[]{:S(2)}) %collective-permute-start.21) | collective-permute-done | bytes 524320 | tf_op jit(solution)/shard_map/ppermute | solution.py:47
  301.3 2.3 convert_add_fusion.3
  307.4 3.2 collective-permute-start.23
  310.6 9.6 %fusion.14 = bf16[512,2048]{1,0:T(8,128)(2,1)S(1)} fusion(bf16[512,2048]{1,0:T(8,128)(2,1)S(1)} %copy-done.18, bf16[2048,4096]{0,1:T(8,128)(2,1)} %all-gather.5.cloned.1.call-done), kind=kOutput, calls=%fused_computation.17 | convolution fusion | flops 4296015872 | bytes 12582912 | tf_op jit(solution)/shard_map/dot_general | solution.py:664
  320.1 2.8 collective-permute-done.25
  322.9 25.4 %collective-permute-done.24 = bf16[128,2048]{1,0:T(8,128)(2,1)S(1)} collective-permute-done((bf16[128,2048]{1,0:T(8,128)(2,1)S(1)}, bf16[128,2048]{1,0:T(8,128)(2,1)S(1)}, u32[]{:S(2)}, u32[]{:S(2)}) %collective-permute-start.24) | collective-permute-done | bytes 524320 | tf_op jit(solution)/shard_map/ppermute | solution.py:47
  349.7 3.0 collective-permute-start.31
  357.2 7.6 %collective-permute-done.28 = bf16[512,128]{1,0:T(8,128)(2,1)S(1)} collective-permute-done((bf16[512,128]{1,0:T(8,128)(2,1)S(1)}, bf16[512,128]{1,0:T(8,128)(2,1)S(1)}, u32[]{:S(2)}, u32[]{:S(2)}) %collective-permute-start.28) | collective-permute-done | bytes 131104 | tf_op jit(solution)/shard_map/ppermute | solution.py:32
  366.1 6.3 %collective-permute-done.26 = bf16[512,128]{1,0:T(8,128)(2,1)S(1)} collective-permute-done((bf16[512,128]{1,0:T(8,128)(2,1)S(1)}, bf16[512,128]{1,0:T(8,128)(2,1)S(1)}, u32[]{:S(2)}, u32[]{:S(2)}) %collective-permute-start.26) | collective-permute-done | bytes 131104 | tf_op jit(solution)/shard_map/ppermute | solution.py:32
  373.3 21.0 %attention_backward.1 = (bf16[2048,128]{1,0:T(8,128)(2,1)}, f32[2048,256]{1,0:T(8,128)}, bf16[2048,256]{1,0:T(8,128)(2,1)}) custom-call(s32[2]{0:T(128)} %pad_add_fusion.2.place, s32[2,8]{1,0:T(2,128)} %pad_add_fusion.1.tiles, s32[2,2048]{1,0:T(2,128)} %pad_add_fusion.refs_0_, bf16[2048,384]{1,0:T(8,128)(2,1)} %copy-done.4, ...), custom_call_target="tpu_custom_call" | custom-call | flops 1 | bytes 1 | tf_op jit(solution)/shard_map/attention_backward/pallas_call | solution.py:250
  394.4 2.4 add_convert_fusion.1
  396.7 2.6 convolution_convert_fusion
  400.6 3.5 merge.1
  404.0 2.0 collective-permute-start.38
  408.0 2.8 collective-permute-start.33
  410.8 10.5 %collective-permute-done.38 = bf16[512,384]{1,0:T(8,128)(2,1)S(1)} collective-permute-done((bf16[512,384]{1,0:T(8,128)(2,1)}, bf16[512,384]{1,0:T(8,128)(2,1)S(1)}, u32[]{:S(2)}, u32[]{:S(2)}) %collective-permute-start.38) | collective-permute-done | bytes 393248 | tf_op jit(solution)/shard_map/ppermute | solution.py:32
  421.3 3.3 collective-permute-start.34
  424.5 4.0 collective-permute-done.37
  433.2 8.3 %input_grad.1 = bf16[512,2048]{1,0:T(8,128)(2,1)} custom-call(s32[2]{0:T(128)} %pad_add_fusion.2.place, bf16[512,1536]{1,0:T(8,128)(2,1)} %copy-done.2, bf16[272,1536]{1,0:T(8,128)(2,1)} %copy-done.9, bf16[272,1536]{1,0:T(8,128)(2,1)} %collective-permute-done.1.refs_1_, bf16[272,1536]{1,0:T(8,128)(2,1)} %collective-permute-done.refs_2_, ...), custom_call_target="tpu_custom_call" | custom-call | flops 1 | bytes 1 | tf_op jit(solution)/shard_map/input_grad/pallas_call | solution.py:404
  441.5 5.6 weight_grad.2
  450.5 2.8 collective-permute-done.39.refs_0_
  453.2 6.5 %weight_grad.3 = bf16[1024,1536]{1,0:T(8,128)(2,1)} custom-call(s32[2]{0:T(128)} %pad_add_fusion.2.place, bf16[512,2048]{1,0:T(8,128)(2,1)} %get-tuple-element.147.rows_in, bf16[512,1536]{1,0:T(8,128)(2,1)} %copy-done.2, bf16[1024,1536]{1,0:T(8,128)(2,1)} %collective-permute-done.39.refs_0_), custom_call_target="tpu_custom_call" | custom-call | flops 1 | bytes 1 | tf_op jit(solution)/shard_map/weight_grad/pallas_call | solution.py:374
  459.9 3.4 collective-permute-start.42
  463.3 7.9 %collective-permute-start.41 = (bf16[128,2048]{1,0:T(8,128)(2,1)S(1)}, bf16[128,2048]{1,0:T(8,128)(2,1)S(1)}, u32[]{:S(2)}, u32[]{:S(2)}) collective-permute-start(bf16[128,2048]{1,0:T(8,128)(2,1)S(1)} %get-tuple-element.227), channel_id=1, source_target_pairs={{0,2},{1,3},{2,0},{3,1},{4,6},{5,7},{6,4},{7,5},{8,10},{9,11},{10,... | collective-permute-start | bytes 1572872 | tf_op jit(solution)/shard_map/ppermute | solution.py:47
  473.4 3.2 collective-permute-done.42
  479.5 30.0 %collective-permute-done.41 = bf16[128,2048]{1,0:T(8,128)(2,1)S(1)} collective-permute-done((bf16[128,2048]{1,0:T(8,128)(2,1)S(1)}, bf16[128,2048]{1,0:T(8,128)(2,1)S(1)}, u32[]{:S(2)}, u32[]{:S(2)}) %collective-permute-start.41) | collective-permute-done | bytes 524320 | tf_op jit(solution)/shard_map/ppermute | solution.py:47
  509.8 6.8 %collective-permute-done.44 = bf16[256,1536]{1,0:T(8,128)(2,1)S(1)} collective-permute-done((bf16[256,1536]{1,0:T(8,128)(2,1)S(1)}, bf16[256,1536]{1,0:T(8,128)(2,1)S(1)}, u32[]{:S(2)}, u32[]{:S(2)}) %collective-permute-start.44) | collective-permute-done | bytes 786464 | tf_op jit(solution)/shard_map/ppermute | solution.py:32
  519.1 2.5 add_convert_fusion
  521.6 4.1 widen.1
  529.5 6.1 %collective-permute-start.50 = (f32[72,128]{1,0:T(8,128)S(1)}, f32[72,128]{1,0:T(8,128)S(1)}, u32[]{:S(2)}, u32[]{:S(2)}) collective-permute-start(f32[72,128]{1,0:T(8,128)S(1)} %concatenate.144), channel_id=1, source_target_pairs={{0,2},{1,3},{2,0},{3,1},{4,6},{5,7},{6,4},{7,5},{8,10},{9,11},{10,... | collective-permute-start | bytes 110600 | tf_op jit(solution)/shard_map/ppermute | solution.py:47
  536.2 2.8 pad_maximum_fusion.4
  539.0 3.2 collective-permute-start.48
  543.6 2.2 collective-permute-start.54
  553.7 17.2 %adam.1 = (f32[768,512]{1,0:T(8,128)}, f32[768,512]{1,0:T(8,128)}, f32[768,512]{1,0:T(8,128)}, f32[512,256]{1,0:T(8,128)}, f32[512,256]{1,0:T(8,128)}, /*index=5...) custom-call(f32[1]{0:T(128)} %bitcast.41.factor, ...), custom_call_target="tpu_custom_call" | custom-call | flops 1 | bytes 1 | tf_op jit(solution)/shard_map/adam/pallas_call | solution.py:488
  571.7 15.2 %collective-permute-done.47 = bf16[128,2048]{1,0:T(8,128)(2,1)S(1)} collective-permute-done((bf16[128,2048]{1,0:T(8,128)(2,1)S(1)}, bf16[128,2048]{1,0:T(8,128)(2,1)S(1)}, u32[]{:S(2)}, u32[]{:S(2)}) %collective-permute-start.47) | collective-permute-done | bytes 524320 | tf_op jit(solution)/shard_map/ppermute | solution.py:47
  (327 shorter events, 82.7 us)
Async XLA Ops:
  7.2 126.7 %all-gather.3.cloned.1.call-start = ((), (), s32[]{:S(2)}) async-start(), calls=%async_computation.2 | async-start | bytes 2359296 | tf_op jit(solution)/shard_map/all_gather | solution.py:590
  10.3 22.5 %collective-permute-start = (bf16[272,1536]{1,0:T(8,128)(2,1)S(1)}, bf16[272,1536]{1,0:T(8,128)(2,1)}, u32[]{:S(2)}, u32[]{:S(2)}) collective-permute-start(bf16[272,1536]{1,0:T(8,128)(2,1)S(1)} %pad_maximum_fusion.9.refs_0_), channel_id=1, source_target_pairs={{0,8},{4,12},{8,0},{12,4},{16,24},{20,28},{24,16},{28,20},{1,9},{5... | collective-permute-start | bytes 2506760 | tf_op jit(solution)/shard_map/ppermute | solution.py:32
  13.3 39.5 %collective-permute-start.1 = (bf16[272,1536]{1,0:T(8,128)(2,1)S(1)}, bf16[272,1536]{1,0:T(8,128)(2,1)}, u32[]{:S(2)}, u32[]{:S(2)}) collective-permute-start(bf16[272,1536]{1,0:T(8,128)(2,1)S(1)} %pad_maximum_fusion.9.refs_0_), channel_id=1, source_target_pairs={{0,4},{4,0},{8,12},{12,8},{16,20},{20,16},{24,28},{28,24},{1,5},{5... | collective-permute-start | bytes 2506760 | tf_op jit(solution)/shard_map/ppermute | solution.py:32
  13.3 39.0 %collective-permute-start.3 = (bf16[272,1536]{1,0:T(8,128)(2,1)S(1)}, bf16[272,1536]{1,0:T(8,128)(2,1)}, u32[]{:S(2)}, u32[]{:S(2)}) collective-permute-start(bf16[272,1536]{1,0:T(8,128)(2,1)S(1)} %pad_maximum_fusion.9.refs_0_), channel_id=1, source_target_pairs={{0,16},{4,20},{8,24},{12,28},{16,0},{20,4},{24,8},{28,12},{1,17},{... | collective-permute-start | bytes 2506760 | tf_op jit(solution)/shard_map/ppermute | solution.py:32
  14.8 37.5 %collective-permute-start.5 = (bf16[272,1536]{1,0:T(8,128)(2,1)S(1)}, bf16[272,1536]{1,0:T(8,128)(2,1)}, u32[]{:S(2)}, u32[]{:S(2)}) collective-permute-start(bf16[272,1536]{1,0:T(8,128)(2,1)S(1)} %pad_maximum_fusion.9.refs_0_), channel_id=1, source_target_pairs={{0,24},{4,28},{8,16},{12,20},{16,8},{20,12},{24,0},{28,4},{1,25},{... | collective-permute-start | bytes 2506760 | tf_op jit(solution)/shard_map/ppermute | solution.py:32
  32.8 20.0 %collective-permute-start.2 = (bf16[272,1536]{1,0:T(8,128)(2,1)}, bf16[272,1536]{1,0:T(8,128)(2,1)S(1)}, u32[]{:S(2)}, u32[]{:S(2)}) collective-permute-start(bf16[272,1536]{1,0:T(8,128)(2,1)} %collective-permute-done.refs_2_), channel_id=1, source_target_pairs={{0,4},{4,0},{8,12},{12,8},{16,20},{20,16},{24,28},{28,24},{1,5},{5... | collective-permute-start | bytes 2506760 | tf_op jit(solution)/shard_map/ppermute | solution.py:32
  52.3 2.6 collective-permute-start.4
  52.3 3.8 collective-permute-start.6
  56.1 142.1 %all-gather.5.cloned.1.call-start = ((), (), s32[]{:S(2)}) async-start(), calls=%async_computation.3 | async-start | bytes 18874368 | tf_op jit(solution)/shard_map/all_gather | solution.py:618
  66.6 27.9 %copy-start.49 = (s32[4]{0:T(128)S(1)}, s32[4]{0:T(128)}, u32[]{:S(2)}) copy-start(s32[4]{0:T(128)} %param.42) | copy-start | bytes 52
  68.2 14.9 %collective-permute-start.7 = (bf16[512,384]{1,0:T(8,128)(2,1)S(1)}, bf16[512,384]{1,0:T(8,128)(2,1)S(1)}, u32[]{:S(2)}, u32[]{:S(2)}) collective-permute-start(bf16[512,384]{1,0:T(8,128)(2,1)S(1)} %get-tuple-element.254), channel_id=1, source_target_pairs={{0,8},{4,12},{8,0},{12,4},{16,24},{20,28},{24,16},{28,20},{1,9},{5... | collective-permute-start | bytes 1179656 | tf_op jit(solution)/shard_map/ppermute | solution.py:32
  68.2 17.2 %collective-permute-start.8 = (bf16[512,384]{1,0:T(8,128)(2,1)S(1)}, bf16[512,384]{1,0:T(8,128)(2,1)S(1)}, u32[]{:S(2)}, u32[]{:S(2)}) collective-permute-start(bf16[512,384]{1,0:T(8,128)(2,1)S(1)} %get-tuple-element.253), channel_id=1, source_target_pairs={{0,16},{4,20},{8,24},{12,28},{16,0},{20,4},{24,8},{28,12},{1,17},{... | collective-permute-start | bytes 1179656 | tf_op jit(solution)/shard_map/ppermute | solution.py:32
  70.3 24.1 %collective-permute-start.9 = (bf16[512,384]{1,0:T(8,128)(2,1)S(1)}, bf16[512,384]{1,0:T(8,128)(2,1)S(1)}, u32[]{:S(2)}, u32[]{:S(2)}) collective-permute-start(bf16[512,384]{1,0:T(8,128)(2,1)S(1)} %get-tuple-element.252), channel_id=1, source_target_pairs={{0,24},{4,28},{8,16},{12,20},{16,8},{20,12},{24,0},{28,4},{1,25},{... | collective-permute-start | bytes 1179656 | tf_op jit(solution)/shard_map/ppermute | solution.py:32
  94.4 337.1 %reduce-scatter.3.cloned.1.call-start = ((), (), s32[]{:S(2)}) async-start(), calls=%async_computation.4 | async-start | bytes 18874368 | tf_op jit(solution)/shard_map/reduce_scatter | solution.py:657
  96.4 3.2 collective-permute-start.10
  99.6 23.3 %copy-start = (bf16[512,2048]{1,0:T(8,128)(2,1)S(1)}, bf16[512,2048]{1,0:T(8,128)(2,1)}, u32[]{:S(2)}) copy-start(bf16[512,2048]{1,0:T(8,128)(2,1)} %pad_maximum_fusion.1.rows_in) | copy-start | bytes 6291460
  119.4 10.1 %collective-permute-start.13 = (bf16[512,128]{1,0:T(8,128)(2,1)S(1)}, bf16[512,128]{1,0:T(8,128)(2,1)S(1)}, u32[]{:S(2)}, u32[]{:S(2)}) collective-permute-start(bf16[512,128]{1,0:T(8,128)(2,1)S(1)} %get-tuple-element.268), channel_id=1, source_target_pairs={{0,24},{4,28},{8,16},{12,20},{16,8},{20,12},{24,0},{28,4},{1,25},{... | collective-permute-start | bytes 393224 | tf_op jit(solution)/shard_map/ppermute | solution.py:32
  120.0 11.2 %collective-permute-start.12 = (bf16[512,128]{1,0:T(8,128)(2,1)S(1)}, bf16[512,128]{1,0:T(8,128)(2,1)S(1)}, u32[]{:S(2)}, u32[]{:S(2)}) collective-permute-start(bf16[512,128]{1,0:T(8,128)(2,1)S(1)} %get-tuple-element.269), channel_id=1, source_target_pairs={{0,16},{4,20},{8,24},{12,28},{16,0},{20,4},{24,8},{28,12},{1,17},{... | collective-permute-start | bytes 393224 | tf_op jit(solution)/shard_map/ppermute | solution.py:32
  121.5 12.2 %collective-permute-start.11 = (bf16[512,128]{1,0:T(8,128)(2,1)S(1)}, bf16[512,128]{1,0:T(8,128)(2,1)S(1)}, u32[]{:S(2)}, u32[]{:S(2)}) collective-permute-start(bf16[512,128]{1,0:T(8,128)(2,1)S(1)} %get-tuple-element.270), channel_id=1, source_target_pairs={{0,8},{4,12},{8,0},{12,4},{16,24},{20,28},{24,16},{28,20},{1,9},{5... | collective-permute-start | bytes 393224 | tf_op jit(solution)/shard_map/ppermute | solution.py:32
  137.0 16.8 %collective-permute-start.16 = (bf16[128,2048]{1,0:T(8,128)(2,1)S(1)}, bf16[128,2048]{1,0:T(8,128)(2,1)S(1)}, u32[]{:S(2)}, u32[]{:S(2)}) collective-permute-start(bf16[128,2048]{1,0:T(8,128)(2,1)S(1)} %get-tuple-element.243), channel_id=1, source_target_pairs={{0,3},{1,2},{2,1},{3,0},{4,7},{5,6},{6,5},{7,4},{8,11},{9,10},{10,... | collective-permute-start | bytes 1572872 | tf_op jit(solution)/shard_map/ppermute | solution.py:47
  140.6 43.8 %collective-permute-start.15 = (bf16[128,2048]{1,0:T(8,128)(2,1)S(1)}, bf16[128,2048]{1,0:T(8,128)(2,1)S(1)}, u32[]{:S(2)}, u32[]{:S(2)}) collective-permute-start(bf16[128,2048]{1,0:T(8,128)(2,1)S(1)} %get-tuple-element.244), channel_id=1, source_target_pairs={{0,2},{1,3},{2,0},{3,1},{4,6},{5,7},{6,4},{7,5},{8,10},{9,11},{10,... | collective-permute-start | bytes 1572872 | tf_op jit(solution)/shard_map/ppermute | solution.py:47
  140.6 43.8 %collective-permute-start.14 = (bf16[128,2048]{1,0:T(8,128)(2,1)S(1)}, bf16[128,2048]{1,0:T(8,128)(2,1)S(1)}, u32[]{:S(2)}, u32[]{:S(2)}) collective-permute-start(bf16[128,2048]{1,0:T(8,128)(2,1)S(1)} %get-tuple-element.242), channel_id=1, source_target_pairs={{0,1},{1,0},{2,3},{3,2},{4,5},{5,4},{6,7},{7,6},{8,9},{9,8},{10,11... | collective-permute-start | bytes 1572872 | tf_op jit(solution)/shard_map/ppermute | solution.py:47
  141.4 44.4 %copy-start.40 = (f32[128]{0:T(128)}, f32[128]{0:T(128)S(1)}, u32[]{:S(2)}) copy-start(f32[128]{0:T(128)S(1)} %broadcast_multiply_fusion.1) | copy-start | bytes 1540
  186.1 24.1 %collective-permute-start.17 = (bf16[128,2048]{1,0:T(8,128)(2,1)S(1)}, bf16[128,2048]{1,0:T(8,128)(2,1)}, u32[]{:S(2)}, u32[]{:S(2)}) collective-permute-start(bf16[128,2048]{1,0:T(8,128)(2,1)S(1)} %add_convert_fusion.2), channel_id=1, source_target_pairs={{0,1},{1,0},{2,3},{3,2},{4,5},{5,4},{6,7},{7,6},{8,9},{9,8},{10,11... | collective-permute-start | bytes 1572872 | tf_op jit(solution)/shard_map/ppermute | solution.py:47
  186.2 38.4 %collective-permute-start.18 = (bf16[128,2048]{1,0:T(8,128)(2,1)S(1)}, bf16[128,2048]{1,0:T(8,128)(2,1)}, u32[]{:S(2)}, u32[]{:S(2)}) collective-permute-start(bf16[128,2048]{1,0:T(8,128)(2,1)S(1)} %add_convert_fusion.2), channel_id=1, source_target_pairs={{0,2},{1,3},{2,0},{3,1},{4,6},{5,7},{6,4},{7,5},{8,10},{9,11},{10,... | collective-permute-start | bytes 1572872 | tf_op jit(solution)/shard_map/ppermute | solution.py:47
  189.2 35.4 %collective-permute-start.19 = (bf16[128,2048]{1,0:T(8,128)(2,1)S(1)}, bf16[128,2048]{1,0:T(8,128)(2,1)}, u32[]{:S(2)}, u32[]{:S(2)}) collective-permute-start(bf16[128,2048]{1,0:T(8,128)(2,1)S(1)} %add_convert_fusion.2), channel_id=1, source_target_pairs={{0,3},{1,2},{2,1},{3,0},{4,7},{5,6},{6,5},{7,4},{8,11},{9,10},{10,... | collective-permute-start | bytes 1572872 | tf_op jit(solution)/shard_map/ppermute | solution.py:47
  246.0 29.4 %collective-permute-start.20 = (bf16[128,2048]{1,0:T(8,128)(2,1)}, bf16[128,2048]{1,0:T(8,128)(2,1)}, u32[]{:S(2)}, u32[]{:S(2)}) collective-permute-start(bf16[128,2048]{1,0:T(8,128)(2,1)} %get-tuple-element.237), channel_id=1, source_target_pairs={{0,1},{1,0},{2,3},{3,2},{4,5},{5,4},{6,7},{7,6},{8,9},{9,8},{10,11... | collective-permute-start | bytes 1572872 | tf_op jit(solution)/shard_map/ppermute | solution.py:47
  255.8 38.4 %collective-permute-start.22 = (bf16[128,2048]{1,0:T(8,128)(2,1)}, bf16[128,2048]{1,0:T(8,128)(2,1)}, u32[]{:S(2)}, u32[]{:S(2)}) collective-permute-start(bf16[128,2048]{1,0:T(8,128)(2,1)} %get-tuple-element.236), channel_id=1, source_target_pairs={{0,3},{1,2},{2,1},{3,0},{4,7},{5,6},{6,5},{7,4},{8,11},{9,10},{10,... | collective-permute-start | bytes 1572872 | tf_op jit(solution)/shard_map/ppermute | solution.py:47
  257.2 44.0 %collective-permute-start.21 = (bf16[128,2048]{1,0:T(8,128)(2,1)}, bf16[128,2048]{1,0:T(8,128)(2,1)}, u32[]{:S(2)}, u32[]{:S(2)}) collective-permute-start(bf16[128,2048]{1,0:T(8,128)(2,1)} %get-tuple-element.235), channel_id=1, source_target_pairs={{0,2},{1,3},{2,0},{3,1},{4,6},{5,7},{6,4},{7,5},{8,10},{9,11},{10,... | collective-permute-start | bytes 1572872 | tf_op jit(solution)/shard_map/ppermute | solution.py:47
  294.2 227.4 %reduce-scatter.5.cloned.1.call-start = ((), (), s32[]{:S(2)}) async-start(), calls=%async_computation.5 | async-start | bytes 2359296 | tf_op jit(solution)/shard_map/reduce_scatter | solution.py:693
  306.2 16.7 %collective-permute-start.25 = (bf16[128,2048]{1,0:T(8,128)(2,1)S(1)}, bf16[128,2048]{1,0:T(8,128)(2,1)S(1)}, u32[]{:S(2)}, u32[]{:S(2)}) collective-permute-start(bf16[128,2048]{1,0:T(8,128)(2,1)S(1)} %get-tuple-element.211), channel_id=1, source_target_pairs={{0,3},{1,2},{2,1},{3,0},{4,7},{5,6},{6,5},{7,4},{8,11},{9,10},{10,... | collective-permute-start | bytes 1572872 | tf_op jit(solution)/shard_map/ppermute | solution.py:47
  307.4 40.9 %collective-permute-start.24 = (bf16[128,2048]{1,0:T(8,128)(2,1)S(1)}, bf16[128,2048]{1,0:T(8,128)(2,1)S(1)}, u32[]{:S(2)}, u32[]{:S(2)}) collective-permute-start(bf16[128,2048]{1,0:T(8,128)(2,1)S(1)} %get-tuple-element.211), channel_id=1, source_target_pairs={{0,2},{1,3},{2,0},{3,1},{4,6},{5,7},{6,4},{7,5},{8,10},{9,11},{10,... | collective-permute-start | bytes 1572872 | tf_op jit(solution)/shard_map/ppermute | solution.py:47
  307.4 40.9 %collective-permute-start.23 = (bf16[128,2048]{1,0:T(8,128)(2,1)S(1)}, bf16[128,2048]{1,0:T(8,128)(2,1)S(1)}, u32[]{:S(2)}, u32[]{:S(2)}) collective-permute-start(bf16[128,2048]{1,0:T(8,128)(2,1)S(1)} %get-tuple-element.211), channel_id=1, source_target_pairs={{0,1},{1,0},{2,3},{3,2},{4,5},{5,4},{6,7},{7,6},{8,9},{9,8},{10,11... | collective-permute-start | bytes 1572872 | tf_op jit(solution)/shard_map/ppermute | solution.py:47
  349.7 44.6 %collective-permute-start.31 = (bf16[128,2048]{1,0:T(8,128)(2,1)}, bf16[128,2048]{1,0:T(8,128)(2,1)S(1)}, u32[]{:S(2)}, u32[]{:S(2)}) collective-permute-start(bf16[128,2048]{1,0:T(8,128)(2,1)} %get-tuple-element.233), channel_id=1, source_target_pairs={{0,3},{1,2},{2,1},{3,0},{4,7},{5,6},{6,5},{7,4},{8,11},{9,10},{10,... | collective-permute-start | bytes 1572872 | tf_op jit(solution)/shard_map/ppermute | solution.py:47
  352.7 41.7 %collective-permute-start.30 = (bf16[128,2048]{1,0:T(8,128)(2,1)}, bf16[128,2048]{1,0:T(8,128)(2,1)}, u32[]{:S(2)}, u32[]{:S(2)}) collective-permute-start(bf16[128,2048]{1,0:T(8,128)(2,1)} %get-tuple-element.234), channel_id=1, source_target_pairs={{0,2},{1,3},{2,0},{3,1},{4,6},{5,7},{6,4},{7,5},{8,10},{9,11},{10,... | collective-permute-start | bytes 1572872 | tf_op jit(solution)/shard_map/ppermute | solution.py:47
  352.7 41.7 %collective-permute-start.29 = (bf16[128,2048]{1,0:T(8,128)(2,1)}, bf16[128,2048]{1,0:T(8,128)(2,1)}, u32[]{:S(2)}, u32[]{:S(2)}) collective-permute-start(bf16[128,2048]{1,0:T(8,128)(2,1)} %get-tuple-element.232), channel_id=1, source_target_pairs={{0,1},{1,0},{2,3},{3,2},{4,5},{5,4},{6,7},{7,6},{8,9},{9,8},{10,11... | collective-permute-start | bytes 1572872 | tf_op jit(solution)/shard_map/ppermute | solution.py:47
  355.5 9.2 %collective-permute-start.28 = (bf16[512,128]{1,0:T(8,128)(2,1)S(1)}, bf16[512,128]{1,0:T(8,128)(2,1)S(1)}, u32[]{:S(2)}, u32[]{:S(2)}) collective-permute-start(bf16[512,128]{1,0:T(8,128)(2,1)S(1)} %get-tuple-element.260), channel_id=1, source_target_pairs={{0,24},{4,28},{8,16},{12,20},{16,8},{20,12},{24,0},{28,4},{1,25},{... | collective-permute-start | bytes 393224 | tf_op jit(solution)/shard_map/ppermute | solution.py:32
  357.1 9.0 %collective-permute-start.27 = (bf16[512,128]{1,0:T(8,128)(2,1)S(1)}, bf16[512,128]{1,0:T(8,128)(2,1)S(1)}, u32[]{:S(2)}, u32[]{:S(2)}) collective-permute-start(bf16[512,128]{1,0:T(8,128)(2,1)S(1)} %get-tuple-element.261), channel_id=1, source_target_pairs={{0,16},{4,20},{8,24},{12,28},{16,0},{20,4},{24,8},{28,12},{1,17},{... | collective-permute-start | bytes 393224 | tf_op jit(solution)/shard_map/ppermute | solution.py:32
  364.7 7.7 %collective-permute-start.26 = (bf16[512,128]{1,0:T(8,128)(2,1)S(1)}, bf16[512,128]{1,0:T(8,128)(2,1)S(1)}, u32[]{:S(2)}, u32[]{:S(2)}) collective-permute-start(bf16[512,128]{1,0:T(8,128)(2,1)S(1)} %get-tuple-element.262), channel_id=1, source_target_pairs={{0,8},{4,12},{8,0},{12,4},{16,24},{20,28},{24,16},{28,20},{1,9},{5... | collective-permute-start | bytes 393224 | tf_op jit(solution)/shard_map/ppermute | solution.py:32
  396.7 2.9 collective-permute-start.35
  404.0 17.2 %collective-permute-start.38 = (bf16[512,384]{1,0:T(8,128)(2,1)}, bf16[512,384]{1,0:T(8,128)(2,1)S(1)}, u32[]{:S(2)}, u32[]{:S(2)}) collective-permute-start(bf16[512,384]{1,0:T(8,128)(2,1)} %get-tuple-element.155), channel_id=1, source_target_pairs={{0,24},{4,28},{8,16},{12,20},{16,8},{20,12},{24,0},{28,4},{1,25},{... | collective-permute-start | bytes 1179656 | tf_op jit(solution)/shard_map/ppermute | solution.py:32
  406.0 22.5 %collective-permute-start.37 = (bf16[512,384]{1,0:T(8,128)(2,1)}, bf16[512,384]{1,0:T(8,128)(2,1)S(1)}, u32[]{:S(2)}, u32[]{:S(2)}) collective-permute-start(bf16[512,384]{1,0:T(8,128)(2,1)} %get-tuple-element.154), channel_id=1, source_target_pairs={{0,16},{4,20},{8,24},{12,28},{16,0},{20,4},{24,8},{28,12},{1,17},{... | collective-permute-start | bytes 1179656 | tf_op jit(solution)/shard_map/ppermute | solution.py:32
  406.0 22.5 %collective-permute-start.36 = (bf16[512,384]{1,0:T(8,128)(2,1)}, bf16[512,384]{1,0:T(8,128)(2,1)S(1)}, u32[]{:S(2)}, u32[]{:S(2)}) collective-permute-start(bf16[512,384]{1,0:T(8,128)(2,1)} %get-tuple-element.153), channel_id=1, source_target_pairs={{0,8},{4,12},{8,0},{12,4},{16,24},{20,28},{24,16},{28,20},{1,9},{5... | collective-permute-start | bytes 1179656 | tf_op jit(solution)/shard_map/ppermute | solution.py:32
  407.5 39.6 %collective-permute-start.32 = (bf16[128,2048]{1,0:T(8,128)(2,1)S(1)}, bf16[128,2048]{1,0:T(8,128)(2,1)S(1)}, u32[]{:S(2)}, u32[]{:S(2)}) collective-permute-start(bf16[128,2048]{1,0:T(8,128)(2,1)S(1)} %copy-done.21), channel_id=1, source_target_pairs={{0,1},{1,0},{2,3},{3,2},{4,5},{5,4},{6,7},{7,6},{8,9},{9,8},{10,11... | collective-permute-start | bytes 1572872 | tf_op jit(solution)/shard_map/ppermute | solution.py:47
  408.0 39.1 %collective-permute-start.33 = (bf16[128,2048]{1,0:T(8,128)(2,1)S(1)}, bf16[128,2048]{1,0:T(8,128)(2,1)S(1)}, u32[]{:S(2)}, u32[]{:S(2)}) collective-permute-start(bf16[128,2048]{1,0:T(8,128)(2,1)S(1)} %copy-done.21), channel_id=1, source_target_pairs={{0,2},{1,3},{2,0},{3,1},{4,6},{5,7},{6,4},{7,5},{8,10},{9,11},{10,... | collective-permute-start | bytes 1572872 | tf_op jit(solution)/shard_map/ppermute | solution.py:47
  421.3 25.9 %collective-permute-start.34 = (bf16[128,2048]{1,0:T(8,128)(2,1)S(1)}, bf16[128,2048]{1,0:T(8,128)(2,1)}, u32[]{:S(2)}, u32[]{:S(2)}) collective-permute-start(bf16[128,2048]{1,0:T(8,128)(2,1)S(1)} %copy-done.21), channel_id=1, source_target_pairs={{0,3},{1,2},{2,1},{3,0},{4,7},{5,6},{6,5},{7,4},{8,11},{9,10},{10,... | collective-permute-start | bytes 1572872 | tf_op jit(solution)/shard_map/ppermute | solution.py:47
  447.2 6.1 %collective-permute-start.39 = (bf16[1024,1536]{1,0:T(8,128)(2,1)}, bf16[1024,1536]{1,0:T(8,128)(2,1)}, u32[]{:S(2)}, u32[]{:S(2)}) collective-permute-start(bf16[1024,1536]{1,0:T(8,128)(2,1)} %weight_grad.2), channel_id=1, source_target_pairs={{0,4},{4,0},{8,12},{12,8},{16,20},{20,16},{24,28},{28,24},{1,5},{5... | collective-permute-start | bytes 9437192 | tf_op jit(solution)/shard_map/ppermute | solution.py:32
  459.9 16.8 %collective-permute-start.42 = (bf16[128,2048]{1,0:T(8,128)(2,1)S(1)}, bf16[128,2048]{1,0:T(8,128)(2,1)S(1)}, u32[]{:S(2)}, u32[]{:S(2)}) collective-permute-start(bf16[128,2048]{1,0:T(8,128)(2,1)S(1)} %get-tuple-element.226), channel_id=1, source_target_pairs={{0,3},{1,2},{2,1},{3,0},{4,7},{5,6},{6,5},{7,4},{8,11},{9,10},{10,... | collective-permute-start | bytes 1572872 | tf_op jit(solution)/shard_map/ppermute | solution.py:47
  463.3 46.2 %collective-permute-start.41 = (bf16[128,2048]{1,0:T(8,128)(2,1)S(1)}, bf16[128,2048]{1,0:T(8,128)(2,1)S(1)}, u32[]{:S(2)}, u32[]{:S(2)}) collective-permute-start(bf16[128,2048]{1,0:T(8,128)(2,1)S(1)} %get-tuple-element.227), channel_id=1, source_target_pairs={{0,2},{1,3},{2,0},{3,1},{4,6},{5,7},{6,4},{7,5},{8,10},{9,11},{10,... | collective-permute-start | bytes 1572872 | tf_op jit(solution)/shard_map/ppermute | solution.py:47
  471.2 38.2 %collective-permute-start.40 = (bf16[128,2048]{1,0:T(8,128)(2,1)S(1)}, bf16[128,2048]{1,0:T(8,128)(2,1)S(1)}, u32[]{:S(2)}, u32[]{:S(2)}) collective-permute-start(bf16[128,2048]{1,0:T(8,128)(2,1)S(1)} %get-tuple-element.225), channel_id=1, source_target_pairs={{0,1},{1,0},{2,3},{3,2},{4,5},{5,4},{6,7},{7,6},{8,9},{9,8},{10,11... | collective-permute-start | bytes 1572872 | tf_op jit(solution)/shard_map/ppermute | solution.py:47
  471.4 38.4 %collective-permute-start.45 = (bf16[256,1536]{1,0:T(8,128)(2,1)S(1)}, bf16[256,1536]{1,0:T(8,128)(2,1)S(1)}, u32[]{:S(2)}, u32[]{:S(2)}) collective-permute-start(bf16[256,1536]{1,0:T(8,128)(2,1)S(1)} %get-tuple-element.218), channel_id=1, source_target_pairs={{0,24},{4,28},{8,16},{12,20},{16,8},{20,12},{24,0},{28,4},{1,25},{... | collective-permute-start | bytes 2359304 | tf_op jit(solution)/shard_map/ppermute | solution.py:32
  473.0 43.7 %collective-permute-start.44 = (bf16[256,1536]{1,0:T(8,128)(2,1)S(1)}, bf16[256,1536]{1,0:T(8,128)(2,1)S(1)}, u32[]{:S(2)}, u32[]{:S(2)}) collective-permute-start(bf16[256,1536]{1,0:T(8,128)(2,1)S(1)} %get-tuple-element.219), channel_id=1, source_target_pairs={{0,16},{4,20},{8,24},{12,28},{16,0},{20,4},{24,8},{28,12},{1,17},{... | collective-permute-start | bytes 2359304 | tf_op jit(solution)/shard_map/ppermute | solution.py:32
  476.6 40.4 %collective-permute-start.43 = (bf16[256,1536]{1,0:T(8,128)(2,1)S(1)}, bf16[256,1536]{1,0:T(8,128)(2,1)S(1)}, u32[]{:S(2)}, u32[]{:S(2)}) collective-permute-start(bf16[256,1536]{1,0:T(8,128)(2,1)S(1)} %get-tuple-element.217), channel_id=1, source_target_pairs={{0,8},{4,12},{8,0},{12,4},{16,24},{20,28},{24,16},{28,20},{1,9},{5... | collective-permute-start | bytes 2359304 | tf_op jit(solution)/shard_map/ppermute | solution.py:32
  529.5 13.3 %collective-permute-start.50 = (f32[72,128]{1,0:T(8,128)S(1)}, f32[72,128]{1,0:T(8,128)S(1)}, u32[]{:S(2)}, u32[]{:S(2)}) collective-permute-start(f32[72,128]{1,0:T(8,128)S(1)} %concatenate.144), channel_id=1, source_target_pairs={{0,2},{1,3},{2,0},{3,1},{4,6},{5,7},{6,4},{7,5},{8,10},{9,11},{10,... | collective-permute-start | bytes 110600 | tf_op jit(solution)/shard_map/ppermute | solution.py:47
  535.6 7.2 %collective-permute-start.51 = (f32[72,128]{1,0:T(8,128)S(1)}, f32[72,128]{1,0:T(8,128)S(1)}, u32[]{:S(2)}, u32[]{:S(2)}) collective-permute-start(f32[72,128]{1,0:T(8,128)S(1)} %concatenate.144), channel_id=1, source_target_pairs={{0,3},{1,2},{2,1},{3,0},{4,7},{5,6},{6,5},{7,4},{8,11},{9,10},{10,... | collective-permute-start | bytes 110600 | tf_op jit(solution)/shard_map/ppermute | solution.py:47
  536.0 6.8 %collective-permute-start.49 = (f32[72,128]{1,0:T(8,128)S(1)}, f32[72,128]{1,0:T(8,128)S(1)}, u32[]{:S(2)}, u32[]{:S(2)}) collective-permute-start(f32[72,128]{1,0:T(8,128)S(1)} %concatenate.144), channel_id=1, source_target_pairs={{0,1},{1,0},{2,3},{3,2},{4,5},{5,4},{6,7},{7,6},{8,9},{9,8},{10,11... | collective-permute-start | bytes 110600 | tf_op jit(solution)/shard_map/ppermute | solution.py:47
  539.0 32.7 %collective-permute-start.48 = (bf16[128,2048]{1,0:T(8,128)(2,1)S(1)}, bf16[128,2048]{1,0:T(8,128)(2,1)S(1)}, u32[]{:S(2)}, u32[]{:S(2)}) collective-permute-start(bf16[128,2048]{1,0:T(8,128)(2,1)S(1)} %copy-done.24), channel_id=1, source_target_pairs={{0,3},{1,2},{2,1},{3,0},{4,7},{5,6},{6,5},{7,4},{8,11},{9,10},{10,... | collective-permute-start | bytes 1572872 | tf_op jit(solution)/shard_map/ppermute | solution.py:47
  542.2 44.7 %collective-permute-start.47 = (bf16[128,2048]{1,0:T(8,128)(2,1)S(1)}, bf16[128,2048]{1,0:T(8,128)(2,1)S(1)}, u32[]{:S(2)}, u32[]{:S(2)}) collective-permute-start(bf16[128,2048]{1,0:T(8,128)(2,1)S(1)} %copy-done.24), channel_id=1, source_target_pairs={{0,2},{1,3},{2,0},{3,1},{4,6},{5,7},{6,4},{7,5},{8,10},{9,11},{10,... | collective-permute-start | bytes 1572872 | tf_op jit(solution)/shard_map/ppermute | solution.py:47
  542.8 4.0 collective-permute-start.53
  543.6 4.9 collective-permute-start.54
  545.8 4.0 collective-permute-start.52
  546.8 40.1 %collective-permute-start.46 = (bf16[128,2048]{1,0:T(8,128)(2,1)S(1)}, bf16[128,2048]{1,0:T(8,128)(2,1)S(1)}, u32[]{:S(2)}, u32[]{:S(2)}) collective-permute-start(bf16[128,2048]{1,0:T(8,128)(2,1)S(1)} %copy-done.24), channel_id=1, source_target_pairs={{0,1},{1,0},{2,3},{3,2},{4,5},{5,4},{6,7},{7,6},{8,9},{9,8},{10,11... | collective-permute-start | bytes 1572872 | tf_op jit(solution)/shard_map/ppermute | solution.py:47
  549.8 1.3 collective-permute-start.55
  553.6 17.3 %copy-start.37 = (f32[2,256]{1,0:T(2,128)S(1)}, f32[2,256]{1,0:T(2,128)}, u32[]{:S(2)}) copy-start(f32[2,256]{1,0:T(2,128)} %param.29) | copy-start | bytes 6148
  (51 other events, 385.9 us)
Sparse Core Ops, SparseCore 0:
  56.2 36.6 all-gather.2
  95.4 102.7 all-gather.4
  294.3 130.5 reduce-scatter.2
  449.3 68.2 reduce-scatter.4

commit v3 on v2

v3 whole, which is shorter than its diff:
```python
import functools
import math

import jax
import jax.numpy as jnp
from jax import lax
from jax.experimental import pallas as pl
from jax.experimental.pallas import tpu as pltpu
from jax.sharding import PartitionSpec as P

HEAD = 128
BLOCK = 256
Q_TILE = 512

eps_norm = 1e-05
neg_big = -1e30
beta_one = 0.9
beta_two = 0.95
adam_eps = 1e-08
learn_rate = 0.001
decay_rate = 0.1
step_count = 10.0
log2_e = math.log2(math.e)
inv_root_two = 1.0 / math.sqrt(2.0)
inv_root_two_pi = 1.0 / math.sqrt(2.0 * math.pi)
bf16 = jnp.bfloat16
f32 = jnp.float32


def ctx_xor(value, mask):
    count = lax.axis_size("ctx")
    return lax.ppermute(value, "ctx", [(place, place ^ mask) for place in range(count)])


def ctx_gather(own, early):
    blocks = [None] * lax.axis_size("ctx")
    for mask in range(0, len(blocks), 2):
        blocks[mask] = own if mask == 0 else ctx_xor(own, mask)
    blocks[2], early = lax.optimization_barrier((blocks[2], early))
    for mask in range(0, len(blocks), 2):
        blocks[mask + 1] = ctx_xor(blocks[mask], 1)
    return (blocks, early)


def tp_xor(value, mask):
    count = lax.axis_size("tp")
    return lax.ppermute(value, "tp", [(place, place ^ mask) for place in range(count)])


def tp_gather(own):
    return tp_gather_last(tp_gather_first(own))


def tp_gather_first(own):
    count = lax.axis_size("tp")
    return [own] + [tp_xor(own, s) for s in range(1, 3 if count == 4 else count)]


def tp_gather_last(parts):
    return parts + [tp_xor(parts[2], 1)] if lax.axis_size("tp") == 4 else parts


def tp_send(partial, behind=None):
    count = lax.axis_size("tp")
    rows = partial.shape[0] // count
    pieces = [partial[s * rows : (s + 1) * rows] for s in range(count)]
    if count != 4:
        return [pieces[0]] + [tp_xor(pieces[s], s) for s in range(1, count)]
    passed = tp_xor(pieces[3], 1)
    passed, near, _ = lax.optimization_barrier((passed, pieces[1], behind))
    joined = (pieces[2].astype(f32) + passed.astype(f32)).astype(bf16)
    return [pieces[0], tp_xor(near, 1), tp_xor(joined, 2)]


def tp_total(parts):
    total = parts[0].astype(f32)
    for piece in parts[1:]:
        total = total + piece.astype(f32)
    return total


def tp_scatter(partial):
    return tp_total(tp_send(partial))


def slots_to_rows(parts, tp_place):
    return in_slots(jnp.concatenate(parts, axis=0), tp_place, len(parts))


def in_slots(value, tp_place, count):
    rows = value.shape[0] // count
    order = [jnp.bitwise_xor(tp_place, s) * rows for s in range(count)]
    return jnp.concatenate([lax.dynamic_slice_in_dim(value, o, rows, 0) for o in order], axis=0)


def sum_over_all(value, later):
    if lax.axis_size("tp") == 4:
        one, two, three = (tp_xor(value, 1), tp_xor(value, 2), tp_xor(value, 3))
        value = (value + one) + (two + three)
    else:
        mask = 1
        while mask < lax.axis_size("tp"):
            value = value + tp_xor(value, mask)
            mask *= 2
    value, later = lax.optimization_barrier((value, later))
    mask = lax.axis_size("ctx") // 2
    while mask:
        value = value + ctx_xor(value, mask)
        mask //= 2
    return (value, later)


def scores_of(keys, query, where, lo, hi, scale):
    raw = lax.dot_general(keys, query, (((1,), (1,)), ((), ())), preferred_element_type=f32) * (scale * log2_e)
    return jnp.where((where >= lo) & (where < hi), raw, neg_big)


def key_halves(rows, place, chip):
    top = pl.multiple_of(jnp.bitwise_xor(chip, place[0] // 2) * rows, rows)
    core = lax.rem(place[0], 2)
    return (top, (2 * chip + core) * rows, (2 * chip + 1 - core) * rows)


def fill_positions(rows, chunks, place, where):
    where[...] = jnp.bitwise_xor(lax.broadcasted_iota(jnp.int32, where.shape, 0), place[1] * (rows // chunks))


def forward_kernel(rows, chunks, left, scale, place, tiles, span, own, *refs):
    even = own if left else refs[0]
    odd, out, out_t, lse_out, vt_even, vt_odd, where = refs[-7:]
    fill_positions(rows, chunks, place, where)
    for slot in range(odd.shape[0] // rows):
        cut = slice(slot * rows, (slot + 1) * rows)
        vt_even[:, cut] = even[cut, left + HEAD : left + 2 * HEAD].T
        vt_odd[:, cut] = odd[cut, HEAD:].T

    @pl.loop(0, own.shape[0] // Q_TILE)
    def _(tile):
        cut = pl.ds(pl.multiple_of(tile * Q_TILE, Q_TILE), Q_TILE)
        query = own[cut, :HEAD]
        lo, hi = span[0:1, cut], span[1:2, cut]

        def step(chip, carry):
            top, total, acc = carry
            at, first, second = key_halves(rows, place, chip)
            here = pl.ds(at, rows)
            one = scores_of(even[here, left : left + HEAD], query, where[...], lo - first, hi - first, scale)
            two = scores_of(odd[here, :HEAD], query, where[...], lo - second, hi - second, scale)
            new_top = jnp.maximum(
                top, jnp.maximum(jnp.max(one, axis=0, keepdims=True), jnp.max(two, axis=0, keepdims=True))
            )
            fade = jnp.exp2(top - new_top)
            one, two = jnp.exp2(one - new_top), jnp.exp2(two - new_top)
            total = total * fade + jnp.sum(one, axis=0, keepdims=True) + jnp.sum(two, axis=0, keepdims=True)
            acc = (
                acc * fade
                + jnp.dot(vt_even[:, here], one.astype(bf16), preferred_element_type=f32)
                + jnp.dot(vt_odd[:, here], two.astype(bf16), preferred_element_type=f32)
            )
            return (new_top, total, acc)

        start = (
            jnp.full((1, Q_TILE), neg_big, f32),
            jnp.zeros((1, Q_TILE), f32),
            jnp.zeros((HEAD, Q_TILE), f32),
        )
        top, total, acc = lax.fori_loop(tiles[0, tile], tiles[1, tile], step, start)
        result = acc / total
        out_t[:, cut] = result
        out[cut, :] = result.T.astype(bf16)
        lse_out[:, cut] = top + jnp.log2(total)


def backward_kernel(rows, chunks, left, scale, place, tiles, span, own, grad_out, out_t, lse_in, *refs):
    even = own if left else refs[0]
    odd, dq_out, dkv_even, dkv_odd, kt_even, kt_odd, d_odd, where = refs[-8:]
    fill_positions(rows, chunks, place, where)
    for slot in range(odd.shape[0] // rows):
        cut = slice(slot * rows, (slot + 1) * rows)
        kt_even[:, cut] = even[cut, left : left + HEAD].T
        kt_odd[:, cut] = odd[cut, :HEAD].T
    dkv_even[...] = jnp.zeros_like(dkv_even)
    d_odd[...] = jnp.zeros_like(d_odd)

    @pl.loop(0, own.shape[0] // Q_TILE)
    def _(tile):
        cut = pl.ds(pl.multiple_of(tile * Q_TILE, Q_TILE), Q_TILE)
        query, grad = own[cut, :HEAD], grad_out[cut, :]
        lo, hi, lse = span[0:1, cut], span[1:2, cut], lse_in[:, cut]
        inner = jnp.sum(grad.astype(f32).T * out_t[:, cut], axis=0, keepdims=True)

        def half(keys, values, keys_t, total, here, first, dq_t):
            scores = scores_of(keys, query, where[...], lo - first, hi - first, scale)
            prob = jnp.exp2(scores - lse)
            grad_prob = lax.dot_general(
                values, grad, (((1,), (1,)), ((), ())), preferred_element_type=f32
            )
            grad_scores = (prob * (grad_prob - inner)).astype(bf16)
            total[here, HEAD:] += jnp.dot(prob.astype(bf16), grad, preferred_element_type=f32)
            total[here, :HEAD] += jnp.dot(grad_scores, query, preferred_element_type=f32)
            return dq_t + jnp.dot(keys_t, grad_scores, preferred_element_type=f32)

        def step(chip, dq_t):
            at, first, second = key_halves(rows, place, chip)
            here = pl.ds(at, rows)
            keys, values = even[here, left : left + HEAD], even[here, left + HEAD : left + 2 * HEAD]
            dq_t = half(keys, values, kt_even[:, here], dkv_even, here, first, dq_t)
            return half(odd[here, :HEAD], odd[here, HEAD:], kt_odd[:, here], d_odd, here, second, dq_t)

        dq_t = lax.fori_loop(
            tiles[0, tile], tiles[1, tile], step, jnp.zeros((HEAD, Q_TILE), f32)
        )
        dq_out[cut, :] = (dq_t * scale).T.astype(bf16)

    dkv_even[:, :HEAD] = dkv_even[:, :HEAD] * scale
    dkv_odd[:, :HEAD] = (d_odd[:, :HEAD] * scale).astype(bf16)
    dkv_odd[:, HEAD:] = d_odd[:, HEAD:].astype(bf16)


LARGE = pl.CostEstimate(flops=145_000_000_000, bytes_accessed=145_000_000, transcendentals=0)
LITTLE = pl.CostEstimate(flops=1, bytes_accessed=1, transcendentals=0)


def in_vmem():
    return pl.BlockSpec(memory_space=pltpu.VMEM)


def in_smem():
    return pl.BlockSpec(memory_space=pltpu.SMEM)


def attention_forward(place, tiles, span, own, even, odd, rows, chunks, scale):
    queries, keys = own.shape[0], odd.shape[0]
    arrays = (own, odd) if even is None else (own, even, odd)
    return pl.pallas_call(
        functools.partial(forward_kernel, rows, chunks, HEAD if even is None else 0, scale),
        out_shape=(
            jax.ShapeDtypeStruct((queries, HEAD), bf16),
            jax.ShapeDtypeStruct((HEAD, queries), f32),
            jax.ShapeDtypeStruct((1, queries), f32),
        ),
        in_specs=[in_smem(), in_smem()] + [in_vmem()] * (1 + len(arrays)),
        out_specs=(in_vmem(), in_vmem(), in_vmem()),
        scratch_shapes=[
            pltpu.VMEM((HEAD, keys), bf16),
            pltpu.VMEM((HEAD, keys), bf16),
            pltpu.VMEM((rows, Q_TILE), jnp.int32),
        ],
        compiler_params=pltpu.CompilerParams(vmem_limit_bytes=58 << 20),
        cost_estimate=LITTLE,
        name="attention_forward",
    )(place, tiles, span, *arrays)


def attention_backward(place, tiles, span, own, grad, out_t, lse, even, odd, rows, chunks, scale):
    queries, keys = own.shape[0], odd.shape[0]
    arrays = (odd,) if even is None else (even, odd)
    return pl.pallas_call(
        functools.partial(backward_kernel, rows, chunks, HEAD if even is None else 0, scale),
        out_shape=(
            jax.ShapeDtypeStruct((queries, HEAD), bf16),
            jax.ShapeDtypeStruct((keys, 2 * HEAD), f32),
            jax.ShapeDtypeStruct((keys, 2 * HEAD), bf16),
        ),
        in_specs=[in_smem(), in_smem()] + [in_vmem()] * (5 + len(arrays)),
        out_specs=(in_vmem(),) * 3,
        scratch_shapes=[
            pltpu.VMEM((HEAD, keys), bf16),
            pltpu.VMEM((HEAD, keys), bf16),
            pltpu.VMEM((keys, 2 * HEAD), f32),
            pltpu.VMEM((rows, Q_TILE), jnp.int32),
        ],
        compiler_params=pltpu.CompilerParams(vmem_limit_bytes=58 << 20),
        cost_estimate=LITTLE,
        name="attention_backward",
    )(place, tiles, span, own, grad, out_t, lse, *arrays)


def merge_kernel(grad_q, grad_kv, *refs):
    got, outs = refs[0], refs[1:]
    rows = outs[0].shape[0]
    for slot, out in enumerate(outs):
        cut = slice(slot * rows, (slot + 1) * rows)
        out[:, :HEAD] = grad_q[cut, :]
        out[:, HEAD:] = (grad_kv[cut, :] + got[cut, :].astype(f32)).astype(bf16)


def merge(grad_q, grad_kv, got, count):
    rows = grad_q.shape[0] // count
    return pl.pallas_call(
        merge_kernel,
        out_shape=(jax.ShapeDtypeStruct((rows, 3 * HEAD), bf16),) * count,
        in_specs=[in_vmem()] * 3,
        out_specs=(in_vmem(),) * count,
        compiler_params=pltpu.CompilerParams(vmem_limit_bytes=58 << 20),
        cost_estimate=LARGE,
        name="merge",
    )(grad_q, grad_kv, got)


def lanes_of(me, mask, depth):
    at = jnp.bitwise_xor(me, mask) * depth
    return pl.ds(pl.multiple_of(at, depth), depth)


def project_kernel(rows, heads, depth, place, rows_in, *refs):
    blocks, outs, (a1, small, weights, result) = refs[: -4 - heads], refs[-4 - heads : -4], refs[-4:]
    me = place[0]
    my_head = lax.rem(me // 2, heads)
    if depth % HEAD:
        small[...] = blocks[-1][...]
        blocks = blocks[:-1]
    for mask, block in enumerate(blocks):
        at = lanes_of(me, mask, depth)
        weights[at, :] = block[:depth, :]
        if depth % HEAD == 0:
            small[:, at] = block[depth : depth + 8, :depth].astype(f32)
    part = rows // 4

    @pl.loop(0, 4)
    def _(quarter):
        cut = pl.ds(pl.multiple_of(quarter * part, part), part)
        normed, _ = norm_parts(rows_in[cut, :].astype(f32))
        a1[cut, :] = (normed * small[0:1, :] + small[2:3, :]).astype(bf16)

    width = heads * HEAD

    @pl.loop(0, 3)
    def _(j):
        cut = pl.ds(pl.multiple_of(j * width, width), width)
        result[:, cut] = jnp.dot(a1[...], weights[:, cut], preferred_element_type=f32).astype(bf16)

    for s in range(heads):
        at = jnp.bitwise_xor(my_head, s) * HEAD
        for j in range(3):
            here = pl.ds(pl.multiple_of(j * width + at, HEAD), HEAD)
            outs[s][:, j * HEAD : (j + 1) * HEAD] = result[:, here]


def project(place, rows_in, blocks, heads, depth):
    rows, width = rows_in.shape
    cols = 3 * heads * HEAD
    if depth % HEAD:
        known = jnp.stack([block[depth : depth + 8, :depth] for block in blocks])
        order = jnp.bitwise_xor(place[0], jnp.arange(len(blocks), dtype=jnp.int32))
        known = jnp.take(known, order, axis=0).transpose(1, 0, 2).reshape(8, width)
        blocks = [*blocks, known.astype(f32)]
    return pl.pallas_call(
        functools.partial(project_kernel, rows, heads, depth),
        out_shape=(
            *[jax.ShapeDtypeStruct((rows, 3 * HEAD), bf16)] * heads,
            jax.ShapeDtypeStruct((rows, width), bf16),
            jax.ShapeDtypeStruct((8, width), f32),
        ),
        in_specs=[in_smem()] + [in_vmem()] * (1 + len(blocks)),
        out_specs=(in_vmem(),) * (heads + 2),
        scratch_shapes=[pltpu.VMEM((width, cols), bf16), pltpu.VMEM((rows, cols), bf16)],
        compiler_params=pltpu.CompilerParams(vmem_limit_bytes=58 << 20),
        cost_estimate=LITTLE,
        name="project",
    )(place, rows_in, *blocks)


def weight_grad_kernel(flip, depth, place, *refs):
    me = place[0]
    pairs, refs = (refs[0:2], refs[2:4]), refs[4:]
    add, outs, whole = (refs[0], refs[1:-1], refs[-1]) if not flip else (None, refs[:-1], refs[-1])
    count = pairs[0][0].shape[1] // depth // 2
    if depth % HEAD:
        left = 0
        for rows_in, grads in pairs:
            cols = slice(left, left + grads.shape[1])
            whole[:, cols] = lax.dot_general(
                rows_in[...], grads[...], (((0,), (0,)), ((), ())), preferred_element_type=f32
            )
            left = cols.stop
    else:

        @pl.loop(0, count)
        def _(slot):
            at = lanes_of(me, 2 * slot + flip, depth)
            here = pl.ds(pl.multiple_of(slot * depth, depth), depth)
            left = 0
            for rows_in, grads in pairs:
                cols = slice(left, left + grads.shape[1])
                whole[here, cols] = lax.dot_general(
                    rows_in[:, at], grads[...], (((0,), (0,)), ((), ())), preferred_element_type=f32
                )
                left = cols.stop

    for slot in range(count):
        here = slice(slot * depth, (slot + 1) * depth)
        block = whole[lanes_of(me, 2 * slot + flip, depth), :] if depth % HEAD else whole[here, :]
        if flip:
            outs[0][here, :] = block.astype(bf16)
        else:
            outs[slot][...] = (block + add[here, :].astype(f32)).astype(bf16)


def weight_grad(place, pairs, depth, add=None):
    width, cols = pairs[0][0].shape[1], sum(grads.shape[1] for _, grads in pairs)
    count = width // depth // 2
    flip, extra = (1, []) if add is None else (0, [add])
    lines = [count * depth] if add is None else [depth] * count
    results = pl.pallas_call(
        functools.partial(weight_grad_kernel, flip, depth),
        out_shape=tuple(jax.ShapeDtypeStruct((n, cols), bf16) for n in lines),
        in_specs=[in_smem()] + [in_vmem()] * (4 + len(extra)),
        out_specs=(in_vmem(),) * len(lines),
        scratch_shapes=[pltpu.VMEM((width if depth % HEAD else count * depth, cols), f32)],
        compiler_params=pltpu.CompilerParams(vmem_limit_bytes=58 << 20),
        cost_estimate=LITTLE,
        name="weight_grad",
    )(place, *pairs[0], *pairs[1], *extra)
    return results if add is not None else results[0]


def input_grad_kernel(depth, place, grads, *refs):
    me = place[0]
    blocks, out, weights = refs[:-2], refs[-2], refs[-1]
    for mask, block in enumerate(blocks):
        weights[lanes_of(me, mask, depth), :] = block[:depth, :]
    step = 512

    @pl.loop(0, out.shape[1] // step)
    def _(part):
        here = pl.ds(pl.multiple_of(part * step, step), step)
        out[:, here] = lax.dot_general(
            grads[...], weights[here, :], (((1,), (1,)), ((), ())), preferred_element_type=f32
        ).astype(bf16)


def input_grad(place, grads, blocks, depth):
    return pl.pallas_call(
        functools.partial(input_grad_kernel, depth),
        out_shape=jax.ShapeDtypeStruct((grads.shape[0], depth * len(blocks)), bf16),
        in_specs=[in_smem()] + [in_vmem()] * (1 + len(blocks)),
        out_specs=in_vmem(),
        scratch_shapes=[pltpu.VMEM((depth * len(blocks), grads.shape[1]), bf16)],
        compiler_params=pltpu.CompilerParams(vmem_limit_bytes=58 << 20),
        cost_estimate=LITTLE,
        name="input_grad",
    )(place, grads, *blocks)


def pair_grad_kernel(half, left, right, other_left, other_right, out):
    def block(rows_in, grads):
        out[0] = lax.dot_general(
            rows_in[...], grads[...], (((0,), (0,)), ((), ())), preferred_element_type=f32
        ).astype(bf16)

    pl.when(pl.program_id(0) < half)(lambda: block(left, right))
    pl.when(pl.program_id(0) >= half)(lambda: block(other_left, other_right))


def pair_grad_of(left, right, other_left, other_right):
    rows, width = left.shape
    cols = right.shape[1]
    step, half = 256, width // 256
    first = pl.BlockSpec((rows, step), lambda i: (0, jnp.minimum(i, half - 1)))
    second = pl.BlockSpec((rows, step), lambda i: (0, jnp.maximum(i - half, 0)))
    return pl.pallas_call(
        functools.partial(pair_grad_kernel, half),
        grid=(2 * half,),
        out_shape=jax.ShapeDtypeStruct((2, width, cols), bf16),
        in_specs=[first, in_vmem(), second, in_vmem()],
        out_specs=pl.BlockSpec((1, step, cols), lambda i: (i // half, i % half, 0)),
        compiler_params=pltpu.CompilerParams(vmem_limit_bytes=58 << 20),
        cost_estimate=LITTLE,
        name="pair_grad",
    )(left, right, other_left, other_right)


def widen_kernel(pair, up, down, square):
    part = jnp.zeros((1, 1), f32)
    for source, target, turn in ((pair.at[0], up, False), (pair.at[1], down, True)):
        value = source[...].astype(f32)
        part = part + jnp.sum(jnp.sum(value * value, axis=0, keepdims=True), axis=1, keepdims=True)
        target[...] = value.T if turn else value
    square[...] = jnp.broadcast_to(part, square.shape)


def widen(pair):
    _, cols, units = pair.shape
    shapes = ((cols, units), (units, cols), (8, HEAD))
    return pl.pallas_call(
        widen_kernel,
        out_shape=tuple(jax.ShapeDtypeStruct(s, f32) for s in shapes),
        in_specs=[in_vmem()],
        out_specs=(in_vmem(),) * 3,
        compiler_params=pltpu.CompilerParams(vmem_limit_bytes=58 << 20),
        cost_estimate=LITTLE,
        name="widen",
    )(pair)


def total_kernel(head_cols, *refs):
    pieces, (qkv, out, square) = refs[:-3], refs[-3:]
    part = jnp.zeros((1, 1), f32)
    for j in range(4):
        cut = slice(j * head_cols, (j + 1) * head_cols)
        value = pieces[0][:, cut].astype(f32)
        for piece in pieces[1:]:
            value = value + piece[:, cut].astype(f32)
        part = part + jnp.sum(jnp.sum(value * value, axis=0, keepdims=True), axis=1, keepdims=True)
        if j < 3:
            qkv[j] = value
        else:
            out[...] = value.T
    square[...] = jnp.broadcast_to(part, square.shape)


def total_of(pieces, head_cols):
    depth = pieces[0].shape[0]
    shapes = ((3, depth, head_cols), (head_cols, depth), (8, HEAD))
    return pl.pallas_call(
        functools.partial(total_kernel, head_cols),
        out_shape=tuple(jax.ShapeDtypeStruct(s, f32) for s in shapes),
        in_specs=[in_vmem()] * len(pieces),
        out_specs=(in_vmem(),) * 3,
        compiler_params=pltpu.CompilerParams(vmem_limit_bytes=58 << 20),
        cost_estimate=LITTLE,
        name="total",
    )(*pieces)


ADAM_STEPS = 8


def adam_kernel(count, factor, decays, *refs):
    ins, outs = refs[: 4 * count], refs[4 * count :]
    for index in range(count):
        master, grad, first, second = (r[...] for r in ins[4 * index : 4 * index + 4])
        results = adam_update(master, grad, first, second, factor[0], decays[index])
        for target, value in zip(outs[3 * index : 3 * index + 3], results):
            target[...] = value


def adam(factor, decays, groups):
    specs, shapes, flat = ([], [], [])
    for group in groups:
        lines, cols = group[0].shape
        spec = pl.BlockSpec((lines // ADAM_STEPS, cols), lambda step: (step, 0))
        flat.extend(group)
        specs.extend([spec] * 3)
        shapes.extend([jax.ShapeDtypeStruct((lines, cols), f32)] * 3)
    in_specs = [s for spec in specs[::3] for s in [spec] * 4]
    results = pl.pallas_call(
        functools.partial(adam_kernel, len(groups)),
        grid=(ADAM_STEPS,),
        out_shape=tuple(shapes),
        in_specs=[in_smem(), in_smem()] + in_specs,
        out_specs=tuple(specs),
        compiler_params=pltpu.CompilerParams(vmem_limit_bytes=58 << 20),
        cost_estimate=LITTLE,
        name="adam",
    )(factor.reshape(1), decays, *flat)
    return [results[3 * i : 3 * i + 3] for i in range(len(groups))]


def norm_parts(rows):
    mean = jnp.mean(rows, axis=1, keepdims=True)
    centred = rows - mean
    rstd = lax.rsqrt(jnp.mean(centred * centred, axis=1, keepdims=True) + eps_norm)
    return (centred * rstd, rstd)


def norm_back(grad_out, normed, rstd, gain):
    scaled = grad_out * gain
    inner = (
        scaled
        - jnp.mean(scaled, axis=1, keepdims=True)
        - normed * jnp.mean(scaled * normed, axis=1, keepdims=True)
    )
    return (inner * rstd, jnp.sum(grad_out * normed, axis=0), jnp.sum(grad_out, axis=0))


def adam_update(master, grad, first, second, factor, decays):
    clipped = grad * factor
    first_new = beta_one * first + (1.0 - beta_one) * clipped
    second_new = beta_two * second + (1.0 - beta_two) * clipped * clipped
    fix_one = 1.0 - beta_one**step_count
    fix_two = 1.0 - beta_two**step_count
    update = first_new / fix_one / (jnp.sqrt(second_new / fix_two) + adam_eps)
    amount = learn_rate * (update + decay_rate * decays * master)
    return (amount, first_new, second_new)


def key_span(positions, seq_lengths):
    ends = jnp.cumsum(seq_lengths)
    starts = ends - seq_lengths
    inside = (positions[:, None] >= starts[None, :]) & (positions[:, None] < ends[None, :])
    begin = jnp.sum(jnp.where(inside, starts[None, :], 0), axis=1)
    end = jnp.sum(jnp.where(inside, ends[None, :], 0), axis=1)
    block = (positions - begin) // BLOCK
    return (begin, jnp.minimum(begin + (block + 1) * BLOCK, end))


def per_device(
    tokens,
    cotangent,
    w_qkv,
    w_out,
    w_up,
    w_down,
    norm_gains,
    norm_biases,
    m_qkv,
    m_out,
    m_up,
    m_down,
    m_gains,
    m_biases,
    v_qkv,
    v_out,
    v_up,
    v_down,
    v_gains,
    v_biases,
    seq_lengths,
    decay_mask,
):
    rows, width = tokens.shape
    ctx_count, tp_count = lax.axis_size("ctx"), lax.axis_size("tp")
    ctx_place = lax.axis_index("ctx").astype(jnp.int32)
    tp_place = lax.axis_index("tp").astype(jnp.int32)
    total_rows = rows * ctx_count
    part_rows = rows // tp_count
    head_cols = w_out.shape[0]
    heads = head_cols // HEAD
    units = w_up.shape[1]
    ctx_cols = w_out.shape[1]
    scale = HEAD ** (-0.5)
    my_head = lax.rem(ctx_place // 2, heads)

    place = jnp.stack((ctx_place, tp_place))

    small = jnp.concatenate((norm_gains, norm_biases), axis=0)
    small = jnp.pad(small, ((0, 12), (0, 3 * head_cols - ctx_cols)))
    qkv_pack = jnp.concatenate((w_qkv[0], w_qkv[1], w_qkv[2]), axis=1)
    qkv_pack = jnp.concatenate((qkv_pack, small), axis=0).astype(bf16)
    out_pack = w_out.T.astype(bf16)
    rest_pack = jnp.concatenate((w_up, w_down.T), axis=1).astype(bf16)

    x_slots = in_slots(tokens, tp_place, tp_count)
    c_slots = in_slots(cotangent, tp_place, tp_count)
    qkv_blocks, early = ctx_gather(qkv_pack, (out_pack, rest_pack, x_slots))
    out_pack, rest_pack, x_slots = early
    out_pack, rest_pack, qkv_blocks = lax.optimization_barrier((out_pack, rest_pack, qkv_blocks))
    out_full = lax.all_gather(out_pack, "ctx", axis=0, tiled=True)

    group = [s << 1 for s in range(heads)]
    far_bits = list(range(heads.bit_length(), ctx_count.bit_length() - 1))
    inner_rows = jnp.arange(part_rows, dtype=jnp.int32)
    positions = jnp.concatenate(
        [
            jnp.bitwise_xor(ctx_place, m) * rows + jnp.bitwise_xor(tp_place, s) * part_rows + inner_rows
            for m in group
            for s in range(tp_count)
        ]
    )
    lo, hi = key_span(positions, seq_lengths)
    span = jnp.stack((lo, hi))
    tiles = jnp.stack(
        (
            jnp.min(lo.reshape(-1, Q_TILE), axis=1) // (2 * rows),
            (jnp.max(hi.reshape(-1, Q_TILE), axis=1) + 2 * rows - 1) // (2 * rows),
        )
    )
    *pieces, a1, small = project(place, x_slots, qkv_blocks, heads, ctx_cols)
    gain_one, gain_two, bias_two = small[0], small[1], small[3]
    own_parts = [pieces[0]] + [ctx_xor(pieces[s], s << 1) for s in range(1, heads)]
    own_parts, rest_pack = lax.optimization_barrier((own_parts, rest_pack))
    rest_full = lax.all_gather(rest_pack, "ctx", axis=0, tiled=True)
    up_full, down_full = rest_full[:, :units], rest_full[:, units:]
    own = jnp.concatenate(own_parts, axis=0)
    even = own[:, HEAD:]
    for bit in far_bits:
        even = jnp.concatenate((even, ctx_xor(even, 1 << bit)), axis=0)
    odd = ctx_xor(even, 1)
    even = even if far_bits else None
    shape = (rows, tp_count, scale)
    mixed_low, mixed_t, lse = attention_forward(place, tiles, span, own, even, odd, *shape)

    back = [mixed_low[:rows]]
    for s in range(1, heads):
        back.append(ctx_xor(mixed_low[s * rows : (s + 1) * rows], s << 1))
    back = jnp.concatenate(back, axis=0)
    attn_vals = jnp.concatenate(
        [lax.dynamic_slice_in_dim(back, jnp.bitwise_xor(my_head, h) * rows, rows, 0) for h in range(heads)],
        axis=1,
    )
    attn = lax.dot_general(attn_vals, out_full, (((1,), (1,)), ((), ())), preferred_element_type=f32)
    x_own = x_slots[:part_rows].astype(f32)
    y1 = x_own + tp_scatter(attn.astype(bf16))
    normed2, rstd2 = norm_parts(y1)
    a2_own = (normed2 * gain_two + bias_two).astype(bf16)
    grad_act = jnp.dot(c_slots, down_full, preferred_element_type=f32)
    a2, grad_act = lax.optimization_barrier((tp_gather(a2_own), grad_act))
    a2 = jnp.concatenate(a2, axis=0)

    up = jnp.dot(a2, up_full, preferred_element_type=f32)
    cdf = 0.5 * (1.0 + lax.erf(up * inv_root_two))
    act = (up * cdf).astype(bf16)
    slope = cdf + up * jnp.exp(-0.5 * up * up) * inv_root_two_pi
    grad_up_in = (grad_act * slope).astype(bf16)
    grad_h2 = lax.dot_general(grad_up_in, up_full, (((1,), (1,)), ((), ())), preferred_element_type=f32).astype(bf16)
    grad_h2, act, grad_up_in = lax.optimization_barrier((grad_h2, act, grad_up_in))
    grad_h2 = tp_send(grad_h2)
    grad_h2 = tp_total(grad_h2)
    pair_grad = pair_grad_of(a2, grad_up_in, c_slots, act)
    pair_shard = lax.psum_scatter(pair_grad, "ctx", scatter_dimension=1, tiled=True)
    grad_h2, pair_grad = lax.optimization_barrier((grad_h2, pair_grad))

    dx2, dg2, dc2 = norm_back(grad_h2, normed2, rstd2, gain_two)
    c_own = c_slots[:part_rows].astype(f32)
    grad_y1 = c_own + dx2
    grad_attn = jnp.concatenate(tp_gather(grad_y1.astype(bf16)), axis=0)
    mixed = lax.dot_general(act, down_full, (((1,), (1,)), ((), ())), preferred_element_type=f32).astype(bf16)
    mixed, grad_attn = lax.optimization_barrier((mixed, grad_attn))
    block_out = (y1 + tp_scatter(mixed)).astype(bf16)

    grad_vals = jnp.dot(grad_attn, out_full, preferred_element_type=f32).astype(bf16)

    grads = []
    for s in range(heads):
        piece = lax.dynamic_slice_in_dim(grad_vals, jnp.bitwise_xor(my_head, s) * HEAD, HEAD, 1)
        grads.append(piece if s == 0 else ctx_xor(piece, s << 1))
    grads = jnp.concatenate(grads, axis=0)
    results = attention_backward(place, tiles, span, own, grads, mixed_t, lse, even, odd, *shape)
    grad_q, grad_kv, grad_odd = results
    got = ctx_xor(grad_odd, 1)
    for bit in reversed(far_bits):
        grad_kv = grad_kv + got.astype(f32)
        half = grad_kv.shape[0] // 2
        got = ctx_xor(grad_kv[half:].astype(bf16), 1 << bit)
        grad_kv = grad_kv[:half]
    got, block_out = lax.optimization_barrier((got, block_out))
    grad_own = merge(grad_q, grad_kv, got, heads)
    back = [grad_own[0]]
    for s in range(1, heads):
        back.append(ctx_xor(grad_own[s], s << 1))
    back = jnp.concatenate(back, axis=0)
    by_head = [
        lax.dynamic_slice_in_dim(back, jnp.bitwise_xor(my_head, h) * rows, rows, 0) for h in range(heads)
    ]
    grad_qkv_in = jnp.concatenate(
        [by_head[h][:, j * HEAD : (j + 1) * HEAD] for j in range(3) for h in range(heads)], axis=1
    )
    chips = list(range(0, ctx_count, 2))
    pairs = ((a1, grad_qkv_in), (grad_attn, attn_vals))
    sent = weight_grad(place, pairs, ctx_cols)
    sent, later, block_out = lax.optimization_barrier((sent, grad_qkv_in, tp_gather_first(block_out)))
    got = ctx_xor(sent, 1)
    grad_h1 = input_grad(place, later, qkv_blocks, ctx_cols)
    block_out, grad_h1 = lax.optimization_barrier((tp_gather_last(block_out), grad_h1))
    got, pair_shard = lax.optimization_barrier((got, pair_shard))
    summed = weight_grad(place, pairs, ctx_cols, got)
    grad_h1 = tp_send(grad_h1, summed)
    up_grad, down_grad, square = widen(pair_shard)
    arrived = [ctx_xor(summed[slot], mask) for slot, mask in enumerate(chips) if slot]
    grad_h1, _, up_grad = lax.optimization_barrier((grad_h1, summed, up_grad))
    grad_h1 = tp_total(grad_h1)
    block_out = slots_to_rows(block_out, tp_place)
    normed1, rstd1 = norm_parts(x_own)
    dx1, dg1, dc1 = norm_back(grad_h1, normed1, rstd1, gain_one)
    grad_tokens = (grad_y1 + dx1).astype(bf16)
    qkv_grad, out_grad, more = total_of([summed[0], *arrived], head_cols)
    square = square[0, 0] + more[0, 0]
    lines = jnp.stack((dg1, dg2, dc1, dc2)).reshape(-1, HEAD)
    sent = jnp.concatenate((lines, jnp.full((8, HEAD), square, f32)), axis=0)
    sent, grad_tokens = lax.optimization_barrier((sent, tp_gather_first(grad_tokens)))
    total, grad_tokens = sum_over_all(sent, grad_tokens)
    grad_tokens = tp_gather_last(grad_tokens)
    small_grad = total[:-8].reshape(4, width)
    total_sq = total[-1, 0] + jnp.sum(small_grad * small_grad)
    grad_norm = jnp.sqrt(total_sq)
    factor = 1.0 / jnp.maximum(grad_norm, 1.0)
    small_own = lax.dynamic_slice_in_dim(small_grad, ctx_place * ctx_cols, ctx_cols, 1)

    flags = decay_mask.astype(f32)
    flat = lambda value: value.reshape(-1, head_cols)
    matrices = adam(
        factor,
        flags,
        (
            (flat(w_qkv), flat(qkv_grad), flat(m_qkv), flat(v_qkv)),
            (w_out, out_grad, m_out, v_out),
            (w_up, up_grad, m_up, v_up),
            (w_down, down_grad, m_down, v_down),
        ),
    )
    matrices[0] = [value.reshape(w_qkv.shape) for value in matrices[0]]
    gains_new = adam_update(norm_gains, small_own[:2], m_gains, v_gains, factor, flags[4])
    biases_new = adam_update(norm_biases, small_own[2:], m_biases, v_biases, factor, flags[5])
    grad_tokens = slots_to_rows(grad_tokens, tp_place)
    shards = (qkv_grad, out_grad, up_grad, down_grad, small_own[:2], small_own[2:])
    updates = list(zip(*matrices, gains_new, biases_new))
    return (block_out, grad_tokens, grad_norm, *shards, *updates[0], *updates[1], *updates[2])


def solution(mesh):
    small = P(None, "ctx")
    weights = (P(None, "ctx", "tp"), P("tp", "ctx"), P("ctx", "tp"), P("tp", "ctx"), small, small)
    rows = (P("ctx", None), P("ctx", None))
    return jax.shard_map(
        per_device,
        mesh=mesh,
        in_specs=(*rows, *weights, *weights, *weights, P(), P()),
        out_specs=(*rows, P(), *weights, *weights, *weights, *weights),
        check_vma=False,
    )
```

time: 604 us -> 548 us (0.907)
  waiting for transfers between devices: 272 us -> 245 us
  starting transfers between devices: 82.8 us -> 58.1 us
  Pallas kernels: 112 us -> 120 us
  other arithmetic: 37.8 us -> 30.5 us
    ppermute x27, waiting for transfers between devices: 158 us -> 121 us  [tp_xor(): lax.ppermute(value, 'tp', [(place, place ^ mask) for place in range(count)])]
    ppermute x27, starting transfers between devices: 58 us -> 33.7 us  [tp_xor(): lax.ppermute(value, 'tp', [(place, place ^ mask) for place in range(count)])]
    ppermute x29 -> x28, waiting for transfers between devices: 106 us -> 124 us  [ctx_xor(): lax.ppermute(value, 'ctx', [(place, place ^ mask) for place in range(coun...]
    all_gather x1, waiting for transfers between devices: 7.62 us -> 0.01 us  [per_device(): rest_full = lax.all_gather(rest_pack, 'ctx', axis=0, tiled=True)]
    pallas_call x4 -> x5, Pallas kernels: 50.7 us -> 56.5 us  [the longest x1 20.3 us: attention_backward(): pl.pallas_call(functools.partial(backward_kernel, rows, chunks, HEAD if e...]
    unnamed x131 -> x143, local copies, waits for them, and re-layouts: 11.2 us -> 14.4 us
    ppermute x29 -> x28, starting transfers between devices: 24.7 us -> 24.3 us  [ctx_xor(): lax.ppermute(value, 'ctx', [(place, place ^ mask) for place in range(coun...]
  transfers between devices with their start and end apart: 60 -> 58, of which waited for: 35 -> 38; matrix products, arithmetic and copies ran while one was open for 13% -> 13% of each run, Pallas kernels for 18% -> 22%
where the time goes in v3:
time: 548 us; the launch traced here: 547 us
  waiting for transfers between devices  245 us (45%)
  Pallas kernels  120 us (22%)
  starting transfers between devices  58.1 us (11%)
  matrix products  39.3 us (7%)
  local copies, waits for them, and re-layouts  33.3 us (6%)
  other arithmetic  30.5 us (6%)
  between operations  20.4 us (4%)
    ppermute x28, waiting for transfers between devices, ctx_xor(): lax.ppermute(value, 'ctx', [(place, place ^ mask) for place in range(coun...  124 us
    ppermute x27, waiting for transfers between devices, tp_xor(): lax.ppermute(value, 'tp', [(place, place ^ mask) for place in range(count)])  121 us
    ppermute x27, starting transfers between devices, tp_xor(): lax.ppermute(value, 'tp', [(place, place ^ mask) for place in range(count)])  33.7 us
    ppermute x28, starting transfers between devices, ctx_xor(): lax.ppermute(value, 'ctx', [(place, place ^ mask) for place in range(coun...  24.3 us
    pallas_call x1, Pallas kernels, attention_backward(): pl.pallas_call(functools.partial(backward_kernel, rows, chunks, HEAD if e...  20.3 us
    pallas_call x1, Pallas kernels, pair_grad_of(): pl.pallas_call(functools.partial(pair_grad_kernel, half), grid=(2 * half,...  18.8 us
    pallas_call x2, Pallas kernels, weight_grad(): pl.pallas_call(functools.partial(weight_grad_kernel, flip, depth), out_sh...  17.8 us
    pallas_call x1, Pallas kernels, adam(): pl.pallas_call(functools.partial(adam_kernel, len(groups)), grid=(ADAM_ST...  17.2 us
  transfers between devices with their start and end apart: 58, of which 38 were waited for; matrix products, arithmetic and copies ran while one was open for 13% of the time, Pallas kernels for 22%

profile of v3, /device:TPU:0, one launch (start us, length us, event | category | flops | bytes accessed | tf_op | source)
XLA Modules:
  0.0 546.7 jit_solution(603005826719527009)
XLA Ops:
  10.3 3.0 collective-permute-start
  16.0 2.9 constant_dynamic-slice_fusion.24
  21.0 3.1 pad_maximum_fusion.1.rows_in
  25.5 7.3 %collective-permute-done.refs_2_ = bf16[272,1536]{1,0:T(8,128)(2,1)} collective-permute-done((bf16[272,1536]{1,0:T(8,128)(2,1)S(1)}, bf16[272,1536]{1,0:T(8,128)(2,1)}, u32[]{:S(2)}, u32[]{:S(2)}) %collective-permute-start) | collective-permute-done | bytes 835616 | tf_op jit(solution)/shard_map/ppermute | solution.py:32
  32.8 19.5 %collective-permute-done.3.refs_4_ = bf16[272,1536]{1,0:T(8,128)(2,1)} collective-permute-done((bf16[272,1536]{1,0:T(8,128)(2,1)S(1)}, bf16[272,1536]{1,0:T(8,128)(2,1)}, u32[]{:S(2)}, u32[]{:S(2)}) %collective-permute-start.3) | collective-permute-done | bytes 835616 | tf_op jit(solution)/shard_map/ppermute | solution.py:32
  52.8 2.0 collective-permute-done.4.refs_5_
  57.0 11.4 %project.1 = (bf16[512,384]{1,0:T(8,128)(2,1)}, bf16[512,384]{1,0:T(8,128)(2,1)}, bf16[512,384]{1,0:T(8,128)(2,1)}, bf16[512,384]{1,0:T(8,128)(2,1)}, bf16[512,2048]{1,0:T(8,128)(2,1)}, /*index=5*/f32[8,2048]{1,0:T(8,128)}) custom-call(s32[2]{0:T(128)} %pad_add_fusion.2.place, bf16[512,2048]{1,0:T(8,128)(2,1)} %pad_maximum_fusion.1.rows_in, ...), custom_call_target="tpu_custom_call" | custom-call | flops 1 | bytes 1 | tf_op jit(solution)/shard_map/project/pallas_call | solution.py:348
  68.5 2.0 collective-permute-start.8
  72.0 12.0 %collective-permute-done.7 = bf16[512,384]{1,0:T(8,128)(2,1)S(1)} collective-permute-done((bf16[512,384]{1,0:T(8,128)(2,1)}, bf16[512,384]{1,0:T(8,128)(2,1)S(1)}, u32[]{:S(2)}, u32[]{:S(2)}) %collective-permute-start.7) | collective-permute-done | bytes 393248 | tf_op jit(solution)/shard_map/ppermute | solution.py:32
  84.0 2.4 collective-permute-done.8
  86.5 8.4 %collective-permute-done.9 = bf16[512,384]{1,0:T(8,128)(2,1)S(1)} collective-permute-done((bf16[512,384]{1,0:T(8,128)(2,1)}, bf16[512,384]{1,0:T(8,128)(2,1)S(1)}, u32[]{:S(2)}, u32[]{:S(2)}) %collective-permute-start.9) | collective-permute-done | bytes 393248 | tf_op jit(solution)/shard_map/ppermute | solution.py:32
  100.0 14.0 %attention_forward.1 = (bf16[2048,128]{1,0:T(8,128)(2,1)}, f32[128,2048]{1,0:T(8,128)}, f32[1,2048]{1,0:T(1,128)}) custom-call(s32[2]{0:T(128)} %pad_add_fusion.2.place, s32[2,4]{1,0:T(2,128)} %pad_add_fusion.1.tiles, s32[2,2048]{1,0:T(2,128)} %pad_add_fusion.span, bf16[2048,384]{1,0:T(8,128)(2,1)} %copy-done.4, bf16[2048,256]{1,0:T(8,128)(2,1)} %copy-done.8), custom_call_target="tpu_custom_call" | custom-call | flops 1 | bytes 1 | tf_op jit(solution)/shard_map/attention_forward/pallas_call | solution.py:235
  118.7 6.4 %collective-permute-done.13 = bf16[512,128]{1,0:T(8,128)(2,1)S(1)} collective-permute-done((bf16[512,128]{1,0:T(8,128)(2,1)S(1)}, bf16[512,128]{1,0:T(8,128)(2,1)S(1)}, u32[]{:S(2)}, u32[]{:S(2)}) %collective-permute-start.13) | collective-permute-done | bytes 131104 | tf_op jit(solution)/shard_map/ppermute | solution.py:32
  125.1 3.0 collective-permute-done.12
  128.1 1.7 collective-permute-done.11
  130.0 3.0 convolution_convert_fusion
  133.1 1.6 collective-permute-start.14
  134.9 12.7 %collective-permute-done.14 = bf16[128,2048]{1,0:T(8,128)(2,1)S(1)} collective-permute-done((bf16[128,2048]{1,0:T(8,128)(2,1)S(1)}, bf16[128,2048]{1,0:T(8,128)(2,1)S(1)}, u32[]{:S(2)}, u32[]{:S(2)}) %collective-permute-start.14) | collective-permute-done | bytes 524320 | tf_op jit(solution)/shard_map/ppermute | solution.py:47
  147.7 2.7 collective-permute-start.16
  153.5 20.2 %collective-permute-done.16 = bf16[128,2048]{1,0:T(8,128)(2,1)S(1)} collective-permute-done((bf16[128,2048]{1,0:T(8,128)(2,1)S(1)}, bf16[128,2048]{1,0:T(8,128)(2,1)S(1)}, u32[]{:S(2)}, u32[]{:S(2)}) %collective-permute-start.16) | collective-permute-done | bytes 524320 | tf_op jit(solution)/shard_map/ppermute | solution.py:47
  177.9 2.4 collective-permute-start.17
  180.3 20.1 %collective-permute-done.18 = bf16[128,2048]{1,0:T(8,128)(2,1)} collective-permute-done((bf16[128,2048]{1,0:T(8,128)(2,1)S(1)}, bf16[128,2048]{1,0:T(8,128)(2,1)}, u32[]{:S(2)}, u32[]{:S(2)}) %collective-permute-start.18) | collective-permute-done | bytes 524320 | tf_op jit(solution)/shard_map/ppermute | solution.py:47
  200.4 10.1 %fusion.6 = f32[512,2048]{1,0:T(8,128)} fusion(bf16[2048,4096]{0,1:T(8,128)(2,1)} %all-gather.5.cloned.1.call-done, bf16[128,2048]{1,0:T(8,128)(2,1)S(1)} %get-tuple-element.275, bf16[128,2048]{1,0:T(8,128)(2,1)} %get-tuple-element.276, bf16[128,2048]{1,0:T(8,128)(2,1)S(1)} %get-tuple-element.274, bf16[128,2048]{1,0:T(8,128)(2,1)S(1)} %get-tuple-element.273), kind=kOutput, calls=%fused_computation.6 | convolution fusion | flops 4303355904 | bytes 14680064 | tf_op jit(solution)/shard_map/dot_general | solution.py:698
  210.6 2.2 collective-permute-done.19
  216.3 11.0 %multiply_convert_fusion = (bf16[512,2048]{1,0:T(8,128)(2,1)}, bf16[512,2048]{1,0:T(8,128)(2,1)S(1)}) fusion(f32[512,2048]{1,0:T(8,128)} %fusion.6, bf16[512,2048]{1,0:T(8,128)(2,1)S(1)} %constant_dynamic-update-slice_fusion.21.left, bf16[2048,4096]{0,1:T(8,128)(2,1)} %all-gather.5.cloned.1.call-done), kind=kOutput, calls=%fused_computation.15 | convolution fusion | flops 4307550208 | bytes 18874368 | tf_op jit(solution)/shard_map/dot_general | solution.py:702
  227.3 4.9 fusion.17
  234.6 10.8 %collective-permute-done.20 = bf16[128,2048]{1,0:T(8,128)(2,1)S(1)} collective-permute-done((bf16[128,2048]{1,0:T(8,128)(2,1)S(1)}, bf16[128,2048]{1,0:T(8,128)(2,1)S(1)}, u32[]{:S(2)}, u32[]{:S(2)}) %collective-permute-start.20) | collective-permute-done | bytes 524320 | tf_op jit(solution)/shard_map/ppermute | solution.py:47
  246.3 4.2 collective-permute-start.22
  253.4 18.8 %pair_grad.1 = bf16[2,2048,2048]{2,1,0:T(8,128)(2,1)} custom-call(bf16[512,2048]{1,0:T(8,128)(2,1)} %copy-done.15, bf16[512,2048]{1,0:T(8,128)(2,1)} %copy-done.16, bf16[512,2048]{1,0:T(8,128)(2,1)} %pad_maximum_fusion.2.other_left, bf16[512,2048]{1,0:T(8,128)(2,1)} %get-tuple-element.162.other_right), custom_call_target="tpu_custom_call" | custom-call | flops 1 | bytes 1 | tf_op jit(solution)/shard_map/pair_grad/pallas_call | solution.py:462
  278.0 2.6 collective-permute-start.23
  280.6 21.8 %collective-permute-done.24 = bf16[128,2048]{1,0:T(8,128)(2,1)S(1)} collective-permute-done((bf16[128,2048]{1,0:T(8,128)(2,1)S(1)}, bf16[128,2048]{1,0:T(8,128)(2,1)S(1)}, u32[]{:S(2)}, u32[]{:S(2)}) %collective-permute-start.24) | collective-permute-done | bytes 524320 | tf_op jit(solution)/shard_map/ppermute | solution.py:47
  302.4 9.0 %fusion.14 = bf16[512,2048]{1,0:T(8,128)(2,1)S(1)} fusion(bf16[512,2048]{1,0:T(8,128)(2,1)} %get-tuple-element.162.other_right, bf16[2048,4096]{0,1:T(8,128)(2,1)} %all-gather.5.cloned.1.call-done), kind=kOutput, calls=%fused_computation.17 | convolution fusion | flops 4296015872 | bytes 12582912 | tf_op jit(solution)/shard_map/dot_general | solution.py:719
  311.4 4.0 collective-permute-done.25
  316.1 1.9 copy-done.50
  320.9 1.6 collective-permute-start.27
  323.0 5.1 collective-permute-done.30
  328.2 1.9 collective-permute-start.32
  331.5 3.0 collective-permute-done.26
  335.3 20.3 %attention_backward.1 = (bf16[2048,128]{1,0:T(8,128)(2,1)}, f32[2048,256]{1,0:T(8,128)}, bf16[2048,256]{1,0:T(8,128)(2,1)}) custom-call(s32[2]{0:T(128)} %pad_add_fusion.2.place, s32[2,4]{1,0:T(2,128)} %pad_add_fusion.1.tiles, s32[2,2048]{1,0:T(2,128)} %pad_add_fusion.span, bf16[2048,384]{1,0:T(8,128)(2,1)} %copy-done.4, ...), custom_call_target="tpu_custom_call" | custom-call | flops 1 | bytes 1 | tf_op jit(solution)/shard_map/attention_backward/pallas_call | solution.py:258
  356.7 1.8 collective-permute-done.29.refs_0_
  359.4 3.3 merge.1
  367.8 2.4 collective-permute-start.37
  371.2 11.4 %collective-permute-done.33 = bf16[512,384]{1,0:T(8,128)(2,1)S(1)} collective-permute-done((bf16[512,384]{1,0:T(8,128)(2,1)}, bf16[512,384]{1,0:T(8,128)(2,1)S(1)}, u32[]{:S(2)}, u32[]{:S(2)}) %collective-permute-start.33) | collective-permute-done | bytes 393248 | tf_op jit(solution)/shard_map/ppermute | solution.py:32
  382.7 2.7 collective-permute-done.34
  385.5 12.2 %collective-permute-done.35 = bf16[512,384]{1,0:T(8,128)(2,1)S(1)} collective-permute-done((bf16[512,384]{1,0:T(8,128)(2,1)}, bf16[512,384]{1,0:T(8,128)(2,1)S(1)}, u32[]{:S(2)}, u32[]{:S(2)}) %collective-permute-start.35) | collective-permute-done | bytes 393248 | tf_op jit(solution)/shard_map/ppermute | solution.py:32
  399.5 8.3 %weight_grad.2 = bf16[1024,2048]{1,0:T(8,128)(2,1)} custom-call(s32[2]{0:T(128)} %pad_add_fusion.2.place, bf16[512,2048]{1,0:T(8,128)(2,1)} %get-tuple-element.141.refs_0_, bf16[512,1536]{1,0:T(8,128)(2,1)} %copy-done.3, bf16[512,2048]{1,0:T(8,128)(2,1)} %copy-done.2, bf16[512,512]{1,0:T(8,128)(2,1)} %pad_maximum_fusion.8.refs_3_), custom_call_target="tpu_custom_call" | custom-call | flops 1 | bytes 1 | tf_op jit(solution)/shard_map/weight_grad/pallas_call | solution.py:405
  408.1 9.3 %input_grad.1 = bf16[512,2048]{1,0:T(8,128)(2,1)} custom-call(s32[2]{0:T(128)} %pad_add_fusion.2.place, bf16[512,1536]{1,0:T(8,128)(2,1)} %copy-done.3, bf16[272,1536]{1,0:T(8,128)(2,1)} %copy-done.7, bf16[272,1536]{1,0:T(8,128)(2,1)} %collective-permute-done.1.refs_1_, bf16[272,1536]{1,0:T(8,128)(2,1)} %collective-permute-done.refs_2_, ...), custom_call_target="tpu_custom_call" | custom-call | flops 1 | bytes 1 | tf_op jit(solution)/shard_map/input_grad/pallas_call | solution.py:434
  417.4 5.0 collective-permute-done.38
  422.4 2.3 fusion.53
  426.9 9.5 %weight_grad.3 = (bf16[256,2048]{1,0:T(8,128)(2,1)}, bf16[256,2048]{1,0:T(8,128)(2,1)}, bf16[256,2048]{1,0:T(8,128)(2,1)}, bf16[256,2048]{1,0:T(8,128)(2,1)}) custom-call(s32[2]{0:T(128)} %pad_add_fusion.2.place, bf16[512,2048]{1,0:T(8,128)(2,1)} %get-tuple-element.141.refs_0_, bf16[512,1536]{1,0:T(8,128)(2,1)} %copy-done.3, bf16[512,2048]{1,0:T(8,128)(2,1)} %copy-done.2, ...), custom_call_target="tpu_custom_call" | custom-call | flops 1 | bytes 1 | tf_op jit(solution)/shard_map/weight_grad/pallas_call | solution.py:405
  436.4 1.8 collective-permute-done.39
  443.5 2.9 collective-permute-start.43
  447.9 3.7 widen.1
  451.7 7.9 %collective-permute-done.41 = bf16[128,2048]{1,0:T(8,128)(2,1)S(1)} collective-permute-done((bf16[128,2048]{1,0:T(8,128)(2,1)}, bf16[128,2048]{1,0:T(8,128)(2,1)S(1)}, u32[]{:S(2)}, u32[]{:S(2)}) %collective-permute-start.41) | collective-permute-done | bytes 524320 | tf_op jit(solution)/shard_map/ppermute | solution.py:47
  459.6 5.0 collective-permute-done.42
  467.6 1.9 constant_dynamic-update-slice_fusion.29
  469.5 1.7 constant_dynamic-slice_fusion.7
  472.5 19.7 %collective-permute-done.44.refs_2_ = bf16[256,2048]{1,0:T(8,128)(2,1)} collective-permute-done((bf16[256,2048]{1,0:T(8,128)(2,1)}, bf16[256,2048]{1,0:T(8,128)(2,1)}, u32[]{:S(2)}, u32[]{:S(2)}) %collective-permute-start.44) | collective-permute-done | bytes 1048608 | tf_op jit(solution)/shard_map/ppermute | solution.py:32
  492.2 4.5 total.1
  500.7 1.7 collective-permute-start.50
  504.6 2.3 collective-permute-done.50
  507.8 3.4 collective-permute-done.52
  512.4 2.8 collective-permute-done.53
  519.0 17.2 %adam.1 = (f32[768,512]{1,0:T(8,128)}, f32[768,512]{1,0:T(8,128)}, f32[768,512]{1,0:T(8,128)}, f32[512,256]{1,0:T(8,128)}, f32[512,256]{1,0:T(8,128)}, /*index=5...) custom-call(f32[1]{0:T(128)} %bitcast.38.factor, ...), custom_call_target="tpu_custom_call" | custom-call | flops 1 | bytes 1 | tf_op jit(solution)/shard_map/adam/pallas_call | solution.py:548
  (334 shorter events, 86.2 us)
Async XLA Ops:
  7.2 122.8 %all-gather.3.cloned.1.call-start = ((), (), s32[]{:S(2)}) async-start(), calls=%async_computation.1 | async-start | bytes 2359296 | tf_op jit(solution)/shard_map/all_gather | solution.py:650
  10.3 22.5 %collective-permute-start = (bf16[272,1536]{1,0:T(8,128)(2,1)S(1)}, bf16[272,1536]{1,0:T(8,128)(2,1)}, u32[]{:S(2)}, u32[]{:S(2)}) collective-permute-start(bf16[272,1536]{1,0:T(8,128)(2,1)S(1)} %pad_maximum_fusion.6.refs_0_), channel_id=1, source_target_pairs={{0,8},{4,12},{8,0},{12,4},{16,24},{20,28},{24,16},{28,20},{1,9},{5... | collective-permute-start | bytes 2506760 | tf_op jit(solution)/shard_map/ppermute | solution.py:32
  13.3 39.5 %collective-permute-start.1 = (bf16[272,1536]{1,0:T(8,128)(2,1)S(1)}, bf16[272,1536]{1,0:T(8,128)(2,1)}, u32[]{:S(2)}, u32[]{:S(2)}) collective-permute-start(bf16[272,1536]{1,0:T(8,128)(2,1)S(1)} %pad_maximum_fusion.6.refs_0_), channel_id=1, source_target_pairs={{0,4},{4,0},{8,12},{12,8},{16,20},{20,16},{24,28},{28,24},{1,5},{5... | collective-permute-start | bytes 2506760 | tf_op jit(solution)/shard_map/ppermute | solution.py:32
  13.3 39.0 %collective-permute-start.3 = (bf16[272,1536]{1,0:T(8,128)(2,1)S(1)}, bf16[272,1536]{1,0:T(8,128)(2,1)}, u32[]{:S(2)}, u32[]{:S(2)}) collective-permute-start(bf16[272,1536]{1,0:T(8,128)(2,1)S(1)} %pad_maximum_fusion.6.refs_0_), channel_id=1, source_target_pairs={{0,16},{4,20},{8,24},{12,28},{16,0},{20,4},{24,8},{28,12},{1,17},{... | collective-permute-start | bytes 2506760 | tf_op jit(solution)/shard_map/ppermute | solution.py:32
  14.8 37.5 %collective-permute-start.5 = (bf16[272,1536]{1,0:T(8,128)(2,1)S(1)}, bf16[272,1536]{1,0:T(8,128)(2,1)}, u32[]{:S(2)}, u32[]{:S(2)}) collective-permute-start(bf16[272,1536]{1,0:T(8,128)(2,1)S(1)} %pad_maximum_fusion.6.refs_0_), channel_id=1, source_target_pairs={{0,24},{4,28},{8,16},{12,20},{16,8},{20,12},{24,0},{28,4},{1,25},{... | collective-permute-start | bytes 2506760 | tf_op jit(solution)/shard_map/ppermute | solution.py:32
  32.8 20.0 %collective-permute-start.2 = (bf16[272,1536]{1,0:T(8,128)(2,1)}, bf16[272,1536]{1,0:T(8,128)(2,1)S(1)}, u32[]{:S(2)}, u32[]{:S(2)}) collective-permute-start(bf16[272,1536]{1,0:T(8,128)(2,1)} %collective-permute-done.refs_2_), channel_id=1, source_target_pairs={{0,4},{4,0},{8,12},{12,8},{16,20},{20,16},{24,28},{28,24},{1,5},{5... | collective-permute-start | bytes 2506760 | tf_op jit(solution)/shard_map/ppermute | solution.py:32
  52.3 2.6 collective-permute-start.4
  52.3 3.8 collective-permute-start.6
  56.1 144.3 %all-gather.5.cloned.1.call-start = ((), (), s32[]{:S(2)}) async-start(), calls=%async_computation.2 | async-start | bytes 18874368 | tf_op jit(solution)/shard_map/all_gather | solution.py:674
  68.4 26.6 %copy-start.52 = (s32[4]{0:T(128)S(1)}, s32[4]{0:T(128)}, u32[]{:S(2)}) copy-start(s32[4]{0:T(128)} %param.42) | copy-start | bytes 52
  68.4 27.5 %copy-start.36 = (bf16[512,384]{1,0:T(8,128)(2,1)S(1)}, bf16[512,384]{1,0:T(8,128)(2,1)}, u32[]{:S(2)}) copy-start(bf16[512,384]{1,0:T(8,128)(2,1)} %get-tuple-element.147) | copy-start | bytes 1179652
  68.4 15.6 %collective-permute-start.7 = (bf16[512,384]{1,0:T(8,128)(2,1)}, bf16[512,384]{1,0:T(8,128)(2,1)S(1)}, u32[]{:S(2)}, u32[]{:S(2)}) collective-permute-start(bf16[512,384]{1,0:T(8,128)(2,1)} %get-tuple-element.143), channel_id=1, source_target_pairs={{0,8},{4,12},{8,0},{12,4},{16,24},{20,28},{24,16},{28,20},{1,9},{5... | collective-permute-start | bytes 1179656 | tf_op jit(solution)/shard_map/ppermute | solution.py:32
  68.5 17.9 %collective-permute-start.8 = (bf16[512,384]{1,0:T(8,128)(2,1)}, bf16[512,384]{1,0:T(8,128)(2,1)S(1)}, u32[]{:S(2)}, u32[]{:S(2)}) collective-permute-start(bf16[512,384]{1,0:T(8,128)(2,1)} %get-tuple-element.144), channel_id=1, source_target_pairs={{0,16},{4,20},{8,24},{12,28},{16,0},{20,4},{24,8},{28,12},{1,17},{... | collective-permute-start | bytes 1179656 | tf_op jit(solution)/shard_map/ppermute | solution.py:32
  70.6 24.3 %collective-permute-start.9 = (bf16[512,384]{1,0:T(8,128)(2,1)}, bf16[512,384]{1,0:T(8,128)(2,1)S(1)}, u32[]{:S(2)}, u32[]{:S(2)}) collective-permute-start(bf16[512,384]{1,0:T(8,128)(2,1)} %get-tuple-element.145), channel_id=1, source_target_pairs={{0,24},{4,28},{8,16},{12,20},{16,8},{20,12},{24,0},{28,4},{1,25},{... | collective-permute-start | bytes 1179656 | tf_op jit(solution)/shard_map/ppermute | solution.py:32
  94.9 332.0 %reduce-scatter.2.cloned.1.call-start = ((), (), s32[]{:S(2)}) async-start(), calls=%async_computation.3 | async-start | bytes 18874368 | tf_op jit(solution)/shard_map/reduce_scatter | solution.py:712
  96.3 2.7 collective-permute-start.10
  115.1 10.0 %collective-permute-start.13 = (bf16[512,128]{1,0:T(8,128)(2,1)S(1)}, bf16[512,128]{1,0:T(8,128)(2,1)S(1)}, u32[]{:S(2)}, u32[]{:S(2)}) collective-permute-start(bf16[512,128]{1,0:T(8,128)(2,1)S(1)} %get-tuple-element.295), channel_id=1, source_target_pairs={{0,24},{4,28},{8,16},{12,20},{16,8},{20,12},{24,0},{28,4},{1,25},{... | collective-permute-start | bytes 393224 | tf_op jit(solution)/shard_map/ppermute | solution.py:32
  116.2 11.9 %collective-permute-start.12 = (bf16[512,128]{1,0:T(8,128)(2,1)S(1)}, bf16[512,128]{1,0:T(8,128)(2,1)S(1)}, u32[]{:S(2)}, u32[]{:S(2)}) collective-permute-start(bf16[512,128]{1,0:T(8,128)(2,1)S(1)} %get-tuple-element.296), channel_id=1, source_target_pairs={{0,16},{4,20},{8,24},{12,28},{16,0},{20,4},{24,8},{28,12},{1,17},{... | collective-permute-start | bytes 393224 | tf_op jit(solution)/shard_map/ppermute | solution.py:32
  117.3 12.6 %collective-permute-start.11 = (bf16[512,128]{1,0:T(8,128)(2,1)S(1)}, bf16[512,128]{1,0:T(8,128)(2,1)S(1)}, u32[]{:S(2)}, u32[]{:S(2)}) collective-permute-start(bf16[512,128]{1,0:T(8,128)(2,1)S(1)} %get-tuple-element.297), channel_id=1, source_target_pairs={{0,8},{4,12},{8,0},{12,4},{16,24},{20,28},{24,16},{28,20},{1,9},{5... | collective-permute-start | bytes 393224 | tf_op jit(solution)/shard_map/ppermute | solution.py:32
  133.1 14.5 %collective-permute-start.14 = (bf16[128,2048]{1,0:T(8,128)(2,1)S(1)}, bf16[128,2048]{1,0:T(8,128)(2,1)S(1)}, u32[]{:S(2)}, u32[]{:S(2)}) collective-permute-start(bf16[128,2048]{1,0:T(8,128)(2,1)S(1)} %get-tuple-element.278), channel_id=1, source_target_pairs={{0,1},{1,0},{2,3},{3,2},{4,5},{5,4},{6,7},{7,6},{8,9},{9,8},{10,11... | collective-permute-start | bytes 1572872 | tf_op jit(solution)/shard_map/ppermute | solution.py:47
  147.7 26.0 %collective-permute-start.16 = (bf16[128,2048]{1,0:T(8,128)(2,1)S(1)}, bf16[128,2048]{1,0:T(8,128)(2,1)S(1)}, u32[]{:S(2)}, u32[]{:S(2)}) collective-permute-start(bf16[128,2048]{1,0:T(8,128)(2,1)S(1)} %add_convert_fusion.5), channel_id=1, source_target_pairs={{0,2},{1,3},{2,0},{3,1},{4,6},{5,7},{6,4},{7,5},{8,10},{9,11},{10,... | collective-permute-start | bytes 1572872 | tf_op jit(solution)/shard_map/ppermute | solution.py:47
  150.4 23.5 %collective-permute-start.15 = (bf16[128,2048]{1,0:T(8,128)(2,1)S(1)}, bf16[128,2048]{1,0:T(8,128)(2,1)S(1)}, u32[]{:S(2)}, u32[]{:S(2)}) collective-permute-start(bf16[128,2048]{1,0:T(8,128)(2,1)S(1)} %get-tuple-element.153), channel_id=1, source_target_pairs={{0,1},{1,0},{2,3},{3,2},{4,5},{5,4},{6,7},{7,6},{8,9},{9,8},{10,11... | collective-permute-start | bytes 1572872 | tf_op jit(solution)/shard_map/ppermute | solution.py:47
  152.0 21.9 %copy-start.43 = (f32[128]{0:T(128)}, f32[128]{0:T(128)S(1)}, u32[]{:S(2)}) copy-start(f32[128]{0:T(128)S(1)} %broadcast_multiply_fusion.2) | copy-start | bytes 1540
  175.5 25.0 %collective-permute-start.18 = (bf16[128,2048]{1,0:T(8,128)(2,1)S(1)}, bf16[128,2048]{1,0:T(8,128)(2,1)}, u32[]{:S(2)}, u32[]{:S(2)}) collective-permute-start(bf16[128,2048]{1,0:T(8,128)(2,1)S(1)} %add_convert_fusion.4), channel_id=1, source_target_pairs={{0,2},{1,3},{2,0},{3,1},{4,6},{5,7},{6,4},{7,5},{8,10},{9,11},{10,... | collective-permute-start | bytes 1572872 | tf_op jit(solution)/shard_map/ppermute | solution.py:47
  177.9 32.7 %collective-permute-start.17 = (bf16[128,2048]{1,0:T(8,128)(2,1)S(1)}, bf16[128,2048]{1,0:T(8,128)(2,1)}, u32[]{:S(2)}, u32[]{:S(2)}) collective-permute-start(bf16[128,2048]{1,0:T(8,128)(2,1)S(1)} %add_convert_fusion.4), channel_id=1, source_target_pairs={{0,1},{1,0},{2,3},{3,2},{4,5},{5,4},{6,7},{7,6},{8,9},{9,8},{10,11... | collective-permute-start | bytes 1572872 | tf_op jit(solution)/shard_map/ppermute | solution.py:47
  200.4 12.3 %collective-permute-start.19 = (bf16[128,2048]{1,0:T(8,128)(2,1)}, bf16[128,2048]{1,0:T(8,128)(2,1)}, u32[]{:S(2)}, u32[]{:S(2)}) collective-permute-start(bf16[128,2048]{1,0:T(8,128)(2,1)} %collective-permute-done.18), channel_id=1, source_target_pairs={{0,1},{1,0},{2,3},{3,2},{4,5},{5,4},{6,7},{7,6},{8,9},{9,8},{10,11... | collective-permute-start | bytes 1572872 | tf_op jit(solution)/shard_map/ppermute | solution.py:47
  233.1 12.2 %collective-permute-start.20 = (bf16[128,2048]{1,0:T(8,128)(2,1)S(1)}, bf16[128,2048]{1,0:T(8,128)(2,1)S(1)}, u32[]{:S(2)}, u32[]{:S(2)}) collective-permute-start(bf16[128,2048]{1,0:T(8,128)(2,1)S(1)} %get-tuple-element.272), channel_id=1, source_target_pairs={{0,1},{1,0},{2,3},{3,2},{4,5},{5,4},{6,7},{7,6},{8,9},{9,8},{10,11... | collective-permute-start | bytes 1572872 | tf_op jit(solution)/shard_map/ppermute | solution.py:47
  246.3 26.4 %collective-permute-start.22 = (bf16[128,2048]{1,0:T(8,128)(2,1)}, bf16[128,2048]{1,0:T(8,128)(2,1)}, u32[]{:S(2)}, u32[]{:S(2)}) collective-permute-start(bf16[128,2048]{1,0:T(8,128)(2,1)} %add_convert_fusion.3), channel_id=1, source_target_pairs={{0,2},{1,3},{2,0},{3,1},{4,6},{5,7},{6,4},{7,5},{8,10},{9,11},{10,... | collective-permute-start | bytes 1572872 | tf_op jit(solution)/shard_map/ppermute | solution.py:47
  250.5 23.0 %collective-permute-start.21 = (bf16[128,2048]{1,0:T(8,128)(2,1)}, bf16[128,2048]{1,0:T(8,128)(2,1)}, u32[]{:S(2)}, u32[]{:S(2)}) collective-permute-start(bf16[128,2048]{1,0:T(8,128)(2,1)} %get-tuple-element.164), channel_id=1, source_target_pairs={{0,1},{1,0},{2,3},{3,2},{4,5},{5,4},{6,7},{7,6},{8,9},{9,8},{10,11... | collective-permute-start | bytes 1572872 | tf_op jit(solution)/shard_map/ppermute | solution.py:47
  277.7 24.7 %collective-permute-start.24 = (bf16[128,2048]{1,0:T(8,128)(2,1)S(1)}, bf16[128,2048]{1,0:T(8,128)(2,1)S(1)}, u32[]{:S(2)}, u32[]{:S(2)}) collective-permute-start(bf16[128,2048]{1,0:T(8,128)(2,1)S(1)} %get-tuple-element.251), channel_id=1, source_target_pairs={{0,2},{1,3},{2,0},{3,1},{4,6},{5,7},{6,4},{7,5},{8,10},{9,11},{10,... | collective-permute-start | bytes 1572872 | tf_op jit(solution)/shard_map/ppermute | solution.py:47
  278.0 33.4 %collective-permute-start.23 = (bf16[128,2048]{1,0:T(8,128)(2,1)S(1)}, bf16[128,2048]{1,0:T(8,128)(2,1)S(1)}, u32[]{:S(2)}, u32[]{:S(2)}) collective-permute-start(bf16[128,2048]{1,0:T(8,128)(2,1)S(1)} %get-tuple-element.251), channel_id=1, source_target_pairs={{0,1},{1,0},{2,3},{3,2},{4,5},{5,4},{6,7},{7,6},{8,9},{9,8},{10,11... | collective-permute-start | bytes 1572872 | tf_op jit(solution)/shard_map/ppermute | solution.py:47
  302.4 13.1 %collective-permute-start.25 = (bf16[128,2048]{1,0:T(8,128)(2,1)S(1)}, bf16[128,2048]{1,0:T(8,128)(2,1)S(1)}, u32[]{:S(2)}, u32[]{:S(2)}) collective-permute-start(bf16[128,2048]{1,0:T(8,128)(2,1)S(1)} %collective-permute-done.24), channel_id=1, source_target_pairs={{0,1},{1,0},{2,3},{3,2},{4,5},{5,4},{6,7},{7,6},{8,9},{9,8},{10,11... | collective-permute-start | bytes 1572872 | tf_op jit(solution)/shard_map/ppermute | solution.py:47
  315.7 12.3 %collective-permute-start.30 = (bf16[128,2048]{1,0:T(8,128)(2,1)S(1)}, bf16[128,2048]{1,0:T(8,128)(2,1)S(1)}, u32[]{:S(2)}, u32[]{:S(2)}) collective-permute-start(bf16[128,2048]{1,0:T(8,128)(2,1)S(1)} %get-tuple-element.270), channel_id=1, source_target_pairs={{0,1},{1,0},{2,3},{3,2},{4,5},{5,4},{6,7},{7,6},{8,9},{9,8},{10,11... | collective-permute-start | bytes 1572872 | tf_op jit(solution)/shard_map/ppermute | solution.py:47
  319.4 12.1 %collective-permute-start.28 = (bf16[512,128]{1,0:T(8,128)(2,1)S(1)}, bf16[512,128]{1,0:T(8,128)(2,1)S(1)}, u32[]{:S(2)}, u32[]{:S(2)}) collective-permute-start(bf16[512,128]{1,0:T(8,128)(2,1)S(1)} %get-tuple-element.287), channel_id=1, source_target_pairs={{0,24},{4,28},{8,16},{12,20},{16,8},{20,12},{24,0},{28,4},{1,25},{... | collective-permute-start | bytes 393224 | tf_op jit(solution)/shard_map/ppermute | solution.py:32
  320.9 10.6 %collective-permute-start.27 = (bf16[512,128]{1,0:T(8,128)(2,1)S(1)}, bf16[512,128]{1,0:T(8,128)(2,1)S(1)}, u32[]{:S(2)}, u32[]{:S(2)}) collective-permute-start(bf16[512,128]{1,0:T(8,128)(2,1)S(1)} %get-tuple-element.288), channel_id=1, source_target_pairs={{0,16},{4,20},{8,24},{12,28},{16,0},{20,4},{24,8},{28,12},{1,17},{... | collective-permute-start | bytes 393224 | tf_op jit(solution)/shard_map/ppermute | solution.py:32
  322.5 12.0 %collective-permute-start.26 = (bf16[512,128]{1,0:T(8,128)(2,1)S(1)}, bf16[512,128]{1,0:T(8,128)(2,1)S(1)}, u32[]{:S(2)}, u32[]{:S(2)}) collective-permute-start(bf16[512,128]{1,0:T(8,128)(2,1)S(1)} %get-tuple-element.289), channel_id=1, source_target_pairs={{0,8},{4,12},{8,0},{12,4},{16,24},{20,28},{24,16},{28,20},{1,9},{5... | collective-permute-start | bytes 393224 | tf_op jit(solution)/shard_map/ppermute | solution.py:32
  328.2 27.4 %collective-permute-start.32 = (bf16[128,2048]{1,0:T(8,128)(2,1)S(1)}, bf16[128,2048]{1,0:T(8,128)(2,1)S(1)}, u32[]{:S(2)}, u32[]{:S(2)}) collective-permute-start(bf16[128,2048]{1,0:T(8,128)(2,1)S(1)} %add_convert_fusion.2), channel_id=1, source_target_pairs={{0,2},{1,3},{2,0},{3,1},{4,6},{5,7},{6,4},{7,5},{8,10},{9,11},{10,... | collective-permute-start | bytes 1572872 | tf_op jit(solution)/shard_map/ppermute | solution.py:47
  330.1 25.5 %collective-permute-start.31 = (bf16[128,2048]{1,0:T(8,128)(2,1)S(1)}, bf16[128,2048]{1,0:T(8,128)(2,1)S(1)}, u32[]{:S(2)}, u32[]{:S(2)}) collective-permute-start(bf16[128,2048]{1,0:T(8,128)(2,1)S(1)} %get-tuple-element.175), channel_id=1, source_target_pairs={{0,1},{1,0},{2,3},{3,2},{4,5},{5,4},{6,7},{7,6},{8,9},{9,8},{10,11... | collective-permute-start | bytes 1572872 | tf_op jit(solution)/shard_map/ppermute | solution.py:47
  355.6 2.9 collective-permute-start.29
  362.8 19.9 %collective-permute-start.33 = (bf16[512,384]{1,0:T(8,128)(2,1)}, bf16[512,384]{1,0:T(8,128)(2,1)S(1)}, u32[]{:S(2)}, u32[]{:S(2)}) collective-permute-start(bf16[512,384]{1,0:T(8,128)(2,1)} %get-tuple-element.179), channel_id=1, source_target_pairs={{0,8},{4,12},{8,0},{12,4},{16,24},{20,28},{24,16},{28,20},{1,9},{5... | collective-permute-start | bytes 1179656 | tf_op jit(solution)/shard_map/ppermute | solution.py:32
  363.4 22.1 %collective-permute-start.34 = (bf16[512,384]{1,0:T(8,128)(2,1)}, bf16[512,384]{1,0:T(8,128)(2,1)S(1)}, u32[]{:S(2)}, u32[]{:S(2)}) collective-permute-start(bf16[512,384]{1,0:T(8,128)(2,1)} %get-tuple-element.180), channel_id=1, source_target_pairs={{0,16},{4,20},{8,24},{12,28},{16,0},{20,4},{24,8},{28,12},{1,17},{... | collective-permute-start | bytes 1179656 | tf_op jit(solution)/shard_map/ppermute | solution.py:32
  364.7 33.0 %collective-permute-start.35 = (bf16[512,384]{1,0:T(8,128)(2,1)}, bf16[512,384]{1,0:T(8,128)(2,1)S(1)}, u32[]{:S(2)}, u32[]{:S(2)}) collective-permute-start(bf16[512,384]{1,0:T(8,128)(2,1)} %get-tuple-element.181), channel_id=1, source_target_pairs={{0,24},{4,28},{8,16},{12,20},{16,8},{20,12},{24,0},{28,4},{1,25},{... | collective-permute-start | bytes 1179656 | tf_op jit(solution)/shard_map/ppermute | solution.py:32
  367.1 40.7 %collective-permute-start.36 = (bf16[128,2048]{1,0:T(8,128)(2,1)S(1)}, bf16[128,2048]{1,0:T(8,128)(2,1)S(1)}, u32[]{:S(2)}, u32[]{:S(2)}) collective-permute-start(bf16[128,2048]{1,0:T(8,128)(2,1)S(1)} %copy-done.20), channel_id=1, source_target_pairs={{0,1},{1,0},{2,3},{3,2},{4,5},{5,4},{6,7},{7,6},{8,9},{9,8},{10,11... | collective-permute-start | bytes 1572872 | tf_op jit(solution)/shard_map/ppermute | solution.py:47
  367.8 40.1 %collective-permute-start.37 = (bf16[128,2048]{1,0:T(8,128)(2,1)S(1)}, bf16[128,2048]{1,0:T(8,128)(2,1)S(1)}, u32[]{:S(2)}, u32[]{:S(2)}) collective-permute-start(bf16[128,2048]{1,0:T(8,128)(2,1)S(1)} %copy-done.20), channel_id=1, source_target_pairs={{0,2},{1,3},{2,0},{3,1},{4,6},{5,7},{6,4},{7,5},{8,10},{9,11},{10,... | collective-permute-start | bytes 1572872 | tf_op jit(solution)/shard_map/ppermute | solution.py:47
  407.9 19.0 %collective-permute-start.40 = (bf16[1024,2048]{1,0:T(8,128)(2,1)}, bf16[1024,2048]{1,0:T(8,128)(2,1)}, u32[]{:S(2)}, u32[]{:S(2)}) collective-permute-start(bf16[1024,2048]{1,0:T(8,128)(2,1)} %weight_grad.2), channel_id=1, source_target_pairs={{0,4},{4,0},{8,12},{12,8},{16,20},{20,16},{24,28},{28,24},{1,5},{5... | collective-permute-start | bytes 12582920 | tf_op jit(solution)/shard_map/ppermute | solution.py:32
  408.0 14.4 %collective-permute-start.38 = (bf16[128,2048]{1,0:T(8,128)(2,1)S(1)}, bf16[128,2048]{1,0:T(8,128)(2,1)}, u32[]{:S(2)}, u32[]{:S(2)}) collective-permute-start(bf16[128,2048]{1,0:T(8,128)(2,1)S(1)} %collective-permute-done.37), channel_id=1, source_target_pairs={{0,1},{1,0},{2,3},{3,2},{4,5},{5,4},{6,7},{7,6},{8,9},{9,8},{10,11... | collective-permute-start | bytes 1572872 | tf_op jit(solution)/shard_map/ppermute | solution.py:47
  424.7 13.5 %collective-permute-start.39 = (bf16[128,2048]{1,0:T(8,128)(2,1)S(1)}, bf16[128,2048]{1,0:T(8,128)(2,1)S(1)}, u32[]{:S(2)}, u32[]{:S(2)}) collective-permute-start(bf16[128,2048]{1,0:T(8,128)(2,1)S(1)} %get-tuple-element.262), channel_id=1, source_target_pairs={{0,1},{1,0},{2,3},{3,2},{4,5},{5,4},{6,7},{7,6},{8,9},{9,8},{10,11... | collective-permute-start | bytes 1572872 | tf_op jit(solution)/shard_map/ppermute | solution.py:47
  438.2 21.4 %collective-permute-start.41 = (bf16[128,2048]{1,0:T(8,128)(2,1)}, bf16[128,2048]{1,0:T(8,128)(2,1)S(1)}, u32[]{:S(2)}, u32[]{:S(2)}) collective-permute-start(bf16[128,2048]{1,0:T(8,128)(2,1)} %get-tuple-element.198), channel_id=1, source_target_pairs={{0,1},{1,0},{2,3},{3,2},{4,5},{5,4},{6,7},{7,6},{8,9},{9,8},{10,11... | collective-permute-start | bytes 1572872 | tf_op jit(solution)/shard_map/ppermute | solution.py:47
  439.8 24.8 %collective-permute-start.42 = (bf16[128,2048]{1,0:T(8,128)(2,1)S(1)}, bf16[128,2048]{1,0:T(8,128)(2,1)S(1)}, u32[]{:S(2)}, u32[]{:S(2)}) collective-permute-start(bf16[128,2048]{1,0:T(8,128)(2,1)S(1)} %add_convert_fusion), channel_id=1, source_target_pairs={{0,2},{1,3},{2,0},{3,1},{4,6},{5,7},{6,4},{7,5},{8,10},{9,11},{10,... | collective-permute-start | bytes 1572872 | tf_op jit(solution)/shard_map/ppermute | solution.py:47
  441.8 22.8 %copy-start.1 = (bf16[512,2048]{1,0:T(8,128)(2,1)S(1)}, bf16[512,2048]{1,0:T(8,128)(2,1)}, u32[]{:S(2)}) copy-start(bf16[512,2048]{1,0:T(8,128)(2,1)} %pad_maximum_fusion.1.rows_in) | copy-start | bytes 6291460
  441.8 22.8 %copy-start.37 = (f32[1,2048]{1,0:T(1,128)S(1)}, f32[1,2048]{1,0:T(1,128)}, u32[]{:S(2)}) copy-start(f32[1,2048]{1,0:T(1,128)} %get-tuple-element.298) | copy-start | bytes 24580
  441.8 22.8 %copy-start.44 = (f32[128]{0:T(128)S(1)}, f32[128]{0:T(128)}, u32[]{:S(2)}) copy-start(f32[128]{0:T(128)} %copy-done.43) | copy-start | bytes 1540
  443.5 28.9 %collective-permute-start.43 = (bf16[256,2048]{1,0:T(8,128)(2,1)}, bf16[256,2048]{1,0:T(8,128)(2,1)}, u32[]{:S(2)}, u32[]{:S(2)}) collective-permute-start(bf16[256,2048]{1,0:T(8,128)(2,1)} %get-tuple-element.195), channel_id=1, source_target_pairs={{0,8},{4,12},{8,0},{12,4},{16,24},{20,28},{24,16},{28,20},{1,9},{5... | collective-permute-start | bytes 3145736 | tf_op jit(solution)/shard_map/ppermute | solution.py:32
  446.4 45.8 %collective-permute-start.44 = (bf16[256,2048]{1,0:T(8,128)(2,1)}, bf16[256,2048]{1,0:T(8,128)(2,1)}, u32[]{:S(2)}, u32[]{:S(2)}) collective-permute-start(bf16[256,2048]{1,0:T(8,128)(2,1)} %get-tuple-element.196), channel_id=1, source_target_pairs={{0,16},{4,20},{8,24},{12,28},{16,0},{20,4},{24,8},{28,12},{1,17},{... | collective-permute-start | bytes 3145736 | tf_op jit(solution)/shard_map/ppermute | solution.py:32
  446.6 45.7 %collective-permute-start.45 = (bf16[256,2048]{1,0:T(8,128)(2,1)}, bf16[256,2048]{1,0:T(8,128)(2,1)}, u32[]{:S(2)}, u32[]{:S(2)}) collective-permute-start(bf16[256,2048]{1,0:T(8,128)(2,1)} %get-tuple-element.197), channel_id=1, source_target_pairs={{0,24},{4,28},{8,16},{12,20},{16,8},{20,12},{24,0},{28,4},{1,25},{... | collective-permute-start | bytes 3145736 | tf_op jit(solution)/shard_map/ppermute | solution.py:32
  466.0 33.2 %collective-permute-start.46 = (bf16[128,2048]{1,0:T(8,128)(2,1)S(1)}, bf16[128,2048]{1,0:T(8,128)(2,1)}, u32[]{:S(2)}, u32[]{:S(2)}) collective-permute-start(bf16[128,2048]{1,0:T(8,128)(2,1)S(1)} %fusion.30), channel_id=1, source_target_pairs={{0,1},{1,0},{2,3},{3,2},{4,5},{5,4},{6,7},{7,6},{8,9},{9,8},{10,11... | collective-permute-start | bytes 1572872 | tf_op jit(solution)/shard_map/ppermute | solution.py:47
  466.1 33.2 %collective-permute-start.47 = (bf16[128,2048]{1,0:T(8,128)(2,1)S(1)}, bf16[128,2048]{1,0:T(8,128)(2,1)S(1)}, u32[]{:S(2)}, u32[]{:S(2)}) collective-permute-start(bf16[128,2048]{1,0:T(8,128)(2,1)S(1)} %fusion.30), channel_id=1, source_target_pairs={{0,2},{1,3},{2,0},{3,1},{4,6},{5,7},{6,4},{7,5},{8,10},{9,11},{10,... | collective-permute-start | bytes 1572872 | tf_op jit(solution)/shard_map/ppermute | solution.py:47
  499.2 5.3 collective-permute-start.49
  500.7 6.2 %collective-permute-start.50 = (f32[72,128]{1,0:T(8,128)S(1)}, f32[72,128]{1,0:T(8,128)S(1)}, u32[]{:S(2)}, u32[]{:S(2)}) collective-permute-start(f32[72,128]{1,0:T(8,128)S(1)} %concatenate.142), channel_id=1, source_target_pairs={{0,3},{1,2},{2,1},{3,0},{4,7},{5,6},{6,5},{7,4},{8,11},{9,10},{10,... | collective-permute-start | bytes 110600 | tf_op jit(solution)/shard_map/ppermute | solution.py:47
  502.5 4.7 collective-permute-start.48
  507.2 4.0 collective-permute-start.52
  507.6 29.4 %collective-permute-start.51 = (bf16[128,2048]{1,0:T(8,128)(2,1)}, bf16[128,2048]{1,0:T(8,128)(2,1)S(1)}, u32[]{:S(2)}, u32[]{:S(2)}) collective-permute-start(bf16[128,2048]{1,0:T(8,128)(2,1)} %copy-done.22), channel_id=1, source_target_pairs={{0,1},{1,0},{2,3},{3,2},{4,5},{5,4},{6,7},{7,6},{8,9},{9,8},{10,11... | collective-permute-start | bytes 1572872 | tf_op jit(solution)/shard_map/ppermute | solution.py:47
  511.2 4.0 collective-permute-start.53
  515.2 1.2 collective-permute-start.54
  (52 other events, 396.4 us)
Sparse Core Ops, SparseCore 0:
  56.2 37.1 all-gather.2
  95.8 102.7 all-gather.4
  272.3 134.4 reduce-scatter.1

commit v4 on v3

--- a/solution.py
+++ b/solution.py
@@ -217,7 +217,7 @@
     dkv_odd[:, HEAD:] = d_odd[:, HEAD:].astype(bf16)
 
 
-LARGE = pl.CostEstimate(flops=145_000_000_000, bytes_accessed=145_000_000, transcendentals=0)
+LARGE = pl.CostEstimate(flops=180_000_000_000, bytes_accessed=180_000_000, transcendentals=0)
 LITTLE = pl.CostEstimate(flops=1, bytes_accessed=1, transcendentals=0)
 
 
@@ -317,17 +317,15 @@
             small[:, at] = block[depth : depth + 8, :depth].astype(f32)
     part = rows // 4
 
-    @pl.loop(0, 4)
-    def _(quarter):
-        cut = pl.ds(pl.multiple_of(quarter * part, part), part)
+    for quarter in range(4):
+        cut = slice(quarter * part, (quarter + 1) * part)
         normed, _ = norm_parts(rows_in[cut, :].astype(f32))
         a1[cut, :] = (normed * small[0:1, :] + small[2:3, :]).astype(bf16)
 
     width = heads * HEAD
 
-    @pl.loop(0, 3)
-    def _(j):
-        cut = pl.ds(pl.multiple_of(j * width, width), width)
+    for j in range(3):
+        cut = slice(j * width, (j + 1) * width)
         result[:, cut] = jnp.dot(a1[...], weights[:, cut], preferred_element_type=f32).astype(bf16)
 
     for s in range(heads):
@@ -361,57 +359,42 @@
     )(place, rows_in, *blocks)
 
 
-def weight_grad_kernel(flip, depth, place, *refs):
+def weight_grad_kernel(flip, depth, place, rows_in, grads, *refs):
     me = place[0]
-    pairs, refs = (refs[0:2], refs[2:4]), refs[4:]
-    add, outs, whole = (refs[0], refs[1:-1], refs[-1]) if not flip else (None, refs[:-1], refs[-1])
-    count = pairs[0][0].shape[1] // depth // 2
+    count = rows_in.shape[1] // depth // 2
+    outs = refs[:1] if flip else refs[1 : 1 + count]
     if depth % HEAD:
-        left = 0
-        for rows_in, grads in pairs:
-            cols = slice(left, left + grads.shape[1])
-            whole[:, cols] = lax.dot_general(
-                rows_in[...], grads[...], (((0,), (0,)), ((), ())), preferred_element_type=f32
+        whole = refs[-1]
+        whole[...] = lax.dot_general(rows_in[...], grads[...], (((0,), (0,)), ((), ())), preferred_element_type=f32)
+    for slot in range(count):
+        at, here = lanes_of(me, 2 * slot + flip, depth), slice(slot * depth, (slot + 1) * depth)
+        if depth % HEAD:
+            block = whole[at, :]
+        else:
+            block = lax.dot_general(
+                rows_in[:, at], grads[...], (((0,), (0,)), ((), ())), preferred_element_type=f32
             )
-            left = cols.stop
-    else:
-
-        @pl.loop(0, count)
-        def _(slot):
-            at = lanes_of(me, 2 * slot + flip, depth)
-            here = pl.ds(pl.multiple_of(slot * depth, depth), depth)
-            left = 0
-            for rows_in, grads in pairs:
-                cols = slice(left, left + grads.shape[1])
-                whole[here, cols] = lax.dot_general(
-                    rows_in[:, at], grads[...], (((0,), (0,)), ((), ())), preferred_element_type=f32
-                )
-                left = cols.stop
-
-    for slot in range(count):
-        here = slice(slot * depth, (slot + 1) * depth)
-        block = whole[lanes_of(me, 2 * slot + flip, depth), :] if depth % HEAD else whole[here, :]
         if flip:
             outs[0][here, :] = block.astype(bf16)
         else:
-            outs[slot][...] = (block + add[here, :].astype(f32)).astype(bf16)
-
-
-def weight_grad(place, pairs, depth, add=None):
-    width, cols = pairs[0][0].shape[1], sum(grads.shape[1] for _, grads in pairs)
+            outs[slot][...] = (block + refs[0][here, :].astype(f32)).astype(bf16)
+
+
+def weight_grad(place, rows_in, grads, depth, add=None):
+    width, cols = rows_in.shape[1], grads.shape[1]
     count = width // depth // 2
     flip, extra = (1, []) if add is None else (0, [add])
     lines = [count * depth] if add is None else [depth] * count
     results = pl.pallas_call(
         functools.partial(weight_grad_kernel, flip, depth),
         out_shape=tuple(jax.ShapeDtypeStruct((n, cols), bf16) for n in lines),
-        in_specs=[in_smem()] + [in_vmem()] * (4 + len(extra)),
+        in_specs=[in_smem()] + [in_vmem()] * (2 + len(extra)),
         out_specs=(in_vmem(),) * len(lines),
-        scratch_shapes=[pltpu.VMEM((width if depth % HEAD else count * depth, cols), f32)],
+        scratch_shapes=[pltpu.VMEM((width, cols), f32)] if depth % HEAD else [],
         compiler_params=pltpu.CompilerParams(vmem_limit_bytes=58 << 20),
         cost_estimate=LITTLE,
         name="weight_grad",
-    )(place, *pairs[0], *pairs[1], *extra)
+    )(place, rows_in, grads, *extra)
     return results if add is not None else results[0]
 
 
@@ -438,7 +421,7 @@
         out_specs=in_vmem(),
         scratch_shapes=[pltpu.VMEM((depth * len(blocks), grads.shape[1]), bf16)],
         compiler_params=pltpu.CompilerParams(vmem_limit_bytes=58 << 20),
-        cost_estimate=LITTLE,
+        cost_estimate=LARGE,
         name="input_grad",
     )(place, grads, *blocks)
 
@@ -456,7 +439,7 @@
 def pair_grad_of(left, right, other_left, other_right):
     rows, width = left.shape
     cols = right.shape[1]
-    step, half = 256, width // 256
+    step, half = 512, width // 512
     first = pl.BlockSpec((rows, step), lambda i: (0, jnp.minimum(i, half - 1)))
     second = pl.BlockSpec((rows, step), lambda i: (0, jnp.maximum(i - half, 0)))
     return pl.pallas_call(
@@ -494,37 +477,36 @@
     )(pair)
 
 
-def total_kernel(head_cols, *refs):
+def total_kernel(head_cols, out_t, *refs):
     pieces, (qkv, out, square) = refs[:-3], refs[-3:]
-    part = jnp.zeros((1, 1), f32)
-    for j in range(4):
+    value = out_t[...].astype(f32)
+    out[...] = value.T
+    part = jnp.sum(jnp.sum(value * value, axis=0, keepdims=True), axis=1, keepdims=True)
+    for j in range(3):
         cut = slice(j * head_cols, (j + 1) * head_cols)
         value = pieces[0][:, cut].astype(f32)
         for piece in pieces[1:]:
             value = value + piece[:, cut].astype(f32)
         part = part + jnp.sum(jnp.sum(value * value, axis=0, keepdims=True), axis=1, keepdims=True)
-        if j < 3:
-            qkv[j] = value
-        else:
-            out[...] = value.T
+        qkv[j] = value
     square[...] = jnp.broadcast_to(part, square.shape)
 
 
-def total_of(pieces, head_cols):
+def total_of(pieces, out_t, head_cols):
     depth = pieces[0].shape[0]
     shapes = ((3, depth, head_cols), (head_cols, depth), (8, HEAD))
     return pl.pallas_call(
         functools.partial(total_kernel, head_cols),
         out_shape=tuple(jax.ShapeDtypeStruct(s, f32) for s in shapes),
-        in_specs=[in_vmem()] * len(pieces),
+        in_specs=[in_vmem()] * (1 + len(pieces)),
         out_specs=(in_vmem(),) * 3,
         compiler_params=pltpu.CompilerParams(vmem_limit_bytes=58 << 20),
         cost_estimate=LITTLE,
         name="total",
-    )(*pieces)
-
-
-ADAM_STEPS = 8
+    )(out_t, *pieces)
+
+
+ADAM_STEPS = 4
 
 
 def adam_kernel(count, factor, decays, *refs):
@@ -720,6 +702,8 @@
     mixed, grad_attn = lax.optimization_barrier((mixed, grad_attn))
     block_out = (y1 + tp_scatter(mixed)).astype(bf16)
 
+    grad_outw = lax.dot_general(grad_attn, attn_vals, (((0,), (0,)), ((), ())), preferred_element_type=f32)
+    grad_outw = grad_outw.astype(bf16)
     grad_vals = jnp.dot(grad_attn, out_full, preferred_element_type=f32).astype(bf16)
 
     grads = []
@@ -741,6 +725,7 @@
     for s in range(1, heads):
         back.append(ctx_xor(grad_own[s], s << 1))
     back = jnp.concatenate(back, axis=0)
+    back, grad_outw = lax.optimization_barrier((back, grad_outw))
     by_head = [
         lax.dynamic_slice_in_dim(back, jnp.bitwise_xor(my_head, h) * rows, rows, 0) for h in range(heads)
     ]
@@ -748,24 +733,24 @@
         [by_head[h][:, j * HEAD : (j + 1) * HEAD] for j in range(3) for h in range(heads)], axis=1
     )
     chips = list(range(0, ctx_count, 2))
-    pairs = ((a1, grad_qkv_in), (grad_attn, attn_vals))
-    sent = weight_grad(place, pairs, ctx_cols)
+    sent = weight_grad(place, a1, grad_qkv_in, ctx_cols)
     sent, later, block_out = lax.optimization_barrier((sent, grad_qkv_in, tp_gather_first(block_out)))
     got = ctx_xor(sent, 1)
+    grad_outw, pair_shard = lax.optimization_barrier((grad_outw, pair_shard))
+    out_shard = lax.psum_scatter(grad_outw, "ctx", scatter_dimension=0, tiled=True)
     grad_h1 = input_grad(place, later, qkv_blocks, ctx_cols)
     block_out, grad_h1 = lax.optimization_barrier((tp_gather_last(block_out), grad_h1))
-    got, pair_shard = lax.optimization_barrier((got, pair_shard))
-    summed = weight_grad(place, pairs, ctx_cols, got)
+    summed = weight_grad(place, a1, grad_qkv_in, ctx_cols, got)
     grad_h1 = tp_send(grad_h1, summed)
     up_grad, down_grad, square = widen(pair_shard)
     arrived = [ctx_xor(summed[slot], mask) for slot, mask in enumerate(chips) if slot]
-    grad_h1, _, up_grad = lax.optimization_barrier((grad_h1, summed, up_grad))
+    grad_h1, _, up_grad, out_shard = lax.optimization_barrier((grad_h1, summed, up_grad, out_shard))
     grad_h1 = tp_total(grad_h1)
     block_out = slots_to_rows(block_out, tp_place)
     normed1, rstd1 = norm_parts(x_own)
     dx1, dg1, dc1 = norm_back(grad_h1, normed1, rstd1, gain_one)
     grad_tokens = (grad_y1 + dx1).astype(bf16)
-    qkv_grad, out_grad, more = total_of([summed[0], *arrived], head_cols)
+    qkv_grad, out_grad, more = total_of([summed[0], *arrived], out_shard, head_cols)
     square = square[0, 0] + more[0, 0]
     lines = jnp.stack((dg1, dg2, dc1, dc2)).reshape(-1, HEAD)
     sent = jnp.concatenate((lines, jnp.full((8, HEAD), square, f32)), axis=0)

time: 548 us -> 540 us (0.985)
  Pallas kernels: 120 us -> 107 us
  waiting for transfers between devices: 245 us -> 235 us
    ppermute x28, waiting for transfers between devices: 124 us -> 112 us  [ctx_xor(): lax.ppermute(value, 'ctx', [(place, place ^ mask) for place in range(coun...]
    pallas_call x2, Pallas kernels: 17.8 us -> 11.4 us  [weight_grad(): pl.pallas_call(functools.partial(weight_grad_kernel, flip, depth), out_sh...]
    unnamed x143 -> x128, local copies, waits for them, and re-layouts: 14.4 us -> 15.1 us
  transfers between devices with their start and end apart: 58 -> 59, of which waited for: 38 -> 38; matrix products, arithmetic and copies ran while one was open for 13% -> 15% of each run, Pallas kernels for 22% -> 20%
where the time goes in v4:
time: 540 us; the launch traced here: 534 us
  waiting for transfers between devices  235 us (44%)
  Pallas kernels  107 us (20%)
  starting transfers between devices  60.8 us (11%)
  matrix products  42.6 us (8%)
  local copies, waits for them, and re-layouts  35.2 us (7%)
  other arithmetic  34.3 us (6%)
  between operations  20.3 us (4%)
    ppermute x27, waiting for transfers between devices, tp_xor(): lax.ppermute(value, 'tp', [(place, place ^ mask) for place in range(count)])  123 us
    ppermute x28, waiting for transfers between devices, ctx_xor(): lax.ppermute(value, 'ctx', [(place, place ^ mask) for place in range(coun...  112 us
    ppermute x27, starting transfers between devices, tp_xor(): lax.ppermute(value, 'tp', [(place, place ^ mask) for place in range(count)])  36.1 us
    ppermute x28, starting transfers between devices, ctx_xor(): lax.ppermute(value, 'ctx', [(place, place ^ mask) for place in range(coun...  24.6 us
    pallas_call x1, Pallas kernels, attention_backward(): pl.pallas_call(functools.partial(backward_kernel, rows, chunks, HEAD if e...  20.7 us
    unnamed x128, local copies, waits for them, and re-layouts  15.1 us
    pallas_call x1, Pallas kernels, adam(): pl.pallas_call(functools.partial(adam_kernel, len(groups)), grid=(ADAM_ST...  14.9 us
    pallas_call x1, Pallas kernels, pair_grad_of(): pl.pallas_call(functools.partial(pair_grad_kernel, half), grid=(2 * half,...  14.9 us
  transfers between devices with their start and end apart: 59, of which 38 were waited for; matrix products, arithmetic and copies ran while one was open for 15% of the time, Pallas kernels for 20%

profile of v4, /device:TPU:0, one launch (start us, length us, event | category | flops | bytes accessed | tf_op | source)
XLA Modules:
  0.0 534.4 jit_solution(16458622358064913742)
XLA Ops:
  11.2 2.9 collective-permute-start
  15.8 3.0 constant_dynamic-slice_fusion.24
  20.9 3.2 pad_maximum_fusion.1.rows_in
  25.6 8.3 %collective-permute-done.refs_2_ = bf16[272,1536]{1,0:T(8,128)(2,1)} collective-permute-done((bf16[272,1536]{1,0:T(8,128)(2,1)}, bf16[272,1536]{1,0:T(8,128)(2,1)}, u32[]{:S(2)}, u32[]{:S(2)}) %collective-permute-start) | collective-permute-done | bytes 835616 | tf_op jit(solution)/shard_map/ppermute | solution.py:32
  33.8 19.5 %collective-permute-done.3.refs_4_ = bf16[272,1536]{1,0:T(8,128)(2,1)} collective-permute-done((bf16[272,1536]{1,0:T(8,128)(2,1)}, bf16[272,1536]{1,0:T(8,128)(2,1)}, u32[]{:S(2)}, u32[]{:S(2)}) %collective-permute-start.3) | collective-permute-done | bytes 835616 | tf_op jit(solution)/shard_map/ppermute | solution.py:32
  53.9 2.0 collective-permute-done.4.refs_5_
  58.0 10.1 %project.1 = (bf16[512,384]{1,0:T(8,128)(2,1)}, bf16[512,384]{1,0:T(8,128)(2,1)}, bf16[512,384]{1,0:T(8,128)(2,1)}, bf16[512,384]{1,0:T(8,128)(2,1)}, bf16[512,2048]{1,0:T(8,128)(2,1)}, /*index=5*/f32[8,2048]{1,0:T(8,128)}) custom-call(s32[2]{0:T(128)} %pad_add_fusion.2.place, bf16[512,2048]{1,0:T(8,128)(2,1)} %pad_maximum_fusion.1.rows_in, ...), custom_call_target="tpu_custom_call" | custom-call | flops 1 | bytes 1 | tf_op jit(solution)/shard_map/project/pallas_call | solution.py:346
  68.2 2.0 collective-permute-start.8
  71.7 10.7 %collective-permute-done.7 = bf16[512,384]{1,0:T(8,128)(2,1)S(1)} collective-permute-done((bf16[512,384]{1,0:T(8,128)(2,1)}, bf16[512,384]{1,0:T(8,128)(2,1)S(1)}, u32[]{:S(2)}, u32[]{:S(2)}) %collective-permute-start.7) | collective-permute-done | bytes 393248 | tf_op jit(solution)/shard_map/ppermute | solution.py:32
  82.4 2.5 collective-permute-done.8
  84.9 9.7 %collective-permute-done.9 = bf16[512,384]{1,0:T(8,128)(2,1)S(1)} collective-permute-done((bf16[512,384]{1,0:T(8,128)(2,1)}, bf16[512,384]{1,0:T(8,128)(2,1)S(1)}, u32[]{:S(2)}, u32[]{:S(2)}) %collective-permute-start.9) | collective-permute-done | bytes 393248 | tf_op jit(solution)/shard_map/ppermute | solution.py:32
  99.7 13.6 %attention_forward.1 = (bf16[2048,128]{1,0:T(8,128)(2,1)}, f32[128,2048]{1,0:T(8,128)}, f32[1,2048]{1,0:T(1,128)}) custom-call(s32[2]{0:T(128)} %pad_add_fusion.2.place, s32[2,4]{1,0:T(2,128)} %pad_add_fusion.1.tiles, s32[2,2048]{1,0:T(2,128)} %pad_add_fusion.span, bf16[2048,384]{1,0:T(8,128)(2,1)} %copy-done.2, bf16[2048,256]{1,0:T(8,128)(2,1)} %copy-done.6), custom_call_target="tpu_custom_call" | custom-call | flops 1 | bytes 1 | tf_op jit(solution)/shard_map/attention_forward/pallas_call | solution.py:235
  118.1 6.4 %collective-permute-done.13 = bf16[512,128]{1,0:T(8,128)(2,1)S(1)} collective-permute-done((bf16[512,128]{1,0:T(8,128)(2,1)S(1)}, bf16[512,128]{1,0:T(8,128)(2,1)S(1)}, u32[]{:S(2)}, u32[]{:S(2)}) %collective-permute-start.13) | collective-permute-done | bytes 131104 | tf_op jit(solution)/shard_map/ppermute | solution.py:32
  124.5 2.8 collective-permute-done.12
  127.3 2.0 collective-permute-done.11
  129.4 3.0 convolution_convert_fusion.1
  134.3 12.7 %collective-permute-done.14 = bf16[128,2048]{1,0:T(8,128)(2,1)S(1)} collective-permute-done((bf16[128,2048]{1,0:T(8,128)(2,1)S(1)}, bf16[128,2048]{1,0:T(8,128)(2,1)S(1)}, u32[]{:S(2)}, u32[]{:S(2)}) %collective-permute-start.14) | collective-permute-done | bytes 524320 | tf_op jit(solution)/shard_map/ppermute | solution.py:47
  147.1 2.7 collective-permute-start.16
  152.9 20.2 %collective-permute-done.16 = bf16[128,2048]{1,0:T(8,128)(2,1)S(1)} collective-permute-done((bf16[128,2048]{1,0:T(8,128)(2,1)S(1)}, bf16[128,2048]{1,0:T(8,128)(2,1)S(1)}, u32[]{:S(2)}, u32[]{:S(2)}) %collective-permute-start.16) | collective-permute-done | bytes 524320 | tf_op jit(solution)/shard_map/ppermute | solution.py:47
  177.3 2.4 collective-permute-start.17
  179.7 20.1 %collective-permute-done.18 = bf16[128,2048]{1,0:T(8,128)(2,1)} collective-permute-done((bf16[128,2048]{1,0:T(8,128)(2,1)S(1)}, bf16[128,2048]{1,0:T(8,128)(2,1)}, u32[]{:S(2)}, u32[]{:S(2)}) %collective-permute-start.18) | collective-permute-done | bytes 524320 | tf_op jit(solution)/shard_map/ppermute | solution.py:47
  199.8 10.1 %fusion.6 = f32[512,2048]{1,0:T(8,128)} fusion(bf16[2048,4096]{0,1:T(8,128)(2,1)} %all-gather.5.cloned.1.call-done, bf16[128,2048]{1,0:T(8,128)(2,1)S(1)} %get-tuple-element.281, bf16[128,2048]{1,0:T(8,128)(2,1)} %get-tuple-element.282, bf16[128,2048]{1,0:T(8,128)(2,1)S(1)} %get-tuple-element.280, bf16[128,2048]{1,0:T(8,128)(2,1)S(1)} %get-tuple-element.279), kind=kOutput, calls=%fused_computation.6 | convolution fusion | flops 4303355904 | bytes 14680064 | tf_op jit(solution)/shard_map/dot_general | solution.py:680
  209.9 2.2 collective-permute-done.19
  215.7 11.0 %multiply_convert_fusion = (bf16[512,2048]{1,0:T(8,128)(2,1)}, bf16[512,2048]{1,0:T(8,128)(2,1)S(1)}) fusion(f32[512,2048]{1,0:T(8,128)} %fusion.6, bf16[512,2048]{1,0:T(8,128)(2,1)S(1)} %constant_dynamic-update-slice_fusion.21.left, bf16[2048,4096]{0,1:T(8,128)(2,1)} %all-gather.5.cloned.1.call-done), kind=kOutput, calls=%fused_computation.15 | convolution fusion | flops 4307550208 | bytes 18874368 | tf_op jit(solution)/shard_map/dot_general | solution.py:684
  226.7 4.9 fusion.17
  234.0 10.8 %collective-permute-done.20 = bf16[128,2048]{1,0:T(8,128)(2,1)S(1)} collective-permute-done((bf16[128,2048]{1,0:T(8,128)(2,1)S(1)}, bf16[128,2048]{1,0:T(8,128)(2,1)S(1)}, u32[]{:S(2)}, u32[]{:S(2)}) %collective-permute-start.20) | collective-permute-done | bytes 524320 | tf_op jit(solution)/shard_map/ppermute | solution.py:47
  245.8 4.2 collective-permute-start.22
  252.8 14.9 %pair_grad.1 = bf16[2,2048,2048]{2,1,0:T(8,128)(2,1)} custom-call(bf16[512,2048]{1,0:T(8,128)(2,1)} %copy-done.9, bf16[512,2048]{1,0:T(8,128)(2,1)} %copy-done.10, bf16[512,2048]{1,0:T(8,128)(2,1)} %pad_maximum_fusion.2.other_left, bf16[512,2048]{1,0:T(8,128)(2,1)} %get-tuple-element.165.other_right), custom_call_target="tpu_custom_call" | custom-call | flops 1 | bytes 1 | tf_op jit(solution)/shard_map/pair_grad/pallas_call | solution.py:445
  267.8 4.4 collective-permute-done.22
  272.9 2.0 convert_add_fusion.2
  277.5 2.6 collective-permute-start.23
  280.1 21.7 %collective-permute-done.24 = bf16[128,2048]{1,0:T(8,128)(2,1)S(1)} collective-permute-done((bf16[128,2048]{1,0:T(8,128)(2,1)S(1)}, bf16[128,2048]{1,0:T(8,128)(2,1)S(1)}, u32[]{:S(2)}, u32[]{:S(2)}) %collective-permute-start.24) | collective-permute-done | bytes 524320 | tf_op jit(solution)/shard_map/ppermute | solution.py:47
  301.8 8.5 %fusion.14 = bf16[512,2048]{1,0:T(8,128)(2,1)S(1)} fusion(bf16[512,2048]{1,0:T(8,128)(2,1)} %get-tuple-element.165.other_right, bf16[2048,4096]{0,1:T(8,128)(2,1)} %all-gather.5.cloned.1.call-done), kind=kOutput, calls=%fused_computation.17 | convolution fusion | flops 4296015872 | bytes 12582912 | tf_op jit(solution)/shard_map/dot_general | solution.py:701
  310.3 4.5 collective-permute-done.25
  315.5 2.0 copy-done.44
  322.5 5.0 collective-permute-done.30
  327.5 1.9 collective-permute-start.32
  330.9 2.8 collective-permute-done.26
  334.5 20.7 %attention_backward.1 = (bf16[2048,128]{1,0:T(8,128)(2,1)}, f32[2048,256]{1,0:T(8,128)}, bf16[2048,256]{1,0:T(8,128)(2,1)}) custom-call(s32[2]{0:T(128)} %pad_add_fusion.2.place, s32[2,4]{1,0:T(2,128)} %pad_add_fusion.1.tiles, s32[2,2048]{1,0:T(2,128)} %pad_add_fusion.span, bf16[2048,384]{1,0:T(8,128)(2,1)} %copy-done.2, ...), custom_call_target="tpu_custom_call" | custom-call | flops 1 | bytes 1 | tf_op jit(solution)/shard_map/attention_backward/pallas_call | solution.py:258
  359.1 4.0 merge.1
  364.6 2.0 collective-permute-start.33
  366.6 3.8 convolution_convert_fusion
  370.4 1.9 collective-permute-start.37
  372.3 12.2 %collective-permute-done.35 = bf16[512,384]{1,0:T(8,128)(2,1)S(1)} collective-permute-done((bf16[512,384]{1,0:T(8,128)(2,1)}, bf16[512,384]{1,0:T(8,128)(2,1)S(1)}, u32[]{:S(2)}, u32[]{:S(2)}) %collective-permute-start.35) | collective-permute-done | bytes 393248 | tf_op jit(solution)/shard_map/ppermute | solution.py:32
  384.5 7.4 %collective-permute-done.34 = bf16[512,384]{1,0:T(8,128)(2,1)} collective-permute-done((bf16[512,384]{1,0:T(8,128)(2,1)}, bf16[512,384]{1,0:T(8,128)(2,1)}, u32[]{:S(2)}, u32[]{:S(2)}) %collective-permute-start.34) | collective-permute-done | bytes 393248 | tf_op jit(solution)/shard_map/ppermute | solution.py:32
  392.0 7.6 %collective-permute-done.33 = bf16[512,384]{1,0:T(8,128)(2,1)} collective-permute-done((bf16[512,384]{1,0:T(8,128)(2,1)}, bf16[512,384]{1,0:T(8,128)(2,1)}, u32[]{:S(2)}, u32[]{:S(2)}) %collective-permute-start.33) | collective-permute-done | bytes 393248 | tf_op jit(solution)/shard_map/ppermute | solution.py:32
  402.6 5.6 %weight_grad.2 = bf16[1024,1536]{1,0:T(8,128)(2,1)} custom-call(s32[2]{0:T(128)} %pad_add_fusion.2.place, bf16[512,2048]{1,0:T(8,128)(2,1)} %get-tuple-element.144.rows_in, bf16[512,1536]{1,0:T(8,128)(2,1)} %copy-done.5), custom_call_target="tpu_custom_call" | custom-call | flops 1 | bytes 1 | tf_op jit(solution)/shard_map/weight_grad/pallas_call | solution.py:388
  409.3 9.3 %input_grad.1 = bf16[512,2048]{1,0:T(8,128)(2,1)} custom-call(s32[2]{0:T(128)} %pad_add_fusion.2.place, bf16[512,1536]{1,0:T(8,128)(2,1)} %copy-done.5, bf16[272,1536]{1,0:T(8,128)(2,1)} %pad_maximum_fusion.7.refs_0_, bf16[272,1536]{1,0:T(8,128)(2,1)} %collective-permute-done.1.refs_1_, bf16[272,1536]{1,0:T(8,128)(2,1)} %collective-permute-done.refs_2_, ...), custom_call_target="tpu_custom_call" | custom-call | flops 179999997952 | bytes 180000000 | tf_op jit(solution)/shard_map/input_grad/pallas_call | solution.py:417
  418.6 3.8 collective-permute-done.38
  422.4 2.3 fusion.55
  427.0 5.8 %weight_grad.3 = (bf16[256,1536]{1,0:T(8,128)(2,1)}, bf16[256,1536]{1,0:T(8,128)(2,1)}, bf16[256,1536]{1,0:T(8,128)(2,1)}, bf16[256,1536]{1,0:T(8,128)(2,1)}) custom-call(s32[2]{0:T(128)} %pad_add_fusion.2.place, bf16[512,2048]{1,0:T(8,128)(2,1)} %get-tuple-element.144.rows_in, bf16[512,1536]{1,0:T(8,128)(2,1)} %copy-done.5, ...), custom_call_target="tpu_custom_call" | custom-call | flops 1 | bytes 1 | tf_op jit(solution)/shard_map/weight_grad/pallas_call | solution.py:388
  432.7 4.1 collective-permute-done.39
  438.4 2.9 collective-permute-start.42
  442.9 1.9 constant_dynamic-update-slice_fusion.26
  448.3 3.7 widen.1
  452.1 6.9 %collective-permute-done.41 = bf16[128,2048]{1,0:T(8,128)(2,1)S(1)} collective-permute-done((bf16[128,2048]{1,0:T(8,128)(2,1)}, bf16[128,2048]{1,0:T(8,128)(2,1)S(1)}, u32[]{:S(2)}, u32[]{:S(2)}) %collective-permute-start.41) | collective-permute-done | bytes 524320 | tf_op jit(solution)/shard_map/ppermute | solution.py:47
  459.0 3.1 collective-permute-done.42
  463.9 2.4 fusion.30
  466.3 3.5 collective-permute-start.47
  474.6 7.7 %collective-permute-done.44.refs_2_ = bf16[256,1536]{1,0:T(8,128)(2,1)} collective-permute-done((bf16[256,1536]{1,0:T(8,128)(2,1)}, bf16[256,1536]{1,0:T(8,128)(2,1)}, u32[]{:S(2)}, u32[]{:S(2)}) %collective-permute-start.44) | collective-permute-done | bytes 786464 | tf_op jit(solution)/shard_map/ppermute | solution.py:32
  482.3 4.0 total.1
  489.9 2.2 collective-permute-start.50
  501.0 3.2 collective-permute-done.53
  508.1 14.9 %adam.1 = (f32[768,512]{1,0:T(8,128)}, f32[768,512]{1,0:T(8,128)}, f32[768,512]{1,0:T(8,128)}, f32[512,256]{1,0:T(8,128)}, f32[512,256]{1,0:T(8,128)}, /*index=5...) custom-call(f32[1]{0:T(128)} %bitcast.38.factor, ...), custom_call_target="tpu_custom_call" | custom-call | flops 1 | bytes 1 | tf_op jit(solution)/shard_map/adam/pallas_call | solution.py:530
  (322 shorter events, 93.7 us)
Async XLA Ops:
  7.2 122.2 %all-gather.3.cloned.1.call-start = ((), (), s32[]{:S(2)}) async-start(), calls=%async_computation.2 | async-start | bytes 2359296 | tf_op jit(solution)/shard_map/all_gather | solution.py:632
  11.2 22.7 %collective-permute-start = (bf16[272,1536]{1,0:T(8,128)(2,1)}, bf16[272,1536]{1,0:T(8,128)(2,1)}, u32[]{:S(2)}, u32[]{:S(2)}) collective-permute-start(bf16[272,1536]{1,0:T(8,128)(2,1)} %pad_maximum_fusion.7.refs_0_), channel_id=1, source_target_pairs={{0,8},{4,12},{8,0},{12,4},{16,24},{20,28},{24,16},{28,20},{1,9},{5... | collective-permute-start | bytes 2506760 | tf_op jit(solution)/shard_map/ppermute | solution.py:32
  14.1 39.8 %collective-permute-start.1 = (bf16[272,1536]{1,0:T(8,128)(2,1)}, bf16[272,1536]{1,0:T(8,128)(2,1)}, u32[]{:S(2)}, u32[]{:S(2)}) collective-permute-start(bf16[272,1536]{1,0:T(8,128)(2,1)} %pad_maximum_fusion.7.refs_0_), channel_id=1, source_target_pairs={{0,4},{4,0},{8,12},{12,8},{16,20},{20,16},{24,28},{28,24},{1,5},{5... | collective-permute-start | bytes 2506760 | tf_op jit(solution)/shard_map/ppermute | solution.py:32
  14.1 39.2 %collective-permute-start.3 = (bf16[272,1536]{1,0:T(8,128)(2,1)}, bf16[272,1536]{1,0:T(8,128)(2,1)}, u32[]{:S(2)}, u32[]{:S(2)}) collective-permute-start(bf16[272,1536]{1,0:T(8,128)(2,1)} %pad_maximum_fusion.7.refs_0_), channel_id=1, source_target_pairs={{0,16},{4,20},{8,24},{12,28},{16,0},{20,4},{24,8},{28,12},{1,17},{... | collective-permute-start | bytes 2506760 | tf_op jit(solution)/shard_map/ppermute | solution.py:32
  15.6 37.7 %collective-permute-start.5 = (bf16[272,1536]{1,0:T(8,128)(2,1)}, bf16[272,1536]{1,0:T(8,128)(2,1)}, u32[]{:S(2)}, u32[]{:S(2)}) collective-permute-start(bf16[272,1536]{1,0:T(8,128)(2,1)} %pad_maximum_fusion.7.refs_0_), channel_id=1, source_target_pairs={{0,24},{4,28},{8,16},{12,20},{16,8},{20,12},{24,0},{28,4},{1,25},{... | collective-permute-start | bytes 2506760 | tf_op jit(solution)/shard_map/ppermute | solution.py:32
  33.8 20.0 %collective-permute-start.2 = (bf16[272,1536]{1,0:T(8,128)(2,1)}, bf16[272,1536]{1,0:T(8,128)(2,1)S(1)}, u32[]{:S(2)}, u32[]{:S(2)}) collective-permute-start(bf16[272,1536]{1,0:T(8,128)(2,1)} %collective-permute-done.refs_2_), channel_id=1, source_target_pairs={{0,4},{4,0},{8,12},{12,8},{16,20},{20,16},{24,28},{28,24},{1,5},{5... | collective-permute-start | bytes 2506760 | tf_op jit(solution)/shard_map/ppermute | solution.py:32
  53.3 2.6 collective-permute-start.4
  53.3 3.8 collective-permute-start.6
  57.1 142.7 %all-gather.5.cloned.1.call-start = ((), (), s32[]{:S(2)}) async-start(), calls=%async_computation.3 | async-start | bytes 18874368 | tf_op jit(solution)/shard_map/all_gather | solution.py:656
  68.1 26.6 %copy-start.46 = (s32[4]{0:T(128)S(1)}, s32[4]{0:T(128)}, u32[]{:S(2)}) copy-start(s32[4]{0:T(128)} %param.42) | copy-start | bytes 52
  68.2 27.5 %copy-start.25 = (bf16[512,384]{1,0:T(8,128)(2,1)S(1)}, bf16[512,384]{1,0:T(8,128)(2,1)}, u32[]{:S(2)}) copy-start(bf16[512,384]{1,0:T(8,128)(2,1)} %get-tuple-element.150) | copy-start | bytes 1179652
  68.2 14.3 %collective-permute-start.7 = (bf16[512,384]{1,0:T(8,128)(2,1)}, bf16[512,384]{1,0:T(8,128)(2,1)S(1)}, u32[]{:S(2)}, u32[]{:S(2)}) collective-permute-start(bf16[512,384]{1,0:T(8,128)(2,1)} %get-tuple-element.146), channel_id=1, source_target_pairs={{0,8},{4,12},{8,0},{12,4},{16,24},{20,28},{24,16},{28,20},{1,9},{5... | collective-permute-start | bytes 1179656 | tf_op jit(solution)/shard_map/ppermute | solution.py:32
  68.2 16.7 %collective-permute-start.8 = (bf16[512,384]{1,0:T(8,128)(2,1)}, bf16[512,384]{1,0:T(8,128)(2,1)S(1)}, u32[]{:S(2)}, u32[]{:S(2)}) collective-permute-start(bf16[512,384]{1,0:T(8,128)(2,1)} %get-tuple-element.147), channel_id=1, source_target_pairs={{0,16},{4,20},{8,24},{12,28},{16,0},{20,4},{24,8},{28,12},{1,17},{... | collective-permute-start | bytes 1179656 | tf_op jit(solution)/shard_map/ppermute | solution.py:32
  70.3 24.3 %collective-permute-start.9 = (bf16[512,384]{1,0:T(8,128)(2,1)}, bf16[512,384]{1,0:T(8,128)(2,1)S(1)}, u32[]{:S(2)}, u32[]{:S(2)}) collective-permute-start(bf16[512,384]{1,0:T(8,128)(2,1)} %get-tuple-element.148), channel_id=1, source_target_pairs={{0,24},{4,28},{8,16},{12,20},{16,8},{20,12},{24,0},{28,4},{1,25},{... | collective-permute-start | bytes 1179656 | tf_op jit(solution)/shard_map/ppermute | solution.py:32
  94.6 314.7 %reduce-scatter.3.cloned.1.call-start = ((), (), s32[]{:S(2)}) async-start(), calls=%async_computation.4 | async-start | bytes 18874368 | tf_op jit(solution)/shard_map/reduce_scatter | solution.py:694
  96.0 2.7 collective-permute-start.10
  114.5 10.0 %collective-permute-start.13 = (bf16[512,128]{1,0:T(8,128)(2,1)S(1)}, bf16[512,128]{1,0:T(8,128)(2,1)S(1)}, u32[]{:S(2)}, u32[]{:S(2)}) collective-permute-start(bf16[512,128]{1,0:T(8,128)(2,1)S(1)} %get-tuple-element.301), channel_id=1, source_target_pairs={{0,24},{4,28},{8,16},{12,20},{16,8},{20,12},{24,0},{28,4},{1,25},{... | collective-permute-start | bytes 393224 | tf_op jit(solution)/shard_map/ppermute | solution.py:32
  115.3 11.9 %collective-permute-start.12 = (bf16[512,128]{1,0:T(8,128)(2,1)S(1)}, bf16[512,128]{1,0:T(8,128)(2,1)S(1)}, u32[]{:S(2)}, u32[]{:S(2)}) collective-permute-start(bf16[512,128]{1,0:T(8,128)(2,1)S(1)} %get-tuple-element.302), channel_id=1, source_target_pairs={{0,16},{4,20},{8,24},{12,28},{16,0},{20,4},{24,8},{28,12},{1,17},{... | collective-permute-start | bytes 393224 | tf_op jit(solution)/shard_map/ppermute | solution.py:32
  116.6 12.6 %collective-permute-start.11 = (bf16[512,128]{1,0:T(8,128)(2,1)S(1)}, bf16[512,128]{1,0:T(8,128)(2,1)S(1)}, u32[]{:S(2)}, u32[]{:S(2)}) collective-permute-start(bf16[512,128]{1,0:T(8,128)(2,1)S(1)} %get-tuple-element.303), channel_id=1, source_target_pairs={{0,8},{4,12},{8,0},{12,4},{16,24},{20,28},{24,16},{28,20},{1,9},{5... | collective-permute-start | bytes 393224 | tf_op jit(solution)/shard_map/ppermute | solution.py:32
  132.5 14.5 %collective-permute-start.14 = (bf16[128,2048]{1,0:T(8,128)(2,1)S(1)}, bf16[128,2048]{1,0:T(8,128)(2,1)S(1)}, u32[]{:S(2)}, u32[]{:S(2)}) collective-permute-start(bf16[128,2048]{1,0:T(8,128)(2,1)S(1)} %get-tuple-element.284), channel_id=1, source_target_pairs={{0,1},{1,0},{2,3},{3,2},{4,5},{5,4},{6,7},{7,6},{8,9},{9,8},{10,11... | collective-permute-start | bytes 1572872 | tf_op jit(solution)/shard_map/ppermute | solution.py:47
  147.1 26.0 %collective-permute-start.16 = (bf16[128,2048]{1,0:T(8,128)(2,1)S(1)}, bf16[128,2048]{1,0:T(8,128)(2,1)S(1)}, u32[]{:S(2)}, u32[]{:S(2)}) collective-permute-start(bf16[128,2048]{1,0:T(8,128)(2,1)S(1)} %add_convert_fusion.5), channel_id=1, source_target_pairs={{0,2},{1,3},{2,0},{3,1},{4,6},{5,7},{6,4},{7,5},{8,10},{9,11},{10,... | collective-permute-start | bytes 1572872 | tf_op jit(solution)/shard_map/ppermute | solution.py:47
  149.8 23.5 %collective-permute-start.15 = (bf16[128,2048]{1,0:T(8,128)(2,1)S(1)}, bf16[128,2048]{1,0:T(8,128)(2,1)S(1)}, u32[]{:S(2)}, u32[]{:S(2)}) collective-permute-start(bf16[128,2048]{1,0:T(8,128)(2,1)S(1)} %get-tuple-element.156), channel_id=1, source_target_pairs={{0,1},{1,0},{2,3},{3,2},{4,5},{5,4},{6,7},{7,6},{8,9},{9,8},{10,11... | collective-permute-start | bytes 1572872 | tf_op jit(solution)/shard_map/ppermute | solution.py:47
  151.4 21.9 %copy-start.37 = (f32[128]{0:T(128)}, f32[128]{0:T(128)S(1)}, u32[]{:S(2)}) copy-start(f32[128]{0:T(128)S(1)} %broadcast_multiply_fusion.2) | copy-start | bytes 1540
  174.8 25.0 %collective-permute-start.18 = (bf16[128,2048]{1,0:T(8,128)(2,1)S(1)}, bf16[128,2048]{1,0:T(8,128)(2,1)}, u32[]{:S(2)}, u32[]{:S(2)}) collective-permute-start(bf16[128,2048]{1,0:T(8,128)(2,1)S(1)} %add_convert_fusion.4), channel_id=1, source_target_pairs={{0,2},{1,3},{2,0},{3,1},{4,6},{5,7},{6,4},{7,5},{8,10},{9,11},{10,... | collective-permute-start | bytes 1572872 | tf_op jit(solution)/shard_map/ppermute | solution.py:47
  177.3 32.7 %collective-permute-start.17 = (bf16[128,2048]{1,0:T(8,128)(2,1)S(1)}, bf16[128,2048]{1,0:T(8,128)(2,1)}, u32[]{:S(2)}, u32[]{:S(2)}) collective-permute-start(bf16[128,2048]{1,0:T(8,128)(2,1)S(1)} %add_convert_fusion.4), channel_id=1, source_target_pairs={{0,1},{1,0},{2,3},{3,2},{4,5},{5,4},{6,7},{7,6},{8,9},{9,8},{10,11... | collective-permute-start | bytes 1572872 | tf_op jit(solution)/shard_map/ppermute | solution.py:47
  199.8 12.3 %collective-permute-start.19 = (bf16[128,2048]{1,0:T(8,128)(2,1)}, bf16[128,2048]{1,0:T(8,128)(2,1)}, u32[]{:S(2)}, u32[]{:S(2)}) collective-permute-start(bf16[128,2048]{1,0:T(8,128)(2,1)} %collective-permute-done.18), channel_id=1, source_target_pairs={{0,1},{1,0},{2,3},{3,2},{4,5},{5,4},{6,7},{7,6},{8,9},{9,8},{10,11... | collective-permute-start | bytes 1572872 | tf_op jit(solution)/shard_map/ppermute | solution.py:47
  232.5 12.3 %collective-permute-start.20 = (bf16[128,2048]{1,0:T(8,128)(2,1)S(1)}, bf16[128,2048]{1,0:T(8,128)(2,1)S(1)}, u32[]{:S(2)}, u32[]{:S(2)}) collective-permute-start(bf16[128,2048]{1,0:T(8,128)(2,1)S(1)} %get-tuple-element.278), channel_id=1, source_target_pairs={{0,1},{1,0},{2,3},{3,2},{4,5},{5,4},{6,7},{7,6},{8,9},{9,8},{10,11... | collective-permute-start | bytes 1572872 | tf_op jit(solution)/shard_map/ppermute | solution.py:47
  245.8 26.4 %collective-permute-start.22 = (bf16[128,2048]{1,0:T(8,128)(2,1)}, bf16[128,2048]{1,0:T(8,128)(2,1)}, u32[]{:S(2)}, u32[]{:S(2)}) collective-permute-start(bf16[128,2048]{1,0:T(8,128)(2,1)} %add_convert_fusion.3), channel_id=1, source_target_pairs={{0,2},{1,3},{2,0},{3,1},{4,6},{5,7},{6,4},{7,5},{8,10},{9,11},{10,... | collective-permute-start | bytes 1572872 | tf_op jit(solution)/shard_map/ppermute | solution.py:47
  249.9 23.0 %collective-permute-start.21 = (bf16[128,2048]{1,0:T(8,128)(2,1)}, bf16[128,2048]{1,0:T(8,128)(2,1)}, u32[]{:S(2)}, u32[]{:S(2)}) collective-permute-start(bf16[128,2048]{1,0:T(8,128)(2,1)} %get-tuple-element.167), channel_id=1, source_target_pairs={{0,1},{1,0},{2,3},{3,2},{4,5},{5,4},{6,7},{7,6},{8,9},{9,8},{10,11... | collective-permute-start | bytes 1572872 | tf_op jit(solution)/shard_map/ppermute | solution.py:47
  267.7 194.4 %reduce-scatter.5.cloned.1.call-start = ((), (), s32[]{:S(2)}) async-start(), calls=%async_computation.5 | async-start | bytes 2359296 | tf_op jit(solution)/shard_map/reduce_scatter | solution.py:740
  277.5 24.3 %collective-permute-start.24 = (bf16[128,2048]{1,0:T(8,128)(2,1)S(1)}, bf16[128,2048]{1,0:T(8,128)(2,1)S(1)}, u32[]{:S(2)}, u32[]{:S(2)}) collective-permute-start(bf16[128,2048]{1,0:T(8,128)(2,1)S(1)} %get-tuple-element.257), channel_id=1, source_target_pairs={{0,2},{1,3},{2,0},{3,1},{4,6},{5,7},{6,4},{7,5},{8,10},{9,11},{10,... | collective-permute-start | bytes 1572872 | tf_op jit(solution)/shard_map/ppermute | solution.py:47
  277.5 32.8 %collective-permute-start.23 = (bf16[128,2048]{1,0:T(8,128)(2,1)S(1)}, bf16[128,2048]{1,0:T(8,128)(2,1)S(1)}, u32[]{:S(2)}, u32[]{:S(2)}) collective-permute-start(bf16[128,2048]{1,0:T(8,128)(2,1)S(1)} %get-tuple-element.257), channel_id=1, source_target_pairs={{0,1},{1,0},{2,3},{3,2},{4,5},{5,4},{6,7},{7,6},{8,9},{9,8},{10,11... | collective-permute-start | bytes 1572872 | tf_op jit(solution)/shard_map/ppermute | solution.py:47
  301.8 13.0 %collective-permute-start.25 = (bf16[128,2048]{1,0:T(8,128)(2,1)S(1)}, bf16[128,2048]{1,0:T(8,128)(2,1)S(1)}, u32[]{:S(2)}, u32[]{:S(2)}) collective-permute-start(bf16[128,2048]{1,0:T(8,128)(2,1)S(1)} %collective-permute-done.24), channel_id=1, source_target_pairs={{0,1},{1,0},{2,3},{3,2},{4,5},{5,4},{6,7},{7,6},{8,9},{9,8},{10,11... | collective-permute-start | bytes 1572872 | tf_op jit(solution)/shard_map/ppermute | solution.py:47
  315.1 12.3 %collective-permute-start.30 = (bf16[128,2048]{1,0:T(8,128)(2,1)S(1)}, bf16[128,2048]{1,0:T(8,128)(2,1)S(1)}, u32[]{:S(2)}, u32[]{:S(2)}) collective-permute-start(bf16[128,2048]{1,0:T(8,128)(2,1)S(1)} %get-tuple-element.276), channel_id=1, source_target_pairs={{0,1},{1,0},{2,3},{3,2},{4,5},{5,4},{6,7},{7,6},{8,9},{9,8},{10,11... | collective-permute-start | bytes 1572872 | tf_op jit(solution)/shard_map/ppermute | solution.py:47
  318.9 12.0 %collective-permute-start.28 = (bf16[512,128]{1,0:T(8,128)(2,1)S(1)}, bf16[512,128]{1,0:T(8,128)(2,1)S(1)}, u32[]{:S(2)}, u32[]{:S(2)}) collective-permute-start(bf16[512,128]{1,0:T(8,128)(2,1)S(1)} %get-tuple-element.293), channel_id=1, source_target_pairs={{0,24},{4,28},{8,16},{12,20},{16,8},{20,12},{24,0},{28,4},{1,25},{... | collective-permute-start | bytes 393224 | tf_op jit(solution)/shard_map/ppermute | solution.py:32
  320.6 10.3 %collective-permute-start.27 = (bf16[512,128]{1,0:T(8,128)(2,1)S(1)}, bf16[512,128]{1,0:T(8,128)(2,1)S(1)}, u32[]{:S(2)}, u32[]{:S(2)}) collective-permute-start(bf16[512,128]{1,0:T(8,128)(2,1)S(1)} %get-tuple-element.294), channel_id=1, source_target_pairs={{0,16},{4,20},{8,24},{12,28},{16,0},{20,4},{24,8},{28,12},{1,17},{... | collective-permute-start | bytes 393224 | tf_op jit(solution)/shard_map/ppermute | solution.py:32
  321.4 12.3 %collective-permute-start.26 = (bf16[512,128]{1,0:T(8,128)(2,1)S(1)}, bf16[512,128]{1,0:T(8,128)(2,1)S(1)}, u32[]{:S(2)}, u32[]{:S(2)}) collective-permute-start(bf16[512,128]{1,0:T(8,128)(2,1)S(1)} %get-tuple-element.295), channel_id=1, source_target_pairs={{0,8},{4,12},{8,0},{12,4},{16,24},{20,28},{24,16},{28,20},{1,9},{5... | collective-permute-start | bytes 393224 | tf_op jit(solution)/shard_map/ppermute | solution.py:32
  327.5 27.7 %collective-permute-start.32 = (bf16[128,2048]{1,0:T(8,128)(2,1)S(1)}, bf16[128,2048]{1,0:T(8,128)(2,1)S(1)}, u32[]{:S(2)}, u32[]{:S(2)}) collective-permute-start(bf16[128,2048]{1,0:T(8,128)(2,1)S(1)} %add_convert_fusion.2), channel_id=1, source_target_pairs={{0,2},{1,3},{2,0},{3,1},{4,6},{5,7},{6,4},{7,5},{8,10},{9,11},{10,... | collective-permute-start | bytes 1572872 | tf_op jit(solution)/shard_map/ppermute | solution.py:47
  329.5 25.7 %collective-permute-start.31 = (bf16[128,2048]{1,0:T(8,128)(2,1)S(1)}, bf16[128,2048]{1,0:T(8,128)(2,1)S(1)}, u32[]{:S(2)}, u32[]{:S(2)}) collective-permute-start(bf16[128,2048]{1,0:T(8,128)(2,1)S(1)} %get-tuple-element.178), channel_id=1, source_target_pairs={{0,1},{1,0},{2,3},{3,2},{4,5},{5,4},{6,7},{7,6},{8,9},{9,8},{10,11... | collective-permute-start | bytes 1572872 | tf_op jit(solution)/shard_map/ppermute | solution.py:47
  355.2 2.9 collective-permute-start.29
  363.1 21.5 %collective-permute-start.35 = (bf16[512,384]{1,0:T(8,128)(2,1)}, bf16[512,384]{1,0:T(8,128)(2,1)S(1)}, u32[]{:S(2)}, u32[]{:S(2)}) collective-permute-start(bf16[512,384]{1,0:T(8,128)(2,1)} %get-tuple-element.184), channel_id=1, source_target_pairs={{0,24},{4,28},{8,16},{12,20},{16,8},{20,12},{24,0},{28,4},{1,25},{... | collective-permute-start | bytes 1179656 | tf_op jit(solution)/shard_map/ppermute | solution.py:32
  363.3 28.7 %collective-permute-start.34 = (bf16[512,384]{1,0:T(8,128)(2,1)}, bf16[512,384]{1,0:T(8,128)(2,1)}, u32[]{:S(2)}, u32[]{:S(2)}) collective-permute-start(bf16[512,384]{1,0:T(8,128)(2,1)} %get-tuple-element.183), channel_id=1, source_target_pairs={{0,16},{4,20},{8,24},{12,28},{16,0},{20,4},{24,8},{28,12},{1,17},{... | collective-permute-start | bytes 1179656 | tf_op jit(solution)/shard_map/ppermute | solution.py:32
  364.6 35.0 %collective-permute-start.33 = (bf16[512,384]{1,0:T(8,128)(2,1)}, bf16[512,384]{1,0:T(8,128)(2,1)}, u32[]{:S(2)}, u32[]{:S(2)}) collective-permute-start(bf16[512,384]{1,0:T(8,128)(2,1)} %get-tuple-element.182), channel_id=1, source_target_pairs={{0,8},{4,12},{8,0},{12,4},{16,24},{20,28},{24,16},{28,20},{1,9},{5... | collective-permute-start | bytes 1179656 | tf_op jit(solution)/shard_map/ppermute | solution.py:32
  366.5 33.0 %copy-start.24 = (bf16[512,384]{1,0:T(8,128)(2,1)S(1)}, bf16[512,384]{1,0:T(8,128)(2,1)}, u32[]{:S(2)}) copy-start(bf16[512,384]{1,0:T(8,128)(2,1)} %get-tuple-element.181) | copy-start | bytes 1179652
  370.4 37.9 %collective-permute-start.36 = (bf16[128,2048]{1,0:T(8,128)(2,1)S(1)}, bf16[128,2048]{1,0:T(8,128)(2,1)S(1)}, u32[]{:S(2)}, u32[]{:S(2)}) collective-permute-start(bf16[128,2048]{1,0:T(8,128)(2,1)S(1)} %copy-done.16), channel_id=1, source_target_pairs={{0,1},{1,0},{2,3},{3,2},{4,5},{5,4},{6,7},{7,6},{8,9},{9,8},{10,11... | collective-permute-start | bytes 1572872 | tf_op jit(solution)/shard_map/ppermute | solution.py:47
  370.4 37.9 %collective-permute-start.37 = (bf16[128,2048]{1,0:T(8,128)(2,1)S(1)}, bf16[128,2048]{1,0:T(8,128)(2,1)}, u32[]{:S(2)}, u32[]{:S(2)}) collective-permute-start(bf16[128,2048]{1,0:T(8,128)(2,1)S(1)} %copy-done.16), channel_id=1, source_target_pairs={{0,2},{1,3},{2,0},{3,1},{4,6},{5,7},{6,4},{7,5},{8,10},{9,11},{10,... | collective-permute-start | bytes 1572872 | tf_op jit(solution)/shard_map/ppermute | solution.py:47
  409.0 13.4 %collective-permute-start.38 = (bf16[128,2048]{1,0:T(8,128)(2,1)}, bf16[128,2048]{1,0:T(8,128)(2,1)}, u32[]{:S(2)}, u32[]{:S(2)}) collective-permute-start(bf16[128,2048]{1,0:T(8,128)(2,1)} %collective-permute-done.37), channel_id=1, source_target_pairs={{0,1},{1,0},{2,3},{3,2},{4,5},{5,4},{6,7},{7,6},{8,9},{9,8},{10,11... | collective-permute-start | bytes 1572872 | tf_op jit(solution)/shard_map/ppermute | solution.py:47
  409.3 17.7 %collective-permute-start.40 = (bf16[1024,1536]{1,0:T(8,128)(2,1)}, bf16[1024,1536]{1,0:T(8,128)(2,1)}, u32[]{:S(2)}, u32[]{:S(2)}) collective-permute-start(bf16[1024,1536]{1,0:T(8,128)(2,1)} %weight_grad.2), channel_id=1, source_target_pairs={{0,4},{4,0},{8,12},{12,8},{16,20},{20,16},{24,28},{28,24},{1,5},{5... | collective-permute-start | bytes 9437192 | tf_op jit(solution)/shard_map/ppermute | solution.py:32
  424.7 12.2 %collective-permute-start.39 = (bf16[128,2048]{1,0:T(8,128)(2,1)S(1)}, bf16[128,2048]{1,0:T(8,128)(2,1)S(1)}, u32[]{:S(2)}, u32[]{:S(2)}) collective-permute-start(bf16[128,2048]{1,0:T(8,128)(2,1)S(1)} %get-tuple-element.268), channel_id=1, source_target_pairs={{0,1},{1,0},{2,3},{3,2},{4,5},{5,4},{6,7},{7,6},{8,9},{9,8},{10,11... | collective-permute-start | bytes 1572872 | tf_op jit(solution)/shard_map/ppermute | solution.py:47
  436.9 22.1 %collective-permute-start.41 = (bf16[128,2048]{1,0:T(8,128)(2,1)}, bf16[128,2048]{1,0:T(8,128)(2,1)S(1)}, u32[]{:S(2)}, u32[]{:S(2)}) collective-permute-start(bf16[128,2048]{1,0:T(8,128)(2,1)} %get-tuple-element.201), channel_id=1, source_target_pairs={{0,1},{1,0},{2,3},{3,2},{4,5},{5,4},{6,7},{7,6},{8,9},{9,8},{10,11... | collective-permute-start | bytes 1572872 | tf_op jit(solution)/shard_map/ppermute | solution.py:47
  438.4 23.7 %collective-permute-start.42 = (bf16[128,2048]{1,0:T(8,128)(2,1)S(1)}, bf16[128,2048]{1,0:T(8,128)(2,1)}, u32[]{:S(2)}, u32[]{:S(2)}) collective-permute-start(bf16[128,2048]{1,0:T(8,128)(2,1)S(1)} %add_convert_fusion), channel_id=1, source_target_pairs={{0,2},{1,3},{2,0},{3,1},{4,6},{5,7},{6,4},{7,5},{8,10},{9,11},{10,... | collective-permute-start | bytes 1572872 | tf_op jit(solution)/shard_map/ppermute | solution.py:47
  442.1 20.0 %copy-start.38 = (f32[128]{0:T(128)S(1)}, f32[128]{0:T(128)}, u32[]{:S(2)}) copy-start(f32[128]{0:T(128)} %copy-done.37) | copy-start | bytes 1540
  444.8 29.8 %collective-permute-start.43 = (bf16[256,1536]{1,0:T(8,128)(2,1)}, bf16[256,1536]{1,0:T(8,128)(2,1)}, u32[]{:S(2)}, u32[]{:S(2)}) collective-permute-start(bf16[256,1536]{1,0:T(8,128)(2,1)} %get-tuple-element.198), channel_id=1, source_target_pairs={{0,8},{4,12},{8,0},{12,4},{16,24},{20,28},{24,16},{28,20},{1,9},{5... | collective-permute-start | bytes 2359304 | tf_op jit(solution)/shard_map/ppermute | solution.py:32
  446.0 36.3 %collective-permute-start.44 = (bf16[256,1536]{1,0:T(8,128)(2,1)}, bf16[256,1536]{1,0:T(8,128)(2,1)}, u32[]{:S(2)}, u32[]{:S(2)}) collective-permute-start(bf16[256,1536]{1,0:T(8,128)(2,1)} %get-tuple-element.199), channel_id=1, source_target_pairs={{0,16},{4,20},{8,24},{12,28},{16,0},{20,4},{24,8},{28,12},{1,17},{... | collective-permute-start | bytes 2359304 | tf_op jit(solution)/shard_map/ppermute | solution.py:32
  447.1 35.2 %collective-permute-start.45 = (bf16[256,1536]{1,0:T(8,128)(2,1)}, bf16[256,1536]{1,0:T(8,128)(2,1)}, u32[]{:S(2)}, u32[]{:S(2)}) collective-permute-start(bf16[256,1536]{1,0:T(8,128)(2,1)} %get-tuple-element.200), channel_id=1, source_target_pairs={{0,24},{4,28},{8,16},{12,20},{16,8},{20,12},{24,0},{28,4},{1,25},{... | collective-permute-start | bytes 2359304 | tf_op jit(solution)/shard_map/ppermute | solution.py:32
  466.3 22.5 %collective-permute-start.46 = (bf16[128,2048]{1,0:T(8,128)(2,1)}, bf16[128,2048]{1,0:T(8,128)(2,1)S(1)}, u32[]{:S(2)}, u32[]{:S(2)}) collective-permute-start(bf16[128,2048]{1,0:T(8,128)(2,1)} %fusion.30), channel_id=1, source_target_pairs={{0,1},{1,0},{2,3},{3,2},{4,5},{5,4},{6,7},{7,6},{8,9},{9,8},{10,11... | collective-permute-start | bytes 1572872 | tf_op jit(solution)/shard_map/ppermute | solution.py:47
  466.3 22.5 %collective-permute-start.47 = (bf16[128,2048]{1,0:T(8,128)(2,1)}, bf16[128,2048]{1,0:T(8,128)(2,1)S(1)}, u32[]{:S(2)}, u32[]{:S(2)}) collective-permute-start(bf16[128,2048]{1,0:T(8,128)(2,1)} %fusion.30), channel_id=1, source_target_pairs={{0,2},{1,3},{2,0},{3,1},{4,6},{5,7},{6,4},{7,5},{8,10},{9,11},{10,... | collective-permute-start | bytes 1572872 | tf_op jit(solution)/shard_map/ppermute | solution.py:47
  488.9 5.3 collective-permute-start.49
  489.9 5.8 %collective-permute-start.50 = (f32[72,128]{1,0:T(8,128)S(1)}, f32[72,128]{1,0:T(8,128)S(1)}, u32[]{:S(2)}, u32[]{:S(2)}) collective-permute-start(f32[72,128]{1,0:T(8,128)S(1)} %concatenate.142), channel_id=1, source_target_pairs={{0,3},{1,2},{2,1},{3,0},{4,7},{5,6},{6,5},{7,4},{8,11},{9,10},{10,... | collective-permute-start | bytes 110600 | tf_op jit(solution)/shard_map/ppermute | solution.py:47
  492.1 4.2 collective-permute-start.48
  496.3 4.0 collective-permute-start.52
  498.6 25.2 %collective-permute-start.51 = (bf16[128,2048]{1,0:T(8,128)(2,1)S(1)}, bf16[128,2048]{1,0:T(8,128)(2,1)}, u32[]{:S(2)}, u32[]{:S(2)}) collective-permute-start(bf16[128,2048]{1,0:T(8,128)(2,1)S(1)} %collective-permute-done.47), channel_id=1, source_target_pairs={{0,1},{1,0},{2,3},{3,2},{4,5},{5,4},{6,7},{7,6},{8,9},{9,8},{10,11... | collective-permute-start | bytes 1572872 | tf_op jit(solution)/shard_map/ppermute | solution.py:47
  500.3 4.0 collective-permute-start.53
  504.3 1.2 collective-permute-start.54
  (47 other events, 368.1 us)
Sparse Core Ops, SparseCore 0:
  57.3 35.8 all-gather.2
  95.6 104.1 all-gather.4
  267.9 135.6 reduce-scatter.2
  409.4 43.1 reduce-scatter.4
